TPU v7x, 32 devices: a whole 2x2x4 slice. The times are simulated.
32 devices in a mesh: dp: 4 (over x, core), fsdp: 8 (over z, y).
Axes of the slice: x: 2, y: 2, z: 4, core: 2. Of those that a mesh axis runs over, the one named last changes fastest.
Arguments:
- tokens: bfloat16 [16384, 768], P(('dp', 'fsdp')), may hold values from -6 to 6
- cotangent: bfloat16 [16384, 768], P(('dp', 'fsdp')), may hold values from -6 to 6
- tile_dest: int32 [128], P(('dp', 'fsdp')), may hold values from 0 to 31, as said below
- seq_lengths: int32 [32, 4], P(('dp', 'fsdp')), may hold values from 0 to 512, as said below
- norm1_gain: float32 [768], P(('dp', 'fsdp')), may hold values from 0.5 to 1.5
- norm1_bias: float32 [768], P(('dp', 'fsdp')), may hold values from -1.5 to 1.5
- w_qkv: float32 [768, 2304], P(('dp', 'fsdp')), may hold values from -0.3125 to 0.3125
- q_bias: float32 [768], P(('dp', 'fsdp')), may hold values from -1.5 to 1.5
- v_bias: float32 [768], P(('dp', 'fsdp')), may hold values from -1.5 to 1.5
- w_out: float32 [768, 768], P(('dp', 'fsdp')), may hold values from -0.75 to 0.75
- out_bias: float32 [768], P(('dp', 'fsdp')), may hold values from -1.5 to 1.5
- norm2_gain: float32 [768], P(('dp', 'fsdp')), may hold values from 0.5 to 1.5
- norm2_bias: float32 [768], P(('dp', 'fsdp')), may hold values from -1.5 to 1.5
- w_up: float32 [768, 3072], P(('dp', 'fsdp')), may hold values from -0.21875 to 0.21875
- up_bias: float32 [3072], P(('dp', 'fsdp')), may hold values from -1.5 to 1.5
- w_down: float32 [3072, 768], P(('dp', 'fsdp')), may hold values from -0.109375 to 0.109375
- down_bias: float32 [768], P(('dp', 'fsdp')), may hold values from -1.5 to 1.5
Outputs:
- mixed: bfloat16 [16384, 768], P(('dp', 'fsdp'))
- grad_tokens: bfloat16 [16384, 768], P(('dp', 'fsdp'))
- grad_norm1_gain: float32 [768], P(('dp', 'fsdp'))
- grad_norm1_bias: float32 [768], P(('dp', 'fsdp'))
- grad_w_qkv: float32 [768, 2304], P(('dp', 'fsdp'))
- grad_q_bias: float32 [768], P(('dp', 'fsdp'))
- grad_v_bias: float32 [768], P(('dp', 'fsdp'))
- grad_w_out: float32 [768, 768], P(('dp', 'fsdp'))
- grad_out_bias: float32 [768], P(('dp', 'fsdp'))
- grad_norm2_gain: float32 [768], P(('dp', 'fsdp'))
- grad_norm2_bias: float32 [768], P(('dp', 'fsdp'))
- grad_w_up: float32 [768, 3072], P(('dp', 'fsdp'))
- grad_up_bias: float32 [3072], P(('dp', 'fsdp'))
- grad_w_down: float32 [3072, 768], P(('dp', 'fsdp'))
- grad_down_bias: float32 [768], P(('dp', 'fsdp'))
Inputs may be any that keep to these rules, and one draw needn't show every extreme that they name: `tile_dest`: within each dp index the entries of its 8 devices form a permutation of 0 to 31; entry e sends its tile to device e // 4 of that dp index, slot e % 4; the 4 tiles of one device go to 4 different devices, so each device sends at most one tile to each device and receives exactly 4. `seq_lengths`: on each device the tile counts ceil(length / 128) of the 4 slots sum to 4; empty slots occur; every dp index has a device holding one sequence of 512 tokens.
All inputs are finite; a program needn't handle non-finite values.
Results may differ from a plain program's by a relative error of at most 0.014.
The roundings to bfloat16 on the way count: a program that leaves them out, or rounds other values in their place, can miss the bound.
Values may be sent and summed in bfloat16 or wider, within the bound.
No kernel may reach another device: no remote copies, remote signals or barrier semaphores. Data moves between devices by JAX's collectives and lax.ppermute only.
A program may use at most 128 MiB of HBM per device.

v0:
```python
import functools

import jax
import jax.numpy as jnp
from jax import lax
from jax.experimental import pallas as pl
from jax.experimental.pallas import tpu as pltpu
from jax.sharding import PartitionSpec as P

HEAD_DIM = 64
LANES = 128
SCALE = 0.125
EPSILON = 1e-06
MASKED = -1000000000.0
F32 = jnp.float32
BF16 = jnp.bfloat16
AXES = ("dp", "fsdp")
LIGHT = pl.CostEstimate(flops=0, transcendentals=0, bytes_accessed=0)


def bits_of(size):
    return size.bit_length() - 1


class Cube:
    def __init__(self, dp_size, fs_size):
        self.size = {"dp": dp_size, "fsdp": fs_size}
        self.dp_high, self.fs_size = dp_size // 2, fs_size
        high_dp = [("dp", b) for b in reversed(range(1, bits_of(dp_size)))]
        low_fs = [("fsdp", 0)]
        self.core = ("dp", 0)
        self.far = [("fsdp", b) for b in reversed(range(1, bits_of(fs_size)))]
        self.near = (high_dp + low_fs, low_fs + high_dp)
        self.natural = high_dp + self.far + low_fs

    def swap(self, value, link):
        axis, bit = link
        pairs = [(i, i ^ (1 << bit)) for i in range(self.size[axis])]
        return lax.ppermute(value, axis, pairs)

    def masks(self, slot, order):
        found = {"dp": 0, "fsdp": 0}
        for k, (axis, bit) in enumerate(order):
            found[axis] |= ((slot >> k) & 1) << bit
        return found["dp"] >> 1, found["fsdp"]


def move(name, scalars, sources, out_shapes, plan):
    count = len(sources)
    total = sum(2 * s.size * s.dtype.itemsize for s in out_shapes)

    def kernel(scalar_ref, *refs):
        srcs, outs = refs[:count], refs[count : count + len(out_shapes)]
        sems = refs[-1]
        copies = [
            pltpu.make_async_copy(src, out, sems.at[i])
            for i, (src, out) in enumerate(plan(scalar_ref, srcs, outs))
        ]
        for copy in copies:
            copy.start()
        for copy in copies:
            copy.wait()

    class Counter:
        def __getitem__(self, key):
            return jnp.int32(0)

    class Blank:
        @property
        def at(self):
            return self

        def __getitem__(self, key):
            return self

    copies = len(
        plan(Counter(), [Blank() for _ in sources], [Blank() for _ in out_shapes])
    )
    return pl.pallas_call(
        kernel,
        out_shape=out_shapes,
        in_specs=[pl.BlockSpec(memory_space=pltpu.SMEM)]
        + [pl.BlockSpec(memory_space=pl.ANY) for _ in sources],
        out_specs=[pl.BlockSpec(memory_space=pltpu.VMEM) for _ in out_shapes],
        scratch_shapes=[pltpu.SemaphoreType.DMA((copies,))],
        cost_estimate=LIGHT,
        name=name,
    )(scalars, *sources)


def after(value, *others):
    return lax.optimization_barrier((value,) + others)[0]


def tied(values, *others):
    if not others:
        return list(values)
    return list(lax.optimization_barrier(tuple(values) + others)[: len(values)])


class Gather:
    def __init__(self, cube, shard, cut):
        self.cube, self.bounds = cube, (0, cut, shard.shape[1])
        self.parts, self.moved = [shard[None]], []
        self.steps = [[link] for link in cube.far] + [list(pair) for pair in zip(*cube.near)]
        self.step = 0

    def advance(self, *others):
        links, count = self.steps[self.step], len(self.parts)
        parts = tied(self.parts + self.moved, *others)
        parts, moved = parts[:count], parts[count:]
        if moved:
            parts = [jnp.concatenate(pair, axis=0) for pair in zip(parts, moved)]
        if len(links) > len(parts):
            bounds = self.bounds
            parts = [lax.slice_in_dim(parts[0], bounds[i], bounds[i + 1], axis=2) for i in range(2)]
        self.parts = parts
        self.moved = [self.cube.swap(part, link) for part, link in zip(parts, links)]
        self.step += 1
        return self.moved

    def cores(self, *others):
        parts = tied(self.parts + self.moved, *others)
        self.parts = [parts[0], parts[2], parts[1], parts[3]]
        self.others = [self.cube.swap(part, self.cube.core) for part in self.parts]
        return self.others

    def matrices(self, me, pieces, *others):
        cube, bounds = self.cube, self.bounds
        half, rows = self.parts[0].shape[:2]

        def plan(me_ref, srcs, outs):
            core = me_ref[0] & 1
            pairs = []
            for i in range(2):
                order = cube.far + cube.near[i]
                for out, (first, wide, blocks) in zip(outs, pieces):
                    each = wide // blocks
                    for j in range(blocks):
                        low = max(bounds[i], first + j * each)
                        high = min(bounds[i + 1], first + (j + 1) * each)
                        if low >= high:
                            continue
                        taken = pl.ds(low - bounds[i], high - low)
                        placed = pl.ds(low - first - j * each, high - low)
                        for slot in range(2 * half):
                            mask_a, mask_f = cube.masks(slot, order)
                            a, f = (me_ref[0] >> 1) ^ mask_a, me_ref[1] ^ mask_f
                            for k in range(2):
                                src = srcs[4 * k + 2 * i + slot // half].at[slot % half, :, taken]
                                pairs.append((src, out.at[a, core ^ k, f, j, :, placed]))
            return pairs

        shapes = [
            jax.ShapeDtypeStruct(
                (cube.dp_high, 2, cube.fs_size, blocks, rows, wide // blocks), BF16
            )
            for _, wide, blocks in pieces
        ]
        sources = tied(self.parts + self.others, *others)
        outs = move("interleave", me, sources, shapes, plan)
        return [out.reshape(-1, out.shape[-1]) for out in outs]


def deal_apart(name, scalars, tiles, peer_count):
    count, shape = tiles.shape[0], tiles.shape[1:]

    def kernel(far_ref, src, *refs):
        outs, held, sems = refs[:peer_count], refs[-2], refs[-1]
        into = [pltpu.make_async_copy(src.at[i], held.at[i], sems.at[0, i]) for i in range(count)]
        for copy in into:
            copy.start()
        for i in range(count):
            into[i].wait()
            for d in range(peer_count):

                @pl.when(far_ref[i] == d)
                def _():
                    pltpu.make_async_copy(held.at[i], outs[d], sems.at[1, i]).start()

        for i in range(count):
            pltpu.make_async_copy(held.at[i], outs[0], sems.at[1, i]).wait()

    return pl.pallas_call(
        kernel,
        out_shape=[jax.ShapeDtypeStruct(shape, tiles.dtype)] * peer_count,
        in_specs=[pl.BlockSpec(memory_space=pltpu.SMEM), pl.BlockSpec(memory_space=pl.ANY)],
        out_specs=[pl.BlockSpec(memory_space=pl.ANY)] * peer_count,
        scratch_shapes=[
            pltpu.VMEM((count,) + shape, tiles.dtype),
            pltpu.SemaphoreType.DMA((2, count)),
        ],
        cost_estimate=LIGHT,
        name=name,
    )(scalars, tiles)


def collect(name, scalars, buckets, count):
    shape, dtype = buckets[0].shape, buckets[0].dtype
    peer_count = len(buckets)

    def kernel(far_ref, *refs):
        srcs, out, held, sems = refs[:peer_count], refs[peer_count], refs[-2], refs[-1]
        back = [pltpu.make_async_copy(held.at[i], out.at[i], sems.at[1, i]) for i in range(count)]
        for i in range(count):
            for d in range(peer_count):

                @pl.when(far_ref[i] == d)
                def _():
                    pltpu.make_async_copy(srcs[d], held.at[i], sems.at[0, i]).start()

        for i in range(count):
            pltpu.make_async_copy(srcs[0], held.at[i], sems.at[0, i]).wait()
            back[i].start()
        for copy in back:
            copy.wait()

    return pl.pallas_call(
        kernel,
        out_shape=jax.ShapeDtypeStruct((count,) + shape, dtype),
        in_specs=[pl.BlockSpec(memory_space=pltpu.SMEM)]
        + [pl.BlockSpec(memory_space=pl.ANY)] * peer_count,
        out_specs=pl.BlockSpec(memory_space=pl.ANY),
        scratch_shapes=[
            pltpu.VMEM((count,) + shape, dtype),
            pltpu.SemaphoreType.DMA((2, count)),
        ],
        cost_estimate=LIGHT,
        name=name,
    )(scalars, *buckets)


def deal_apart(name, scalars, tiles, peer_count):
    count, shape = tiles.shape[0], tiles.shape[1:]

    def kernel(far_ref, src, *refs):
        outs, held, sems = refs[:peer_count], refs[-2], refs[-1]
        into = [pltpu.make_async_copy(src.at[i], held.at[i], sems.at[0, i]) for i in range(count)]
        for copy in into:
            copy.start()
        for i in range(count):
            into[i].wait()
            for d in range(peer_count):

                @pl.when(far_ref[i] == d)
                def _():
                    pltpu.make_async_copy(held.at[i], outs[d], sems.at[1, i]).start()

        for i in range(count):
            pltpu.make_async_copy(held.at[i], outs[0], sems.at[1, i]).wait()

    return pl.pallas_call(
        kernel,
        out_shape=[jax.ShapeDtypeStruct(shape, tiles.dtype)] * peer_count,
        in_specs=[pl.BlockSpec(memory_space=pltpu.SMEM), pl.BlockSpec(memory_space=pl.ANY)],
        out_specs=[pl.BlockSpec(memory_space=pl.ANY)] * peer_count,
        scratch_shapes=[
            pltpu.VMEM((count,) + shape, tiles.dtype),
            pltpu.SemaphoreType.DMA((2, count)),
        ],
        cost_estimate=LIGHT,
        name=name,
    )(scalars, tiles)


def collect(name, scalars, buckets, count):
    shape, dtype = buckets[0].shape, buckets[0].dtype
    peer_count = len(buckets)

    def kernel(far_ref, *refs):
        srcs, out, held, sems = refs[:peer_count], refs[peer_count], refs[-2], refs[-1]
        back = [pltpu.make_async_copy(held.at[i], out.at[i], sems.at[1, i]) for i in range(count)]
        for i in range(count):
            for d in range(peer_count):

                @pl.when(far_ref[i] == d)
                def _():
                    pltpu.make_async_copy(srcs[d], held.at[i], sems.at[0, i]).start()

        for i in range(count):
            pltpu.make_async_copy(srcs[0], held.at[i], sems.at[0, i]).wait()
            back[i].start()
        for copy in back:
            copy.wait()

    return pl.pallas_call(
        kernel,
        out_shape=jax.ShapeDtypeStruct((count,) + shape, dtype),
        in_specs=[pl.BlockSpec(memory_space=pltpu.SMEM)]
        + [pl.BlockSpec(memory_space=pl.ANY)] * peer_count,
        out_specs=pl.BlockSpec(memory_space=pl.ANY),
        scratch_shapes=[
            pltpu.VMEM((count,) + shape, dtype),
            pltpu.SemaphoreType.DMA((2, count)),
        ],
        cost_estimate=LIGHT,
        name=name,
    )(scalars, *buckets)


def deal(name, peers, tiles, buckets):
    source = buckets if tiles is None else tiles
    count, shape = peers.shape[0], source.shape[1:]
    out_count = count if tiles is None else buckets

    def kernel(peers_ref, src, out, held, sems):
        into, back = [], []
        for i in range(count):
            peer = peers_ref[i]
            here, there = (peer, i) if tiles is None else (i, peer)
            into.append(pltpu.make_async_copy(src.at[here], held.at[i], sems.at[0, i]))
            back.append(pltpu.make_async_copy(held.at[i], out.at[there], sems.at[1, i]))
        for copy in into:
            copy.start()
        for first, second in zip(into, back):
            first.wait()
            second.start()
        for copy in back:
            copy.wait()

    return pl.pallas_call(
        kernel,
        out_shape=jax.ShapeDtypeStruct((out_count,) + shape, source.dtype),
        in_specs=[pl.BlockSpec(memory_space=pltpu.SMEM), pl.BlockSpec(memory_space=pl.ANY)],
        out_specs=pl.BlockSpec(memory_space=pl.ANY),
        scratch_shapes=[
            pltpu.VMEM((count,) + shape, source.dtype),
            pltpu.SemaphoreType.DMA((2, count)),
        ],
        cost_estimate=LIGHT,
        name=name,
    )(peers, source)


def weight_grads(cube, me, jobs, rows, blocks):
    slots = cube.dp_high * cube.fs_size
    order = cube.natural[::-1]
    tokens, height = jobs[0][0].shape
    columns = jobs[0][1].shape[1] if blocks > 1 else min(height, jobs[-1][1].shape[1])
    aligned = rows % 8 == 0
    counts = [right.shape[1] // columns for _, right in jobs]
    starts = [sum(counts[:i]) for i in range(len(jobs))]
    steps = sum(counts)

    def kernel(me_ref, *refs):
        lefts, rights = refs[0 : 2 * len(jobs) : 2], refs[1 : 2 * len(jobs) : 2]
        outs, product = refs[2 * len(jobs) : 2 * len(jobs) + 2], refs[-1]
        step = pl.program_id(0)
        for left, right, start, count in zip(lefts, rights, starts, counts):

            @pl.when((step >= start) & (step < start + count))
            def _():
                value = dot_tn(left[...], right[...])
                if aligned:
                    product[...] = value
                else:
                    for i in range(height // rows):
                        product[i] = value[i * rows : (i + 1) * rows]

        core = me_ref[0] & 1
        for slot in range(slots):
            mask_a, mask_f = cube.masks(slot, order)
            a, f = (me_ref[0] >> 1) ^ mask_a, me_ref[1] ^ mask_f
            for k, out in enumerate(outs):
                owner = (2 * a + (core ^ k)) * cube.fs_size + f
                for j in range(blocks):
                    piece = owner * blocks + j
                    if aligned:
                        value = product[pl.ds(pl.multiple_of(piece * rows, 8), rows), :]
                    else:
                        value = product[piece]
                    out[slot, :, j * columns : (j + 1) * columns] = value.astype(BF16)

    def column(start, count):
        return lambda i, me_ref: (0, jnp.clip(i - start, 0, count - 1))

    in_specs, operands = [], []
    for (left, right), start, count in zip(jobs, starts, counts):
        in_specs.append(pl.BlockSpec((tokens, height), lambda i, me_ref: (0, 0)))
        in_specs.append(pl.BlockSpec((tokens, columns), column(start, count)))
        operands += [left, right]
    shape = jax.ShapeDtypeStruct((slots, rows, steps * blocks * columns), BF16)
    keep, give = pl.pallas_call(
        kernel,
        out_shape=[shape, shape],
        grid_spec=pltpu.PrefetchScalarGridSpec(
            num_scalar_prefetch=1,
            grid=(steps,),
            in_specs=in_specs,
            out_specs=[
                pl.BlockSpec((slots, rows, blocks * columns), lambda i, me_ref: (0, 0, i))
            ]
            * 2,
            scratch_shapes=[
                pltpu.VMEM((height, columns) if aligned else (height // rows, rows, columns), F32)
            ],
        ),
        cost_estimate=LIGHT,
        name="weight_grads",
    )(me, *operands)
    return give, keep


class Scatter:
    def __init__(self, cube, give, keep, cut):
        self.cube, self.cut = cube, cut
        self.give, self.keep = [give], [keep]
        self.left = [cube.natural[::-1]]
        self.plan = [[cube.core]] + [list(pair) for pair in zip(cube.near[0][::-1], cube.near[1][::-1])]
        self.plan += [[link] for link in cube.far[::-1]]
        self.step = 0

    def start(self):
        links = self.plan[self.step]
        return [self.cube.swap(give, link) for give, link in zip(self.give, links)]

    def finish(self, got, pieces=None):
        self.step += 1
        rows = self.keep[0].shape[1]
        widths = [k.shape[2] for k in self.keep]
        copies = []
        if self.step == len(self.plan):
            shapes = [
                jax.ShapeDtypeStruct((blocks * rows, wide // blocks), F32)
                for _, wide, blocks in pieces
            ]
            for o, (first, wide, blocks) in enumerate(pieces):
                each = wide // blocks
                for j in range(blocks):
                    low = first + j * each
                    target = (slice(j * rows, (j + 1) * rows), slice(None))
                    copies.append((0, 0, slice(low, low + each), o, target))
            return self.add(got, shapes, copies)
        links = self.plan[self.step]
        if len(links) > len(widths):
            ranges = [(0, 0, self.cut, 0, 0), (0, self.cut, widths[0], 1, 0)]
            self.left = [self.left[0], list(self.left[0])]
            new_widths = [self.cut, widths[0] - self.cut]
        elif len(links) < len(widths):
            ranges = [(0, 0, widths[0], 0, 0), (1, 0, widths[1], 0, widths[0])]
            new_widths = [sum(widths)]
        else:
            ranges = [(i, 0, w, i, 0) for i, w in enumerate(widths)]
            new_widths = widths
        slots = self.keep[0].shape[0]
        for source, low, high, part, first in ranges:
            bit = self.left[part].index(links[part])
            for slot in range(slots):
                side, rest = (slot >> bit) & 1, (slot >> (bit + 1) << bit) | (slot & ((1 << bit) - 1))
                target = (rest, slice(None), slice(first, first + high - low))
                copies.append((source, slot, slice(low, high), 2 * part + side, target))
        shapes = [
            jax.ShapeDtypeStruct((slots // 2, rows, w), BF16) for w in new_widths for _ in range(2)
        ]
        outs = self.add(got, shapes, copies)
        self.keep, self.give = outs[0::2], outs[1::2]
        self.left = [
            [link for link in self.left[i] if link != links[i]] for i in range(len(links))
        ]
        return None

    def add(self, got, shapes, copies):
        count = len(got)
        if self.keep[0].shape[0] <= 2:
            rows = {}
            for source, slot, columns, o, target in copies:
                mine = self.keep[source][slot, :, columns].astype(F32)
                total = (mine + got[source][slot, :, columns].astype(F32)).astype(shapes[o].dtype)
                rows.setdefault(o, []).append(total)
            outs = []
            for o, shape in enumerate(shapes):
                value = rows[o][0] if len(rows[o]) == 1 else jnp.concatenate(rows[o], axis=0)
                outs.append(value.reshape(shape.shape))
            return outs

        def kernel(*refs):
            outs = refs[2 * count :]
            for source, slot, columns, o, target in copies:
                mine = refs[source][slot, :, columns].astype(F32)
                came = refs[count + source][slot, :, columns].astype(F32)
                outs[o][target] = (mine + came).astype(outs[o].dtype)

        total = sum(2 * v.size * 2 for v in self.keep)
        return pl.pallas_call(
            kernel,
            out_shape=shapes,
            in_specs=[pl.BlockSpec(memory_space=pltpu.VMEM)] * (2 * count),
            out_specs=[pl.BlockSpec(memory_space=pltpu.VMEM)] * len(shapes),
            cost_estimate=LIGHT,
            name="add_step",
        )(*self.keep, *got)


def dot_nn(left, right):
    return jnp.dot(left, right, preferred_element_type=F32)


def dot_tn(left, right):
    return lax.dot_general(left, right, (((0,), (0,)), ((), ())), preferred_element_type=F32)


def dot_nt(left, right):
    return lax.dot_general(left, right, (((1,), (1,)), ((), ())), preferred_element_type=F32)


def attend_forward(qkv, query_segment, key_segment):
    rows, width = qkv.shape
    width = width // 3
    blocks = width // LANES

    def kernel(q_ref, k_ref, v_ref, qs_ref, ks_ref, out_ref, lse_ref):
        allowed = ks_ref[...] == qs_ref[...]
        q = q_ref[...] * SCALE
        k = k_ref[...]
        v_t = v_ref[...].T
        lane = lax.broadcasted_iota(jnp.int32, (1, LANES), 1)
        outs = []
        for h in range(LANES // HEAD_DIM):
            k_h = jnp.where(lane // HEAD_DIM == h, k, jnp.zeros_like(k))
            scores = jnp.where(allowed, dot_nt(k_h, q), MASKED)
            top = jnp.max(scores, axis=0, keepdims=True)
            weight = jnp.exp(scores - top)
            total = jnp.sum(weight, axis=0, keepdims=True)
            probs = (weight * (1.0 / total)).astype(BF16)
            outs.append(dot_nn(v_t[h * HEAD_DIM : (h + 1) * HEAD_DIM], probs))
            lse_ref[0, h : h + 1, :] = top + jnp.log(total)
        out_ref[...] = jnp.concatenate(outs, axis=0).T.astype(BF16)

    return pl.pallas_call(
        kernel,
        out_shape=[
            jax.ShapeDtypeStruct((rows, width), BF16),
            jax.ShapeDtypeStruct((blocks, LANES // HEAD_DIM, rows), F32),
        ],
        grid=(blocks,),
        in_specs=[
            pl.BlockSpec((rows, LANES), lambda i: (0, i)),
            pl.BlockSpec((rows, LANES), lambda i: (0, blocks + i)),
            pl.BlockSpec((rows, LANES), lambda i: (0, 2 * blocks + i)),
            pl.BlockSpec((1, rows), lambda i: (0, 0)),
            pl.BlockSpec((rows, 1), lambda i: (0, 0)),
        ],
        out_specs=[
            pl.BlockSpec((rows, LANES), lambda i: (0, i)),
            pl.BlockSpec((1, LANES // HEAD_DIM, rows), lambda i: (i, 0, 0)),
        ],
        cost_estimate=LIGHT,
        name="attend_forward",
    )(qkv, qkv, qkv, query_segment, key_segment)


def attend_backward(qkv, d_attn, lse, query_segment, key_segment):
    rows, width = d_attn.shape
    blocks = width // LANES

    def kernel(q_ref, k_ref, v_ref, d_ref, lse_ref, qs_ref, ks_ref, out_ref):
        allowed = ks_ref[...] == qs_ref[...]
        q = q_ref[...] * SCALE
        k = k_ref[...]
        v = v_ref[...]
        d_out = d_ref[...]
        k_t = k.T
        lane = lax.broadcasted_iota(jnp.int32, (1, LANES), 1)
        d_q, d_k, d_v = [], 0.0, 0.0
        for h in range(LANES // HEAD_DIM):
            here = lane // HEAD_DIM == h
            zero = jnp.zeros_like(k)
            k_h = jnp.where(here, k, zero)
            scores = dot_nt(k_h, q)
            probs = jnp.where(allowed, jnp.exp(scores - lse_ref[0, h : h + 1, :]), 0.0)
            d_out_h = jnp.where(here, d_out, zero)
            d_v = d_v + dot_nn(probs.astype(BF16), d_out_h)
            d_probs = dot_nt(v, d_out_h)
            inner = jnp.sum(probs * d_probs, axis=0, keepdims=True)
            d_scores = (probs * (d_probs - inner)).astype(BF16)
            d_k = d_k + dot_nn(d_scores, jnp.where(here, q, zero))
            d_q.append(dot_nn(k_t[h * HEAD_DIM : (h + 1) * HEAD_DIM], d_scores))
        d_q = jnp.concatenate(d_q, axis=0).T * SCALE
        for part, value in enumerate((d_q, d_k, d_v)):
            place = pl.multiple_of((pl.program_id(0) + part * blocks) * LANES, LANES)
            out_ref[:, pl.ds(place, LANES)] = value.astype(BF16)

    return pl.pallas_call(
        kernel,
        out_shape=jax.ShapeDtypeStruct((rows, 3 * width), BF16),
        grid=(blocks,),
        in_specs=[
            pl.BlockSpec((rows, LANES), lambda i: (0, i)),
            pl.BlockSpec((rows, LANES), lambda i: (0, blocks + i)),
            pl.BlockSpec((rows, LANES), lambda i: (0, 2 * blocks + i)),
            pl.BlockSpec((rows, LANES), lambda i: (0, i)),
            pl.BlockSpec((1, LANES // HEAD_DIM, rows), lambda i: (i, 0, 0)),
            pl.BlockSpec((1, rows), lambda i: (0, 0)),
            pl.BlockSpec((rows, 1), lambda i: (0, 0)),
        ],
        out_specs=pl.BlockSpec((rows, 3 * width), lambda i: (0, 0)),
        cost_estimate=LIGHT,
        name="attend_backward",
    )(qkv, qkv, qkv, d_attn, lse, query_segment, key_segment)


def normalize(stream):
    middle = jnp.mean(stream, axis=-1, keepdims=True)
    centered = stream - middle
    spread = jnp.mean(centered * centered, axis=-1, keepdims=True)
    rho = lax.rsqrt(spread + EPSILON)
    return centered * rho, rho


def normalize_back(grad, gain, hat, rho):
    scaled = grad * gain
    return rho * (
        scaled
        - jnp.mean(scaled, axis=-1, keepdims=True)
        - hat * jnp.mean(scaled * hat, axis=-1, keepdims=True)
    )


def gelu_tanh(values):
    return jax.nn.gelu(values, approximate=True)


def layout(lengths, row_count, tile_rows):
    tile_counts = (lengths + tile_rows - 1) // tile_rows
    seg_ends = jnp.cumsum(tile_counts) * tile_rows
    seg_starts = seg_ends - tile_counts * tile_rows
    position = jnp.arange(row_count, dtype=jnp.int32)[:, None]
    inside = (position >= seg_starts[None, :]) & (position < seg_ends[None, :])
    segment = jnp.sum((position >= seg_ends[None, :]).astype(jnp.int32), axis=1)
    offset = jnp.sum(jnp.where(inside, position - seg_starts[None, :], 0), axis=1)
    length_here = jnp.sum(jnp.where(inside, lengths[None, :], 0), axis=1)
    return (segment, offset < length_here)


def col_sums(values):
    return jnp.sum(values.astype(F32), axis=0, keepdims=True)


def per_device(
    tokens,
    cotangent,
    tile_dest,
    seq_lengths,
    norm1_gain,
    norm1_bias,
    w_qkv,
    q_bias,
    v_bias,
    w_out,
    out_bias,
    norm2_gain,
    norm2_bias,
    w_up,
    up_bias,
    w_down,
    down_bias,
):
    dp_size = lax.axis_size("dp")
    peer_count = lax.axis_size("fsdp")
    cube = Cube(dp_size, peer_count)
    my_dp, my_fs = lax.axis_index("dp"), lax.axis_index("fsdp")
    me = jnp.stack([my_dp, my_fs]).astype(jnp.int32)
    tile_count = tile_dest.shape[0]
    row_count, width = tokens.shape
    tile_rows = row_count // tile_count
    shard = w_qkv.shape[0]
    hidden = w_up.shape[1]
    hidden_shard = w_down.shape[0]
    spread = hidden // width

    small = [norm1_gain, norm1_bias, q_bias, v_bias, out_bias, norm2_gain, norm2_bias, down_bias]
    dest_row = jnp.pad(tile_dest.astype(F32), (0, shard - tile_count))
    block = jnp.concatenate(
        [v.reshape(1, shard) for v in small + [dest_row]] + [up_bias.reshape(spread, shard)], axis=0
    )
    block_rows = block.shape[0]
    groups = -(-block_rows // shard)
    block = jnp.pad(block, ((0, groups * shard - block_rows), (0, LANES - shard)))
    if groups > 1:
        block = jnp.concatenate(jnp.split(block, groups, axis=0), axis=1)
    block_width = groups * LANES
    target = tile_dest // tile_count
    tiled = (tile_count, tile_rows, width)
    bucketed = (peer_count, tile_rows, width)

    wide = 3 * width
    half = hidden // 2
    chunk_a = jnp.concatenate([w_qkv, block], axis=1).astype(BF16)
    pieces = [w_out] + [w_up[:, j * width : (j + 1) * width] for j in range(spread)] + [w_down]
    chunk_b = jnp.concatenate([p.astype(BF16) for p in pieces], axis=0)
    full = lax.all_gather(chunk_b, AXES, axis=0, tiled=False)
    mat_out = full[:, :shard].reshape(-1, width)
    mat_up = jnp.concatenate(
        [full[:, (1 + j) * shard : (2 + j) * shard].reshape(-1, width) for j in range(spread)], axis=1
    )
    mat_down = full[:, (1 + spread) * shard :].reshape(hidden, width)
    distance = target ^ my_fs
    token_tiles = after(tokens.reshape(tiled), chunk_a)
    buckets = deal_apart("deal_tokens", distance, token_tiles, peer_count)

    def cross(bucket, d):
        return lax.ppermute(bucket, "fsdp", [(i, i ^ d) for i in range(peer_count)])

    cut_a = (chunk_a.shape[1] // 2 + LANES - 1) // LANES * LANES
    ga = Gather(cube, chunk_a, cut_a)
    steps = len(ga.steps)
    far = sorted(range(peer_count // 2, peer_count), key=lambda d: (d & 1, d))
    near = list(range(1, peer_count // 2))
    groups = [far[k::steps] + near[k::steps] for k in range(steps)]
    got = {0: buckets[0]}
    came_a, landed = [], []
    for k in range(steps):
        came_a.append(ga.advance(*(landed[k - 2] if k >= 2 else [])))
        landed.append([])
        for d in groups[k]:
            got[d] = cross(after(buckets[d], *came_a[k - 1]) if k else buckets[d], d)
            landed[k].append(got[d])
    ga.cores()
    mat_qkv, vectors = ga.matrices(me, [(0, wide, 1), (wide, block_width, 1)])
    devices = dp_size * peer_count
    here = ga.parts[2][:, :, wide - ga.bounds[1] :]
    slots = [cube.masks(slot, cube.far + cube.near[1]) for slot in range(here.shape[0])]
    dest_peers = [mask_f for mask_a, mask_f in slots if mask_a == 0]
    here = jnp.stack([here[i] for i, (mask_a, _) in enumerate(slots) if mask_a == 0])

    def rows_of(blocks, first, count):
        rows = [
            blocks[:, r % shard, (r // shard) * LANES : (r // shard + 1) * LANES]
            for r in range(first, first + count)
        ]
        return jnp.stack(rows, axis=1)

    def spread_lanes(values, size):
        lanes = lax.broadcasted_iota(jnp.int32, (LANES, size), 0)
        places = lax.broadcasted_iota(jnp.int32, (LANES, size), 1)
        return dot_nn(values, (places % shard == lanes).astype(BF16))

    vectors = vectors.reshape(devices, shard, block_width)
    flat = spread_lanes(rows_of(vectors, 0, 8).reshape(devices * 8, LANES), width)
    place = lax.broadcasted_iota(jnp.int32, (devices, 8, width), 2) // shard
    owner = lax.broadcasted_iota(jnp.int32, (devices, 8, width), 0)
    flat = jnp.sum(jnp.where(place == owner, flat.reshape(devices, 8, width), 0.0), axis=0)
    gain_one, shift_one, bias_q, bias_v, bias_out, gain_two, shift_two, bias_down = flat
    count = devices * spread
    flat = spread_lanes(rows_of(vectors, 9, spread).reshape(count, LANES), hidden)
    place = lax.broadcasted_iota(jnp.int32, (count, hidden), 1) // shard
    owner = lax.broadcasted_iota(jnp.int32, (count, hidden), 0)
    bias_up = jnp.sum(jnp.where(place == owner, flat, 0.0), axis=0)

    here = rows_of(here, 8, 1)[:, 0, :tile_count].astype(jnp.int32)
    wanted = my_fs * tile_count + jnp.arange(tile_count, dtype=jnp.int32)
    found = here[None] == wanted[:, None, None]
    dest_peers = jnp.array(dest_peers, dtype=jnp.int32)
    came_far = jnp.sum(jnp.where(found, dest_peers[None, :, None], 0), axis=(1, 2))
    origin = came_far ^ my_fs

    local_tokens = collect(
        "take_tokens", came_far, [got[d] for d in range(peer_count)], tile_count
    ).reshape(row_count, width)
    cot_buckets = deal(
        "deal_cotangent", target, after(cotangent.reshape(tiled), local_tokens), peer_count
    )
    segment, valid_rows = layout(seq_lengths[0], row_count, tile_rows)
    query_segment = segment[None, :]
    key_segment = jnp.where(valid_rows, segment, -1)[:, None]

    stream = local_tokens.astype(F32)
    hat_one, rho_one = normalize(stream)
    norm_one = (hat_one * gain_one + shift_one).astype(BF16)
    qkv_shift = jnp.concatenate([bias_q, jnp.zeros((width,), F32), bias_v])
    norm_one = after(norm_one, cot_buckets)
    qkv_low = (dot_nn(norm_one, mat_qkv) + qkv_shift).astype(BF16)
    got_cot = lax.all_to_all(
        after(cot_buckets, qkv_low), "fsdp", split_axis=0, concat_axis=0, tiled=True
    )
    attn_out, lse = attend_forward(qkv_low, query_segment, key_segment)
    mid_stream = stream + dot_nn(attn_out, mat_out) + bias_out
    hat_two, rho_two = normalize(mid_stream)
    norm_two = (hat_two * gain_two + shift_two).astype(BF16)
    pre_act = dot_nn(norm_two, mat_up) + bias_up
    act_value, gelu_pull = jax.vjp(gelu_tanh, pre_act)
    act_low = lax.optimization_barrier(act_value.astype(BF16))
    result = (mid_stream + dot_nn(act_low, mat_down) + bias_down).astype(BF16)
    mixed_buckets = deal("return_mixed", origin, result.reshape(tiled), peer_count)
    got_mixed = lax.all_to_all(mixed_buckets, "fsdp", split_axis=0, concat_axis=0, tiled=True)

    local_cot = deal("take_cotangent", origin, None, after(got_cot, mixed_buckets))
    local_cot = local_cot.reshape(row_count, width)
    grad_out_rows = local_cot.astype(F32) * valid_rows.astype(F32)[:, None]
    grad_out_low = after(grad_out_rows.astype(BF16), mixed_buckets)
    d_down_bias = col_sums(grad_out_low)
    d_w_down = dot_tn(act_low, grad_out_low).astype(BF16)
    sum_down = lax.psum_scatter(d_w_down, AXES, scatter_dimension=0, tiled=True)

    d_act = dot_nt(after(grad_out_low, d_w_down), mat_down)
    d_pre = gelu_pull(d_act)[0].astype(BF16)

    d_up_bias = col_sums(d_pre)
    d_norm_two = dot_nt(d_pre, mat_up)
    d_gain_two = jnp.sum(d_norm_two * hat_two, axis=0, keepdims=True)
    d_shift_two = jnp.sum(d_norm_two, axis=0, keepdims=True)
    d_mid = grad_out_rows + normalize_back(d_norm_two, gain_two, hat_two, rho_two)
    d_proj_low = d_mid.astype(BF16)
    d_out_bias = col_sums(d_proj_low)
    give, keep = weight_grads(cube, me, [(norm_two, d_pre), (attn_out, d_proj_low)], shard, 1)
    up = Scatter(cube, give, keep, (hidden + width) // 2)
    sent_up = up.start()
    d_attn = dot_nt(after(d_proj_low, give, got_mixed), mat_out).astype(BF16)

    up.finish(tied(sent_up, d_attn))
    sent_up = up.start()
    d_attn = after(d_attn, *up.give)
    d_qkv = attend_backward(qkv_low, d_attn, lse, query_segment, key_segment)
    up.finish(tied(sent_up, d_qkv))
    sent_up = up.start()
    d_qkv = after(d_qkv, *up.give)
    d_q_bias = col_sums(d_qkv[:, :width])
    d_v_bias = col_sums(d_qkv[:, 2 * width :])
    give, keep = weight_grads(cube, me, [(norm_one, d_qkv)], shard, 1)
    qkv = Scatter(cube, give, keep, wide // 2)
    sent_qkv = qkv.start()
    d_norm_one = dot_nt(after(d_qkv, give), mat_qkv)
    d_gain_one = jnp.sum(d_norm_one * hat_one, axis=0, keepdims=True)
    d_shift_one = jnp.sum(d_norm_one, axis=0, keepdims=True)
    d_stream = d_mid + normalize_back(d_norm_one, gain_one, hat_one, rho_one)
    qkv.finish(tied(sent_qkv, d_norm_one))
    sent_qkv = qkv.start()

    tiles = after(d_stream.astype(BF16).reshape(tiled), *qkv.give, *sent_up)
    buckets = deal_apart("return_gradient", came_far, tiles, peer_count)

    d_small = [
        d_gain_one,
        d_shift_one,
        d_q_bias,
        d_v_bias,
        d_out_bias,
        d_gain_two,
        d_shift_two,
        d_down_bias,
    ]
    d_rows = d_small + [d_up_bias[:, j * width : (j + 1) * width] for j in range(spread)]
    value = jnp.concatenate(d_rows, axis=0)
    vector_links = [cube.core] + cube.near[0][::-1] + cube.far[::-1]

    vector_links = [cube.core] + cube.near[0][::-1] + cube.far[::-1]
    up_pieces = [(0, hidden, 1), (hidden, width, 1)]
    got = {0: buckets[0]}
    first = [d for d in far + near if not d & 1]
    second = [d for d in far + near if d & 1]
    waits = [first[:1], first[1:], second[:2], second[2:]]
    for d in first:
        got[d] = cross(buckets[d], d)
    s_qkv = s_up = None
    value = value + cube.swap(value, vector_links[0])
    moved, k = list(buckets), 0
    while s_qkv is None or k + 1 < len(vector_links):
        due = list(moved)
        if k < len(waits):
            due += [got[d] for d in waits[k]]
        if k == 0:
            due.append(sum_down)
        if s_qkv is None:
            came = tied(sent_qkv, *due)
            s_qkv = qkv.finish(came, [(0, wide, 1)])
            if s_qkv is None:
                sent_qkv = qkv.start()
        if k + 1 < len(vector_links):
            value = after(value, *moved)
            value = value + cube.swap(value, vector_links[k + 1])
        moved = came
        if s_up is None:
            s_up = up.finish(tied(sent_up, *moved), up_pieces)
            if s_up is None:
                sent_up = up.start()
        if k == 0:
            for d, bucket in zip(second, tied([buckets[d] for d in second], *moved)):
                got[d] = cross(bucket, d)
        k += 1
    s_rows = value
    grad_tokens = collect(
        "take_gradient", distance, [got[d] for d in range(peer_count)], tile_count
    ).reshape(row_count, width)
    mixed = deal("take_mixed", target, None, after(got_mixed, *buckets)).reshape(row_count, width)
    my_place = my_dp * peer_count + my_fs
    s_block = lax.dynamic_slice(s_rows, (0, my_place * shard), (8, shard))
    s_up_bias = lax.dynamic_slice(
        s_rows[8:].reshape(hidden), (my_place * hidden_shard,), (hidden_shard,)
    )

    return (
        mixed,
        grad_tokens,
        s_block[0],
        s_block[1],
        s_qkv[0],
        s_block[2],
        s_block[3],
        s_up[1],
        s_block[4],
        s_block[5],
        s_block[6],
        s_up[0],
        s_up_bias,
        sum_down.astype(F32),
        s_block[7],
    )


def solution(mesh):
    rows, matrix = P(AXES), P(AXES, None)
    in_specs = (
        matrix,
        matrix,
        rows,
        matrix,
        rows,
        rows,
        matrix,
        rows,
        rows,
        matrix,
        rows,
        rows,
        rows,
        matrix,
        rows,
        matrix,
        rows,
    )
    out_specs = (
        matrix,
        matrix,
        rows,
        rows,
        matrix,
        rows,
        rows,
        matrix,
        rows,
        rows,
        rows,
        matrix,
        rows,
        matrix,
        rows,
    )
    return jax.shard_map(
        per_device, mesh=mesh, in_specs=in_specs, out_specs=out_specs, check_vma=False
    )
```

profile of v0, /device:TPU:0, one launch (start us, length us, event | category | flops | bytes accessed | tf_op | source)
XLA Modules:
  0.0 360.5 jit_solution(14271501651555450005)
XLA Ops:
  12.0 4.1 %collective-permute-start = (bf16[1,24,2432]{2,1,0:T(8,128)(2,1)S(1)}, bf16[1,24,2432]{2,1,0:T(8,128)(2,1)S(1)}, u32[]{:S(2)}, u32[]{:S(2)}) collective-permute-start(bf16[1,24,2432]{2,1,0:T(8,128)(2,1)S(1)} %pad_maximum_fusion.4), channel_id=1, source_target_pairs={{0,4},{1,5},{2,6},{3,7},{4,0},{5,1},{6,2},{7,3},{8,12},{9,13},{10,... | collective-permute-start | bytes 350216 | tf_op jit(solution)/shard_map/ppermute | solution.py:39
  16.1 2.6 deal_tokens.1
  18.9 1.8 collective-permute-start.3
  21.9 7.8 %collective-permute-start.1 = (bf16[2,24,2432]{2,1,0:T(8,128)(2,1)S(1)}, bf16[2,24,2432]{2,1,0:T(8,128)(2,1)S(1)}, u32[]{:S(2)}, u32[]{:S(2)}) collective-permute-start(bf16[2,24,2432]{2,1,0:T(8,128)(2,1)S(1)} %pad_maximum_fusion.3), channel_id=1, source_target_pairs={{0,2},{1,3},{2,0},{3,1},{4,6},{5,7},{6,4},{7,5},{8,10},{9,11},{10,... | collective-permute-start | bytes 700424 | tf_op jit(solution)/shard_map/ppermute | solution.py:39
  30.3 5.5 %collective-permute-done.2.refs_4_ = bf16[128,768]{1,0:T(8,128)(2,1)S(1)} collective-permute-done((bf16[128,768]{1,0:T(8,128)(2,1)}, bf16[128,768]{1,0:T(8,128)(2,1)S(1)}, u32[]{:S(2)}, u32[]{:S(2)}) %collective-permute-start.2) | collective-permute-done | bytes 196640 | tf_op jit(solution)/shard_map/ppermute | solution.py:702
  35.8 6.7 %collective-permute-done.1 = bf16[2,24,2432]{2,1,0:T(8,128)(2,1)S(1)} collective-permute-done((bf16[2,24,2432]{2,1,0:T(8,128)(2,1)S(1)}, bf16[2,24,2432]{2,1,0:T(8,128)(2,1)S(1)}, u32[]{:S(2)}, u32[]{:S(2)}) %collective-permute-start.1) | collective-permute-done | bytes 233504 | tf_op jit(solution)/shard_map/ppermute | solution.py:39
  45.1 3.5 collective-permute-start.6
  51.8 11.5 %collective-permute-done.7.refs_2_ = bf16[128,768]{1,0:T(8,128)(2,1)S(1)} collective-permute-done((bf16[128,768]{1,0:T(8,128)(2,1)S(1)}, bf16[128,768]{1,0:T(8,128)(2,1)S(1)}, u32[]{:S(2)}, u32[]{:S(2)}) %collective-permute-start.7) | collective-permute-done | bytes 196640 | tf_op jit(solution)/shard_map/ppermute | solution.py:702
  63.3 3.2 collective-permute-done.6.refs_6_
  70.6 15.4 %collective-permute-done.9.refs_5_ = bf16[128,768]{1,0:T(8,128)(2,1)S(1)} collective-permute-done((bf16[128,768]{1,0:T(8,128)(2,1)S(1)}, bf16[128,768]{1,0:T(8,128)(2,1)S(1)}, u32[]{:S(2)}, u32[]{:S(2)}) %collective-permute-start.9) | collective-permute-done | bytes 196640 | tf_op jit(solution)/shard_map/ppermute | solution.py:702
  87.2 3.0 take_tokens.1
  92.2 2.7 deal_cotangent.1
  96.9 5.4 %interleave.1 = (bf16[2,2,8,1,24,2304]{5,4,3,2,1,0:T(8,128)(2,1)}, bf16[2,2,8,1,24,128]{5,4,3,2,1,0:T(8,128)(2,1)}) custom-call(s32[2]{0:T(128)} %pad_add_fusion.scalar_ref.me_ref, bf16[8,24,1280]{2,1,0:T(8,128)(2,1)} %copy-done.19, bf16[8,24,1280]{2,1,0:T(8,128)(2,1)} %copy-done.24, bf16[8,24,1152]{2,1,0:T(8,128)(2,1)} %copy-done.20, ...), custom_call_target="tpu_custom_call" | custom-call | tf_op jit(solution)/shard_map/interleave/pallas_call | solution.py:79
  105.6 5.5 %fusion.7.q_ref.k_ref.v_ref = bf16[512,2304]{1,0:T(8,128)(2,1)} fusion(bf16[512,768]{1,0:T(8,128)(2,1)S(1)} %fusion.14.refs_0_, bf16[768,2304]{1,0:T(8,128)(2,1)} %bitcast.147, f32[2304]{0:T(1024)S(1)} %pad_maximum_fusion.5), kind=kOutput, calls=%fused_computation.14 | convolution fusion | flops 1814298624 | bytes 6693888 | tf_op jit(solution)/shard_map/dot_general | solution.py:495
  111.1 6.3 %all-to-all-start.1 = ((bf16[8,128,768]{2,1,0:T(8,128)(2,1)}), bf16[8,128,768]{2,1,0:T(8,128)(2,1)}, u32[]{:S(2)}, u32[]{:S(2)}) async-start(bf16[8,128,768]{2,1,0:T(8,128)(2,1)} %deal_cotangent.1), calls=%async_computation.1 | async-start | bytes 3145728 | tf_op jit(solution)/shard_map/all_to_all | solution.py:773
  117.4 10.5 %attend_forward.1 = (bf16[512,768]{1,0:T(8,128)(2,1)}, f32[6,2,512]{2,1,0:T(2,128)}) custom-call(bf16[512,2304]{1,0:T(8,128)(2,1)} %fusion.7.q_ref.k_ref.v_ref, bf16[512,2304]{1,0:T(8,128)(2,1)} %fusion.7.q_ref.k_ref.v_ref, bf16[512,2304]{1,0:T(8,128)(2,1)} %fusion.7.q_ref.k_ref.v_ref, s32[1,512]{1,0:T(1,128)} %bitcast.139, s32[512,1]{1,0:T(8,128)} %copy.43.ks_ref), custom_call_target="tpu_custom_call" | custom-call | tf_op jit(solution)/shard_map/attend_forward/pallas_call | solution.py:529
  128.5 2.6 slice.219
  131.2 4.8 %fusion.59 = (bf16[32,24,768]{2,1,0:T(8,128)(2,1)S(1)}, bf16[32,24,768]{2,1,0:T(8,128)(2,1)S(1)}, bf16[32,24,768]{2,1,0:T(8,128)(2,1)S(1)}, bf16[32,24,768]{2,1,0:T(8,128)(2,1)S(1)}, bf16[32,24,768]{2,1,0:T(8,128)(2,1)S(1)}) fusion(bf16[32,216,768]{2,1,0:T(8,128)(2,1)} %bitcast.119), kind=kLoop, calls=%fused_computation.182 | loop fusion | bytes 11796480 | tf_op jit(solution)/shard_map/slice | solution.py:694
  138.4 7.9 %multiply_convert_fusion = (bf16[512,3072]{1,0:T(8,128)(2,1)S(1)}, f32[512,3072]{1,0:T(8,128)}) fusion(f32[3072]{0:T(1024)S(1)} %fusion.26, bf16[512,768]{1,0:T(8,128)(2,1)S(1)} %add_convert_fusion.1.refs_0_, bf16[768,768]{1,0:T(8,128)(2,1)S(1)} %bitcast.127, bf16[768,768]{1,0:T(8,128)(2,1)S(1)} %bitcast.129, bf16[768,768]{1,0:T(8,128)(2,1)S(1)} %bitcast.131, ...), kind=kOutput, calls=%fused_computation.10 | convolution fusion | flops 2450522112 | bytes 14954496 | tf_op jit(solution)/shard_map/dot_general | solution.py:495
  146.4 3.5 add_convert_fusion
  149.9 2.6 return_mixed.1
  152.5 4.4 %all-to-all-done.1.src = bf16[8,128,768]{2,1,0:T(8,128)(2,1)} async-done(((bf16[8,128,768]{2,1,0:T(8,128)(2,1)}), bf16[8,128,768]{2,1,0:T(8,128)(2,1)}, u32[]{:S(2)}, u32[]{:S(2)}) %all-to-all-start.1) | async-done | bytes 1572896 | tf_op jit(solution)/shard_map/all_to_all | solution.py:773
  156.9 4.3 %all-to-all-start = ((bf16[8,128,768]{2,1,0:T(8,128)(2,1)}), bf16[8,128,768]{2,1,0:T(8,128)(2,1)}, u32[]{:S(2)}, u32[]{:S(2)}) async-start(bf16[8,128,768]{2,1,0:T(8,128)(2,1)} %return_mixed.1), calls=%async_computation | async-start | bytes 3145728 | tf_op jit(solution)/shard_map/all_to_all | solution.py:785
  161.3 2.6 take_cotangent.1
  165.3 7.0 %convolution_convert_fusion = bf16[3072,768]{1,0:T(8,128)(2,1)} fusion(bf16[512,3072]{1,0:T(8,128)(2,1)} %copy-done.81, bf16[512,768]{1,0:T(8,128)(2,1)S(1)} %fusion.25), kind=kOutput, calls=%fused_computation.11 | convolution fusion | flops 2418278400 | bytes 8650752 | tf_op jit(solution)/shard_map/dot_general | solution.py:499
  172.4 9.4 %convert_reduce_fusion = (f32[3072]{0:T(1024)S(1)}, bf16[512,3072]{1,0:T(8,128)(2,1)S(1)}) fusion(f32[512,3072]{1,0:T(8,128)} %get-tuple-element.248, f32[3072]{0:T(1024)S(1)} %fusion.26, bf16[512,768]{1,0:T(8,128)(2,1)S(1)} %fusion.25, bf16[3072,768]{1,0:T(8,128)(2,1)} %bitcast.121), kind=kOutput, calls=%fused_computation.9 | convolution fusion | flops 2452091904 | bytes 14966784 | tf_op jit(solution)/shard_map/dot_general | solution.py:503
  181.8 3.5 multiply_reduce_fusion
  185.3 2.1 convert_reduce_fusion.3
  187.4 9.4 %weight_grads.2 = (bf16[16,24,3840]{2,1,0:T(8,128)(2,1)}, bf16[16,24,3840]{2,1,0:T(8,128)(2,1)}) custom-call(s32[2]{0:T(128)} %pad_add_fusion.scalar_ref.me_ref, bf16[512,768]{1,0:T(8,128)(2,1)} %copy-done.7, bf16[512,3072]{1,0:T(8,128)(2,1)} %copy-done.5, bf16[512,768]{1,0:T(8,128)(2,1)} %get-tuple-element.127.refs_2_, ...), custom_call_target="tpu_custom_call" | custom-call | tf_op jit(solution)/shard_map/weight_grads/pallas_call | solution.py:383
  196.8 1.9 all-to-all-done.src
  200.4 2.5 collective-permute-done.17.refs_1_
  202.9 4.7 %add_step.6 = (bf16[8,24,1920]{2,1,0:T(8,128)(2,1)}, bf16[8,24,1920]{2,1,0:T(8,128)(2,1)}, bf16[8,24,1920]{2,1,0:T(8,128)(2,1)}, bf16[8,24,1920]{2,1,0:T(8,128)(2,1)}) custom-call(bf16[16,24,3840]{2,1,0:T(8,128)(2,1)} %get-tuple-element.134.refs_0_, bf16[16,24,3840]{2,1,0:T(8,128)(2,1)} %collective-permute-done.17.refs_1_), custom_call_target="tpu_custom_call" | custom-call | tf_op jit(solution)/shard_map/add_step/pallas_call | solution.py:484
  207.6 1.9 collective-permute-start.18
  210.9 14.6 %attend_backward.1.refs_1_ = bf16[512,2304]{1,0:T(8,128)(2,1)} custom-call(bf16[512,2304]{1,0:T(8,128)(2,1)} %fusion.7.q_ref.k_ref.v_ref, bf16[512,2304]{1,0:T(8,128)(2,1)} %fusion.7.q_ref.k_ref.v_ref, bf16[512,2304]{1,0:T(8,128)(2,1)} %fusion.7.q_ref.k_ref.v_ref, bf16[512,768]{1,0:T(8,128)(2,1)} %convolution_convert_fusion.1.d_ref, ...), custom_call_target="tpu_custom_call" | custom-call | tf_op jit(solution)/shard_map/attend_backward/pallas_call | solution.py:583
  225.5 4.5 %collective-permute-done.18.refs_2_ = bf16[8,24,1920]{2,1,0:T(8,128)(2,1)S(1)} collective-permute-done((bf16[8,24,1920]{2,1,0:T(8,128)(2,1)}, bf16[8,24,1920]{2,1,0:T(8,128)(2,1)S(1)}, u32[]{:S(2)}, u32[]{:S(2)}) %collective-permute-start.18) | collective-permute-done | bytes 737312 | tf_op jit(solution)/shard_map/ppermute | solution.py:39
  230.0 2.5 collective-permute-done.19.refs_3_
  233.4 3.0 add_step.7
  236.4 6.8 %weight_grads.3 = (bf16[16,24,2304]{2,1,0:T(8,128)(2,1)}, bf16[16,24,2304]{2,1,0:T(8,128)(2,1)}) custom-call(s32[2]{0:T(128)} %pad_add_fusion.scalar_ref.me_ref, bf16[512,768]{1,0:T(8,128)(2,1)} %copy-done.6, bf16[512,2304]{1,0:T(8,128)(2,1)} %attend_backward.1.refs_1_), custom_call_target="tpu_custom_call" | custom-call | tf_op jit(solution)/shard_map/weight_grads/pallas_call | solution.py:383
  243.2 2.5 collective-permute-start.21
  245.6 6.0 %fusion.20 = (f32[768]{0:T(1024)}, f32[512]{0:T(512)S(1)}, f32[512]{0:T(512)S(1)}, f32[768]{0:T(1024)}, f32[512,768]{1,0:T(8,128)}) fusion(f32[512]{0:T(512)S(1)} %rsqrt_bitcast_fusion, f32[512]{0:T(512)S(1)} %get-tuple-element.242, bf16[4,128,768]{2,1,0:T(8,128)(2,1)S(1)} %copy-done, f32[768]{0:T(1024)S(1)} %get-tuple-element.210, ...), kind=kOutput, calls=%fused_computation.32 | convolution fusion | flops 1815868928 | bytes 8274944 | tf_op jit(solution)/shard_map/dot_general | solution.py:503
  251.6 3.3 add_step.8
  254.9 2.0 collective-permute-start.23
  257.1 3.3 fusion.19
  261.6 2.8 return_gradient.1
  264.4 1.9 collective-permute-start.25
  269.7 7.3 %collective-permute-done.25.refs_4_ = bf16[128,768]{1,0:T(8,128)(2,1)S(1)} collective-permute-done((bf16[128,768]{1,0:T(8,128)(2,1)}, bf16[128,768]{1,0:T(8,128)(2,1)S(1)}, u32[]{:S(2)}, u32[]{:S(2)}) %collective-permute-start.25) | collective-permute-done | bytes 196640 | tf_op jit(solution)/shard_map/ppermute | solution.py:702
  277.0 2.0 collective-permute-start.30
  279.0 14.4 %reduce-scatter.2.cloned.1.call-done = bf16[96,768]{1,0:T(8,128)(2,1)} async-done(((bf16[3072,768]{1,0:T(8,128)(2,1)}), bf16[96,768]{1,0:T(8,128)(2,1)}) %reduce-scatter.2.cloned.1.call-update) | async-done | bytes 147472 | tf_op jit(solution)/shard_map/reduce_scatter | solution.py:793
  293.4 2.4 add_step.9
  295.8 2.3 collective-permute-start.35
  300.3 2.4 add_step.11
  302.6 2.4 collective-permute-done.33
  308.2 2.1 collective-permute-done.34
  311.9 1.9 collective-permute-start.29
  313.7 2.6 collective-permute-start.31
  316.3 4.3 %collective-permute-start.37 = (f32[12,768]{1,0:T(8,128)S(1)}, f32[12,768]{1,0:T(8,128)S(1)}, u32[]{:S(2)}, u32[]{:S(2)}) collective-permute-start(f32[12,768]{1,0:T(8,128)S(1)} %add.238), channel_id=1, source_target_pairs={{0,2},{1,3},{2,0},{3,1},{4,6},{5,7},{6,4},{7,5},{8,10},{9,11},{10,... | collective-permute-start | bytes 110600 | tf_op jit(solution)/shard_map/ppermute | solution.py:39
  320.7 2.6 take_mixed.1
  325.8 2.7 collective-permute-done.31.refs_7_
  329.2 2.6 take_gradient.1
  331.8 2.1 add_step.10
  334.0 2.4 collective-permute-start.38
  336.9 3.7 %collective-permute-done.38 = bf16[2,24,2304]{2,1,0:T(8,128)(2,1)S(1)} collective-permute-done((bf16[2,24,2304]{2,1,0:T(8,128)(2,1)}, bf16[2,24,2304]{2,1,0:T(8,128)(2,1)S(1)}, u32[]{:S(2)}, u32[]{:S(2)}) %collective-permute-start.38) | collective-permute-done | bytes 221216 | tf_op jit(solution)/shard_map/ppermute | solution.py:39
  340.6 2.4 collective-permute-start.39
  344.6 5.8 %collective-permute-done.39 = f32[12,768]{1,0:T(8,128)S(1)} collective-permute-done((f32[12,768]{1,0:T(8,128)S(1)}, f32[12,768]{1,0:T(8,128)S(1)}, u32[]{:S(2)}, u32[]{:S(2)}) %collective-permute-start.39) | collective-permute-done | bytes 36896 | tf_op jit(solution)/shard_map/ppermute | solution.py:39
  (324 shorter events, 53.0 us)
Async XLA Ops:
  7.3 121.2 %all-gather.3.cloned.1.call-start = ((), (), s32[]{:S(2)}) async-start(), calls=%async_computation.4 | async-start | bytes 10948608 | tf_op jit(solution)/shard_map/all_gather | solution.py:691
  12.0 9.8 %collective-permute-start = (bf16[1,24,2432]{2,1,0:T(8,128)(2,1)S(1)}, bf16[1,24,2432]{2,1,0:T(8,128)(2,1)S(1)}, u32[]{:S(2)}, u32[]{:S(2)}) collective-permute-start(bf16[1,24,2432]{2,1,0:T(8,128)(2,1)S(1)} %pad_maximum_fusion.4), channel_id=1, source_target_pairs={{0,4},{1,5},{2,6},{3,7},{4,0},{5,1},{6,2},{7,3},{8,12},{9,13},{10,... | collective-permute-start | bytes 350216 | tf_op jit(solution)/shard_map/ppermute | solution.py:39
  18.8 26.3 %copy-start.79 = (bf16[128,768]{1,0:T(8,128)(2,1)S(1)}, bf16[128,768]{1,0:T(8,128)(2,1)}, u32[]{:S(2)}) copy-start(bf16[128,768]{1,0:T(8,128)(2,1)} %get-tuple-element.111) | copy-start | bytes 589828
  18.8 26.3 %copy-start.78 = (bf16[128,768]{1,0:T(8,128)(2,1)S(1)}, bf16[128,768]{1,0:T(8,128)(2,1)}, u32[]{:S(2)}) copy-start(bf16[128,768]{1,0:T(8,128)(2,1)} %get-tuple-element.109) | copy-start | bytes 589828
  18.8 32.5 %copy-start.77 = (bf16[128,768]{1,0:T(8,128)(2,1)S(1)}, bf16[128,768]{1,0:T(8,128)(2,1)}, u32[]{:S(2)}) copy-start(bf16[128,768]{1,0:T(8,128)(2,1)} %get-tuple-element.118) | copy-start | bytes 589828
  18.8 44.4 %copy-start.75 = (bf16[128,768]{1,0:T(8,128)(2,1)S(1)}, bf16[128,768]{1,0:T(8,128)(2,1)}, u32[]{:S(2)}) copy-start(bf16[128,768]{1,0:T(8,128)(2,1)} %get-tuple-element.116) | copy-start | bytes 589828
  18.8 17.0 %collective-permute-start.2 = (bf16[128,768]{1,0:T(8,128)(2,1)}, bf16[128,768]{1,0:T(8,128)(2,1)S(1)}, u32[]{:S(2)}, u32[]{:S(2)}) collective-permute-start(bf16[128,768]{1,0:T(8,128)(2,1)} %get-tuple-element.104), channel_id=1, source_target_pairs={{0,4},{1,5},{2,6},{3,7},{4,0},{5,1},{6,2},{7,3},{8,12},{9,13},{10,... | collective-permute-start | bytes 589832 | tf_op jit(solution)/shard_map/ppermute | solution.py:702
  18.9 16.9 %collective-permute-start.3 = (bf16[128,768]{1,0:T(8,128)(2,1)}, bf16[128,768]{1,0:T(8,128)(2,1)S(1)}, u32[]{:S(2)}, u32[]{:S(2)}) collective-permute-start(bf16[128,768]{1,0:T(8,128)(2,1)} %get-tuple-element.105), channel_id=1, source_target_pairs={{0,1},{1,0},{2,3},{3,2},{4,5},{5,4},{6,7},{7,6},{8,9},{9,8},{10,11... | collective-permute-start | bytes 589832 | tf_op jit(solution)/shard_map/ppermute | solution.py:702
  21.1 45.4 %copy-start.49 = (s32[512]{0:T(512)}, s32[512]{0:T(512)S(1)}, u32[]{:S(2)}) copy-start(s32[512]{0:T(512)S(1)} %get-tuple-element.213) | copy-start | bytes 6148
  21.9 20.7 %collective-permute-start.1 = (bf16[2,24,2432]{2,1,0:T(8,128)(2,1)S(1)}, bf16[2,24,2432]{2,1,0:T(8,128)(2,1)S(1)}, u32[]{:S(2)}, u32[]{:S(2)}) collective-permute-start(bf16[2,24,2432]{2,1,0:T(8,128)(2,1)S(1)} %pad_maximum_fusion.3), channel_id=1, source_target_pairs={{0,2},{1,3},{2,0},{3,1},{4,6},{5,7},{6,4},{7,5},{8,10},{9,11},{10,... | collective-permute-start | bytes 700424 | tf_op jit(solution)/shard_map/ppermute | solution.py:39
  35.8 30.7 %copy-start.35 = (bf16[128,768]{1,0:T(8,128)(2,1)}, bf16[128,768]{1,0:T(8,128)(2,1)S(1)}, u32[]{:S(2)}) copy-start(bf16[128,768]{1,0:T(8,128)(2,1)S(1)} %collective-permute-done.2.refs_4_) | copy-start | bytes 589828
  35.8 30.7 %copy-start.36 = (bf16[128,768]{1,0:T(8,128)(2,1)}, bf16[128,768]{1,0:T(8,128)(2,1)S(1)}, u32[]{:S(2)}) copy-start(bf16[128,768]{1,0:T(8,128)(2,1)S(1)} %collective-permute-done.3.refs_1_) | copy-start | bytes 589828
  42.6 27.3 %copy-start.62 = (s32[8]{0:T(128)S(1)}, s32[8]{0:T(128)}, u32[]{:S(2)}) copy-start(s32[8]{0:T(128)} %constant.115.clone) | copy-start | bytes 100
  42.6 23.8 %collective-permute-start.4 = (bf16[4,24,1280]{2,1,0:T(8,128)(2,1)S(1)}, bf16[4,24,1280]{2,1,0:T(8,128)(2,1)S(1)}, u32[]{:S(2)}, u32[]{:S(2)}) collective-permute-start(bf16[4,24,1280]{2,1,0:T(8,128)(2,1)S(1)} %slice.205), channel_id=1, source_target_pairs={{0,16},{8,24},{16,0},{24,8},{1,17},{9,25},{17,1},{25,9},{2,18},{10... | collective-permute-start | bytes 737288 | tf_op jit(solution)/shard_map/ppermute | solution.py:39
  45.0 18.2 %collective-permute-start.7 = (bf16[128,768]{1,0:T(8,128)(2,1)S(1)}, bf16[128,768]{1,0:T(8,128)(2,1)S(1)}, u32[]{:S(2)}, u32[]{:S(2)}) collective-permute-start(bf16[128,768]{1,0:T(8,128)(2,1)S(1)} %copy-done.79), channel_id=1, source_target_pairs={{0,2},{1,3},{2,0},{3,1},{4,6},{5,7},{6,4},{7,5},{8,10},{9,11},{10,... | collective-permute-start | bytes 589832 | tf_op jit(solution)/shard_map/ppermute | solution.py:702
  45.1 21.4 %collective-permute-start.6 = (bf16[128,768]{1,0:T(8,128)(2,1)S(1)}, bf16[128,768]{1,0:T(8,128)(2,1)S(1)}, u32[]{:S(2)}, u32[]{:S(2)}) collective-permute-start(bf16[128,768]{1,0:T(8,128)(2,1)S(1)} %copy-done.78), channel_id=1, source_target_pairs={{0,6},{1,7},{2,4},{3,5},{4,2},{5,3},{6,0},{7,1},{8,14},{9,15},{10,... | collective-permute-start | bytes 589832 | tf_op jit(solution)/shard_map/ppermute | solution.py:702
  48.6 17.9 %collective-permute-start.5 = (bf16[4,24,1152]{2,1,0:T(8,128)(2,1)S(1)}, bf16[4,24,1152]{2,1,0:T(8,128)(2,1)S(1)}, u32[]{:S(2)}, u32[]{:S(2)}) collective-permute-start(bf16[4,24,1152]{2,1,0:T(8,128)(2,1)S(1)} %slice.206), channel_id=1, source_target_pairs={{0,1},{1,0},{2,3},{3,2},{4,5},{5,4},{6,7},{7,6},{8,9},{9,8},{10,11... | collective-permute-start | bytes 663560 | tf_op jit(solution)/shard_map/ppermute | solution.py:39
  51.3 34.7 %collective-permute-start.9 = (bf16[128,768]{1,0:T(8,128)(2,1)S(1)}, bf16[128,768]{1,0:T(8,128)(2,1)S(1)}, u32[]{:S(2)}, u32[]{:S(2)}) collective-permute-start(bf16[128,768]{1,0:T(8,128)(2,1)S(1)} %copy-done.77), channel_id=1, source_target_pairs={{0,5},{1,4},{2,7},{3,6},{4,1},{5,0},{6,3},{7,2},{8,13},{9,12},{10,... | collective-permute-start | bytes 589832 | tf_op jit(solution)/shard_map/ppermute | solution.py:702
  63.3 23.3 %copy-start.39 = (bf16[128,768]{1,0:T(8,128)(2,1)}, bf16[128,768]{1,0:T(8,128)(2,1)S(1)}, u32[]{:S(2)}) copy-start(bf16[128,768]{1,0:T(8,128)(2,1)S(1)} %collective-permute-done.7.refs_2_) | copy-start | bytes 589828
  63.3 22.8 %collective-permute-start.8 = (bf16[128,768]{1,0:T(8,128)(2,1)S(1)}, bf16[128,768]{1,0:T(8,128)(2,1)S(1)}, u32[]{:S(2)}, u32[]{:S(2)}) collective-permute-start(bf16[128,768]{1,0:T(8,128)(2,1)S(1)} %copy-done.75), channel_id=1, source_target_pairs={{0,3},{1,2},{2,1},{3,0},{4,7},{5,6},{6,5},{7,4},{8,11},{9,10},{10,... | collective-permute-start | bytes 589832 | tf_op jit(solution)/shard_map/ppermute | solution.py:702
  66.4 20.1 %copy-start.40 = (bf16[128,768]{1,0:T(8,128)(2,1)}, bf16[128,768]{1,0:T(8,128)(2,1)S(1)}, u32[]{:S(2)}) copy-start(bf16[128,768]{1,0:T(8,128)(2,1)S(1)} %collective-permute-done.6.refs_6_) | copy-start | bytes 589828
  66.5 23.6 %copy-start.19 = (bf16[8,24,1280]{2,1,0:T(8,128)(2,1)}, bf16[8,24,1280]{2,1,0:T(8,128)(2,1)S(1)}, u32[]{:S(2)}) copy-start(bf16[8,24,1280]{2,1,0:T(8,128)(2,1)S(1)} %constant_dynamic-update-slice_fusion.4.refs_0_) | copy-start | bytes 1474564
  66.6 25.2 %collective-permute-start.11 = (bf16[8,24,1280]{2,1,0:T(8,128)(2,1)S(1)}, bf16[8,24,1280]{2,1,0:T(8,128)(2,1)S(1)}, u32[]{:S(2)}, u32[]{:S(2)}) collective-permute-start(bf16[8,24,1280]{2,1,0:T(8,128)(2,1)S(1)} %constant_dynamic-update-slice_fusion.4.refs_0_), channel_id=1, source_target_pairs={{0,1},{1,0},{2,3},{3,2},{4,5},{5,4},{6,7},{7,6},{8,9},{9,8},{10,11... | collective-permute-start | bytes 1474568 | tf_op jit(solution)/shard_map/ppermute | solution.py:39
  68.2 23.4 %copy-start.20 = (bf16[8,24,1152]{2,1,0:T(8,128)(2,1)}, bf16[8,24,1152]{2,1,0:T(8,128)(2,1)S(1)}, u32[]{:S(2)}) copy-start(bf16[8,24,1152]{2,1,0:T(8,128)(2,1)S(1)} %constant_dynamic-update-slice_fusion.2.refs_2_) | copy-start | bytes 1327108
  68.2 23.4 %collective-permute-start.12 = (bf16[8,24,1152]{2,1,0:T(8,128)(2,1)S(1)}, bf16[8,24,1152]{2,1,0:T(8,128)(2,1)}, u32[]{:S(2)}, u32[]{:S(2)}) collective-permute-start(bf16[8,24,1152]{2,1,0:T(8,128)(2,1)S(1)} %constant_dynamic-update-slice_fusion.2.refs_2_), channel_id=1, source_target_pairs={{0,16},{8,24},{16,0},{24,8},{1,17},{9,25},{17,1},{25,9},{2,18},{10... | collective-permute-start | bytes 1327112 | tf_op jit(solution)/shard_map/ppermute | solution.py:39
  68.3 18.2 %collective-permute-start.10 = (bf16[128,768]{1,0:T(8,128)(2,1)}, bf16[128,768]{1,0:T(8,128)(2,1)S(1)}, u32[]{:S(2)}, u32[]{:S(2)}) collective-permute-start(bf16[128,768]{1,0:T(8,128)(2,1)} %get-tuple-element.120), channel_id=1, source_target_pairs={{0,7},{1,6},{2,5},{3,4},{4,3},{5,2},{6,1},{7,0},{8,15},{9,14},{10,... | collective-permute-start | bytes 589832 | tf_op jit(solution)/shard_map/ppermute | solution.py:702
  86.0 9.3 %collective-permute-start.15 = (bf16[8,24,1152]{2,1,0:T(8,128)(2,1)S(1)}, bf16[8,24,1152]{2,1,0:T(8,128)(2,1)}, u32[]{:S(2)}, u32[]{:S(2)}) collective-permute-start(bf16[8,24,1152]{2,1,0:T(8,128)(2,1)S(1)} %constant_dynamic-update-slice_fusion.2.refs_2_), channel_id=1, source_target_pairs={{0,8},{8,0},{16,24},{24,16},{1,9},{9,1},{17,25},{25,17},{2,10},{10... | collective-permute-start | bytes 1327112 | tf_op jit(solution)/shard_map/ppermute | solution.py:39
  86.0 9.3 %collective-permute-start.13 = (bf16[8,24,1280]{2,1,0:T(8,128)(2,1)S(1)}, bf16[8,24,1280]{2,1,0:T(8,128)(2,1)S(1)}, u32[]{:S(2)}, u32[]{:S(2)}) collective-permute-start(bf16[8,24,1280]{2,1,0:T(8,128)(2,1)S(1)} %constant_dynamic-update-slice_fusion.4.refs_0_), channel_id=1, source_target_pairs={{0,8},{8,0},{16,24},{24,16},{1,9},{9,1},{17,25},{25,17},{2,10},{10... | collective-permute-start | bytes 1474568 | tf_op jit(solution)/shard_map/ppermute | solution.py:39
  91.6 3.7 %collective-permute-start.16 = (bf16[8,24,1152]{2,1,0:T(8,128)(2,1)}, bf16[8,24,1152]{2,1,0:T(8,128)(2,1)}, u32[]{:S(2)}, u32[]{:S(2)}) collective-permute-start(bf16[8,24,1152]{2,1,0:T(8,128)(2,1)} %collective-permute-done.12.refs_3_), channel_id=1, source_target_pairs={{0,8},{8,0},{16,24},{24,16},{1,9},{9,1},{17,25},{25,17},{2,10},{10... | collective-permute-start | bytes 1327112 | tf_op jit(solution)/shard_map/ppermute | solution.py:39
  91.8 3.6 collective-permute-start.14
  111.1 45.8 %all-to-all-start.1 = ((bf16[8,128,768]{2,1,0:T(8,128)(2,1)}), bf16[8,128,768]{2,1,0:T(8,128)(2,1)}, u32[]{:S(2)}, u32[]{:S(2)}) async-start(bf16[8,128,768]{2,1,0:T(8,128)(2,1)} %deal_cotangent.1), calls=%async_computation.1 | async-start | bytes 3145728 | tf_op jit(solution)/shard_map/all_to_all | solution.py:773
  156.9 41.8 %all-to-all-start = ((bf16[8,128,768]{2,1,0:T(8,128)(2,1)}), bf16[8,128,768]{2,1,0:T(8,128)(2,1)}, u32[]{:S(2)}, u32[]{:S(2)}) async-start(bf16[8,128,768]{2,1,0:T(8,128)(2,1)} %return_mixed.1), calls=%async_computation | async-start | bytes 3145728 | tf_op jit(solution)/shard_map/all_to_all | solution.py:785
  161.3 132.1 %reduce-scatter.2.cloned.1.call-start = ((), (), s32[]{:S(2)}) async-start(), calls=%async_computation.3 | async-start | bytes 4866048 | tf_op jit(solution)/shard_map/reduce_scatter | solution.py:793
  196.8 6.1 %collective-permute-start.17 = (bf16[16,24,3840]{2,1,0:T(8,128)(2,1)}, bf16[16,24,3840]{2,1,0:T(8,128)(2,1)}, u32[]{:S(2)}, u32[]{:S(2)}) collective-permute-start(bf16[16,24,3840]{2,1,0:T(8,128)(2,1)} %get-tuple-element.132), channel_id=1, source_target_pairs={{0,8},{8,0},{16,24},{24,16},{1,9},{9,1},{17,25},{25,17},{2,10},{10... | collective-permute-start | bytes 8847368 | tf_op jit(solution)/shard_map/ppermute | solution.py:39
  207.6 22.4 %collective-permute-start.18 = (bf16[8,24,1920]{2,1,0:T(8,128)(2,1)}, bf16[8,24,1920]{2,1,0:T(8,128)(2,1)S(1)}, u32[]{:S(2)}, u32[]{:S(2)}) collective-permute-start(bf16[8,24,1920]{2,1,0:T(8,128)(2,1)} %get-tuple-element.136), channel_id=1, source_target_pairs={{0,1},{1,0},{2,3},{3,2},{4,5},{5,4},{6,7},{7,6},{8,9},{9,8},{10,11... | collective-permute-start | bytes 2211848 | tf_op jit(solution)/shard_map/ppermute | solution.py:39
  209.5 23.0 %collective-permute-start.19 = (bf16[8,24,1920]{2,1,0:T(8,128)(2,1)}, bf16[8,24,1920]{2,1,0:T(8,128)(2,1)S(1)}, u32[]{:S(2)}, u32[]{:S(2)}) collective-permute-start(bf16[8,24,1920]{2,1,0:T(8,128)(2,1)} %get-tuple-element.137), channel_id=1, source_target_pairs={{0,16},{8,24},{16,0},{24,8},{1,17},{9,25},{17,1},{25,9},{2,18},{10... | collective-permute-start | bytes 2211848 | tf_op jit(solution)/shard_map/ppermute | solution.py:39
  243.2 8.4 %collective-permute-start.20 = (bf16[16,24,2304]{2,1,0:T(8,128)(2,1)}, bf16[16,24,2304]{2,1,0:T(8,128)(2,1)}, u32[]{:S(2)}, u32[]{:S(2)}) collective-permute-start(bf16[16,24,2304]{2,1,0:T(8,128)(2,1)} %get-tuple-element.147), channel_id=1, source_target_pairs={{0,8},{8,0},{16,24},{24,16},{1,9},{9,1},{17,25},{25,17},{2,10},{10... | collective-permute-start | bytes 5308424 | tf_op jit(solution)/shard_map/ppermute | solution.py:39
  243.2 17.3 %collective-permute-start.21 = (bf16[4,24,1920]{2,1,0:T(8,128)(2,1)}, bf16[4,24,1920]{2,1,0:T(8,128)(2,1)S(1)}, u32[]{:S(2)}, u32[]{:S(2)}) collective-permute-start(bf16[4,24,1920]{2,1,0:T(8,128)(2,1)} %get-tuple-element.144), channel_id=1, source_target_pairs={{0,16},{8,24},{16,0},{24,8},{1,17},{9,25},{17,1},{25,9},{2,18},{10... | collective-permute-start | bytes 1105928 | tf_op jit(solution)/shard_map/ppermute | solution.py:39
  245.6 16.0 %collective-permute-start.22 = (bf16[4,24,1920]{2,1,0:T(8,128)(2,1)}, bf16[4,24,1920]{2,1,0:T(8,128)(2,1)}, u32[]{:S(2)}, u32[]{:S(2)}) collective-permute-start(bf16[4,24,1920]{2,1,0:T(8,128)(2,1)} %get-tuple-element.145), channel_id=1, source_target_pairs={{0,1},{1,0},{2,3},{3,2},{4,5},{5,4},{6,7},{7,6},{8,9},{9,8},{10,11... | collective-permute-start | bytes 1105928 | tf_op jit(solution)/shard_map/ppermute | solution.py:39
  254.9 24.1 %collective-permute-start.23 = (bf16[8,24,1152]{2,1,0:T(8,128)(2,1)}, bf16[8,24,1152]{2,1,0:T(8,128)(2,1)}, u32[]{:S(2)}, u32[]{:S(2)}) collective-permute-start(bf16[8,24,1152]{2,1,0:T(8,128)(2,1)} %get-tuple-element.151), channel_id=1, source_target_pairs={{0,1},{1,0},{2,3},{3,2},{4,5},{5,4},{6,7},{7,6},{8,9},{9,8},{10,11... | collective-permute-start | bytes 1327112 | tf_op jit(solution)/shard_map/ppermute | solution.py:39
  256.9 22.1 %collective-permute-start.24 = (bf16[8,24,1152]{2,1,0:T(8,128)(2,1)}, bf16[8,24,1152]{2,1,0:T(8,128)(2,1)}, u32[]{:S(2)}, u32[]{:S(2)}) collective-permute-start(bf16[8,24,1152]{2,1,0:T(8,128)(2,1)} %get-tuple-element.152), channel_id=1, source_target_pairs={{0,16},{8,24},{16,0},{24,8},{1,17},{9,25},{17,1},{25,9},{2,18},{10... | collective-permute-start | bytes 1327112 | tf_op jit(solution)/shard_map/ppermute | solution.py:39
  264.4 12.6 %collective-permute-start.25 = (bf16[128,768]{1,0:T(8,128)(2,1)}, bf16[128,768]{1,0:T(8,128)(2,1)S(1)}, u32[]{:S(2)}, u32[]{:S(2)}) collective-permute-start(bf16[128,768]{1,0:T(8,128)(2,1)} %get-tuple-element.158), channel_id=1, source_target_pairs={{0,4},{1,5},{2,6},{3,7},{4,0},{5,1},{6,2},{7,3},{8,12},{9,13},{10,... | collective-permute-start | bytes 589832 | tf_op jit(solution)/shard_map/ppermute | solution.py:702
  268.1 30.9 %collective-permute-start.32 = (f32[12,768]{1,0:T(8,128)S(1)}, f32[12,768]{1,0:T(8,128)S(1)}, u32[]{:S(2)}, u32[]{:S(2)}) collective-permute-start(f32[12,768]{1,0:T(8,128)S(1)} %concatenate.54), channel_id=1, source_target_pairs={{0,8},{8,0},{16,24},{24,16},{1,9},{9,1},{17,25},{25,17},{2,10},{10... | collective-permute-start | bytes 110600 | tf_op jit(solution)/shard_map/ppermute | solution.py:39
  268.2 37.9 %collective-permute-start.27 = (bf16[128,768]{1,0:T(8,128)(2,1)}, bf16[128,768]{1,0:T(8,128)(2,1)S(1)}, u32[]{:S(2)}, u32[]{:S(2)}) collective-permute-start(bf16[128,768]{1,0:T(8,128)(2,1)} %get-tuple-element.156), channel_id=1, source_target_pairs={{0,2},{1,3},{2,0},{3,1},{4,6},{5,7},{6,4},{7,5},{8,10},{9,11},{10,... | collective-permute-start | bytes 589832 | tf_op jit(solution)/shard_map/ppermute | solution.py:702
  277.0 25.6 %copy-start.34 = (bf16[128,768]{1,0:T(8,128)(2,1)}, bf16[128,768]{1,0:T(8,128)(2,1)S(1)}, u32[]{:S(2)}) copy-start(bf16[128,768]{1,0:T(8,128)(2,1)S(1)} %collective-permute-done.25.refs_4_) | copy-start | bytes 589828
  277.0 29.4 %collective-permute-start.30 = (bf16[128,768]{1,0:T(8,128)(2,1)}, bf16[128,768]{1,0:T(8,128)(2,1)S(1)}, u32[]{:S(2)}, u32[]{:S(2)}) collective-permute-start(bf16[128,768]{1,0:T(8,128)(2,1)} %get-tuple-element.160), channel_id=1, source_target_pairs={{0,6},{1,7},{2,4},{3,5},{4,2},{5,3},{6,0},{7,1},{8,14},{9,15},{10,... | collective-permute-start | bytes 589832 | tf_op jit(solution)/shard_map/ppermute | solution.py:702
  293.4 20.4 %copy-start.72 = (bf16[128,768]{1,0:T(8,128)(2,1)S(1)}, bf16[128,768]{1,0:T(8,128)(2,1)}, u32[]{:S(2)}) copy-start(bf16[128,768]{1,0:T(8,128)(2,1)} %get-tuple-element.168) | copy-start | bytes 589828
  295.8 16.0 %collective-permute-start.35 = (bf16[4,24,1152]{2,1,0:T(8,128)(2,1)}, bf16[4,24,1152]{2,1,0:T(8,128)(2,1)S(1)}, u32[]{:S(2)}, u32[]{:S(2)}) collective-permute-start(bf16[4,24,1152]{2,1,0:T(8,128)(2,1)} %get-tuple-element.173), channel_id=1, source_target_pairs={{0,16},{8,24},{16,0},{24,8},{1,17},{9,25},{17,1},{25,9},{2,18},{10... | collective-permute-start | bytes 663560 | tf_op jit(solution)/shard_map/ppermute | solution.py:39
  298.2 15.6 %collective-permute-start.36 = (bf16[4,24,1152]{2,1,0:T(8,128)(2,1)}, bf16[4,24,1152]{2,1,0:T(8,128)(2,1)S(1)}, u32[]{:S(2)}, u32[]{:S(2)}) collective-permute-start(bf16[4,24,1152]{2,1,0:T(8,128)(2,1)} %get-tuple-element.174), channel_id=1, source_target_pairs={{0,1},{1,0},{2,3},{3,2},{4,5},{5,4},{6,7},{7,6},{8,9},{9,8},{10,11... | collective-permute-start | bytes 663560 | tf_op jit(solution)/shard_map/ppermute | solution.py:39
  299.0 6.0 %collective-permute-start.33 = (f32[12,768]{1,0:T(8,128)S(1)}, f32[12,768]{1,0:T(8,128)S(1)}, u32[]{:S(2)}, u32[]{:S(2)}) collective-permute-start(f32[12,768]{1,0:T(8,128)S(1)} %add.236), channel_id=1, source_target_pairs={{0,1},{1,0},{2,3},{3,2},{4,5},{5,4},{6,7},{7,6},{8,9},{9,8},{10,11... | collective-permute-start | bytes 110600 | tf_op jit(solution)/shard_map/ppermute | solution.py:39
  302.6 20.7 %copy-start.48 = (bf16[96,768]{1,0:T(8,128)(2,1)S(1)}, bf16[96,768]{1,0:T(8,128)(2,1)}, u32[]{:S(2)}) copy-start(bf16[96,768]{1,0:T(8,128)(2,1)} %reduce-scatter.2.cloned.1.call-done) | copy-start | bytes 442372
  305.1 31.3 %collective-permute-start.41 = (bf16[2,24,3840]{2,1,0:T(8,128)(2,1)}, bf16[2,24,3840]{2,1,0:T(8,128)(2,1)S(1)}, u32[]{:S(2)}, u32[]{:S(2)}) collective-permute-start(bf16[2,24,3840]{2,1,0:T(8,128)(2,1)} %get-tuple-element.190), channel_id=1, source_target_pairs={{0,2},{1,3},{2,0},{3,1},{4,6},{5,7},{6,4},{7,5},{8,10},{9,11},{10,... | collective-permute-start | bytes 1105928 | tf_op jit(solution)/shard_map/ppermute | solution.py:39
  306.1 22.4 %copy-start.37 = (bf16[128,768]{1,0:T(8,128)(2,1)}, bf16[128,768]{1,0:T(8,128)(2,1)S(1)}, u32[]{:S(2)}) copy-start(bf16[128,768]{1,0:T(8,128)(2,1)S(1)} %collective-permute-done.27.refs_2_) | copy-start | bytes 589828
  306.1 4.2 %collective-permute-start.34 = (f32[12,768]{1,0:T(8,128)S(1)}, f32[12,768]{1,0:T(8,128)S(1)}, u32[]{:S(2)}, u32[]{:S(2)}) collective-permute-start(f32[12,768]{1,0:T(8,128)S(1)} %add.237), channel_id=1, source_target_pairs={{0,16},{8,24},{16,0},{24,8},{1,17},{9,25},{17,1},{25,9},{2,18},{10... | collective-permute-start | bytes 110600 | tf_op jit(solution)/shard_map/ppermute | solution.py:39
  306.5 22.0 %copy-start.38 = (bf16[128,768]{1,0:T(8,128)(2,1)}, bf16[128,768]{1,0:T(8,128)(2,1)S(1)}, u32[]{:S(2)}) copy-start(bf16[128,768]{1,0:T(8,128)(2,1)S(1)} %collective-permute-done.30.refs_6_) | copy-start | bytes 589828
  306.5 9.8 %collective-permute-start.26 = (bf16[128,768]{1,0:T(8,128)(2,1)S(1)}, bf16[128,768]{1,0:T(8,128)(2,1)S(1)}, u32[]{:S(2)}, u32[]{:S(2)}) collective-permute-start(bf16[128,768]{1,0:T(8,128)(2,1)S(1)} %copy-done.76), channel_id=1, source_target_pairs={{0,1},{1,0},{2,3},{3,2},{4,5},{5,4},{6,7},{7,6},{8,9},{9,8},{10,11... | collective-permute-start | bytes 589832 | tf_op jit(solution)/shard_map/ppermute | solution.py:702
  310.3 14.2 %collective-permute-start.28 = (bf16[128,768]{1,0:T(8,128)(2,1)S(1)}, bf16[128,768]{1,0:T(8,128)(2,1)S(1)}, u32[]{:S(2)}, u32[]{:S(2)}) collective-permute-start(bf16[128,768]{1,0:T(8,128)(2,1)S(1)} %copy-done.74), channel_id=1, source_target_pairs={{0,3},{1,2},{2,1},{3,0},{4,7},{5,6},{6,5},{7,4},{8,11},{9,10},{10,... | collective-permute-start | bytes 589832 | tf_op jit(solution)/shard_map/ppermute | solution.py:702
  311.9 13.9 %collective-permute-start.29 = (bf16[128,768]{1,0:T(8,128)(2,1)S(1)}, bf16[128,768]{1,0:T(8,128)(2,1)S(1)}, u32[]{:S(2)}, u32[]{:S(2)}) collective-permute-start(bf16[128,768]{1,0:T(8,128)(2,1)S(1)} %copy-done.73), channel_id=1, source_target_pairs={{0,5},{1,4},{2,7},{3,6},{4,1},{5,0},{6,3},{7,2},{8,13},{9,12},{10,... | collective-permute-start | bytes 589832 | tf_op jit(solution)/shard_map/ppermute | solution.py:702
  313.7 14.7 %collective-permute-start.31 = (bf16[128,768]{1,0:T(8,128)(2,1)S(1)}, bf16[128,768]{1,0:T(8,128)(2,1)S(1)}, u32[]{:S(2)}, u32[]{:S(2)}) collective-permute-start(bf16[128,768]{1,0:T(8,128)(2,1)S(1)} %copy-done.72), channel_id=1, source_target_pairs={{0,7},{1,6},{2,5},{3,4},{4,3},{5,2},{6,1},{7,0},{8,15},{9,14},{10,... | collective-permute-start | bytes 589832 | tf_op jit(solution)/shard_map/ppermute | solution.py:702
  316.3 20.0 %collective-permute-start.37 = (f32[12,768]{1,0:T(8,128)S(1)}, f32[12,768]{1,0:T(8,128)S(1)}, u32[]{:S(2)}, u32[]{:S(2)}) collective-permute-start(f32[12,768]{1,0:T(8,128)S(1)} %add.238), channel_id=1, source_target_pairs={{0,2},{1,3},{2,0},{3,1},{4,6},{5,7},{6,4},{7,5},{8,10},{9,11},{10,... | collective-permute-start | bytes 110600 | tf_op jit(solution)/shard_map/ppermute | solution.py:39
  334.0 6.7 %collective-permute-start.38 = (bf16[2,24,2304]{2,1,0:T(8,128)(2,1)}, bf16[2,24,2304]{2,1,0:T(8,128)(2,1)S(1)}, u32[]{:S(2)}, u32[]{:S(2)}) collective-permute-start(bf16[2,24,2304]{2,1,0:T(8,128)(2,1)} %get-tuple-element.180), channel_id=1, source_target_pairs={{0,2},{1,3},{2,0},{3,1},{4,6},{5,7},{6,4},{7,5},{8,10},{9,11},{10,... | collective-permute-start | bytes 663560 | tf_op jit(solution)/shard_map/ppermute | solution.py:39
  336.5 15.1 %collective-permute-start.42 = (bf16[1,24,3840]{2,1,0:T(8,128)(2,1)S(1)}, bf16[1,24,3840]{2,1,0:T(8,128)(2,1)S(1)}, u32[]{:S(2)}, u32[]{:S(2)}) collective-permute-start(bf16[1,24,3840]{2,1,0:T(8,128)(2,1)S(1)} %get-tuple-element.228), channel_id=1, source_target_pairs={{0,4},{1,5},{2,6},{3,7},{4,0},{5,1},{6,2},{7,3},{8,12},{9,13},{10,... | collective-permute-start | bytes 552968 | tf_op jit(solution)/shard_map/ppermute | solution.py:39
  340.6 9.7 %collective-permute-start.39 = (f32[12,768]{1,0:T(8,128)S(1)}, f32[12,768]{1,0:T(8,128)S(1)}, u32[]{:S(2)}, u32[]{:S(2)}) collective-permute-start(f32[12,768]{1,0:T(8,128)S(1)} %add.239), channel_id=1, source_target_pairs={{0,4},{1,5},{2,6},{3,7},{4,0},{5,1},{6,2},{7,3},{8,12},{9,13},{10,... | collective-permute-start | bytes 110600 | tf_op jit(solution)/shard_map/ppermute | solution.py:39
  343.9 9.0 %collective-permute-start.40 = (bf16[1,24,2304]{2,1,0:T(8,128)(2,1)S(1)}, bf16[1,24,2304]{2,1,0:T(8,128)(2,1)S(1)}, u32[]{:S(2)}, u32[]{:S(2)}) collective-permute-start(bf16[1,24,2304]{2,1,0:T(8,128)(2,1)S(1)} %add_convert_fusion.4), channel_id=1, source_target_pairs={{0,4},{1,5},{2,6},{3,7},{4,0},{5,1},{6,2},{7,3},{8,12},{9,13},{10,... | collective-permute-start | bytes 331784 | tf_op jit(solution)/shard_map/ppermute | solution.py:39
  (65 other events, 450.9 us)
Sparse Core Ops, SparseCore 0:
  11.3 114.7 all-gather.2
  172.4 120.9 reduce-scatter.1
where the time goes:
time: 362 us; the launch traced here: 361 us
  waiting for transfers between devices  99.5 us (27%)
  Pallas kernels  86.1 us (24%)
  starting transfers between devices  73 us (20%)
  matrix products  47 us (13%)
  other arithmetic  22 us (6%)
  local copies, waits for them, and re-layouts  17.5 us (5%)
  between operations  15.4 us (4%)
    ppermute x14, waiting for transfers between devices, cross(): return lax.ppermute(bucket, 'fsdp', [(i, i ^ d) for i in range(peer_count)])  47.2 us
    ppermute x29, starting transfers between devices, swap(): return lax.ppermute(value, axis, pairs)  41.9 us
    ppermute x29, waiting for transfers between devices, swap(): return lax.ppermute(value, axis, pairs)  31.5 us
    dot_general x4, matrix products, dot_nt(): lax.dot_general(left, right, (((1,), (1,)), ((), ())), preferred_element_...  20.5 us
    ppermute x14, starting transfers between devices, cross(): return lax.ppermute(bucket, 'fsdp', [(i, i ^ d) for i in range(peer_count)])  20.5 us
    dot_general x6, matrix products, dot_nn(): return jnp.dot(left, right, preferred_element_type=F32)  19.5 us
    pallas_call x6, Pallas kernels, add(): pl.pallas_call(kernel, out_shape=shapes, in_specs=[pl.BlockSpec(memory_sp...  18 us
    pallas_call x2, Pallas kernels, weight_grads(): pl.pallas_call(kernel, out_shape=[shape, shape], grid_spec=pltpu.Prefetch...  16.1 us
  transfers between devices with their start and end apart: 47, of which 21 were waited for; matrix products, arithmetic and copies ran while one was open for 21% of the time, Pallas kernels for 24%

commit v1 on v0

--- a/solution.py
+++ b/solution.py
@@ -1,4 +1,4 @@
-import functools
+import math
 
 import jax
 import jax.numpy as jnp
@@ -616,8 +616,13 @@
     )
 
 
-def gelu_tanh(values):
-    return jax.nn.gelu(values, approximate=True)
+def gelu_and_slope(values):
+    scale, cubic = math.sqrt(2.0 / math.pi), 0.044715
+    square = values * values
+    bent = jnp.tanh(scale * (values + cubic * (square * values)))
+    half = 0.5 * (1.0 + bent)
+    slope = half + 0.5 * values * (1.0 - bent * bent) * (scale * (1.0 + 3.0 * cubic * square))
+    return values * half, slope
 
 
 def layout(lengths, row_count, tile_rows):
@@ -778,8 +783,8 @@
     hat_two, rho_two = normalize(mid_stream)
     norm_two = (hat_two * gain_two + shift_two).astype(BF16)
     pre_act = dot_nn(norm_two, mat_up) + bias_up
-    act_value, gelu_pull = jax.vjp(gelu_tanh, pre_act)
-    act_low = lax.optimization_barrier(act_value.astype(BF16))
+    act_value, gelu_slope = gelu_and_slope(pre_act)
+    act_low, gelu_slope = lax.optimization_barrier((act_value.astype(BF16), gelu_slope))
     result = (mid_stream + dot_nn(act_low, mat_down) + bias_down).astype(BF16)
     mixed_buckets = deal("return_mixed", origin, result.reshape(tiled), peer_count)
     got_mixed = lax.all_to_all(mixed_buckets, "fsdp", split_axis=0, concat_axis=0, tiled=True)
@@ -793,7 +798,7 @@
     sum_down = lax.psum_scatter(d_w_down, AXES, scatter_dimension=0, tiled=True)
 
     d_act = dot_nt(after(grad_out_low, d_w_down), mat_down)
-    d_pre = gelu_pull(d_act)[0].astype(BF16)
+    d_pre = (d_act * gelu_slope).astype(BF16)
 
     d_up_bias = col_sums(d_pre)
     d_norm_two = dot_nt(d_pre, mat_up)

time: 362 us -> 358 us (0.989)
    ppermute x29, waiting for transfers between devices: 31.5 us -> 26.3 us  [swap(): return lax.ppermute(value, axis, pairs)]
  transfers between devices with their start and end apart: 47 -> 47, of which waited for: 21 -> 18; matrix products, arithmetic and copies ran while one was open for 21% -> 21% of each run, Pallas kernels for 24% -> 24%
where the time goes in v1:
time: 358 us; the launch traced here: 357 us
  waiting for transfers between devices  97.5 us (27%)
  Pallas kernels  86.1 us (24%)
  starting transfers between devices  72 us (20%)
  matrix products  46 us (13%)
  other arithmetic  22 us (6%)
  local copies, waits for them, and re-layouts  17.5 us (5%)
  between operations  15.4 us (4%)
    ppermute x14, waiting for transfers between devices, cross(): return lax.ppermute(bucket, 'fsdp', [(i, i ^ d) for i in range(peer_count)])  47.5 us
    ppermute x29, starting transfers between devices, swap(): return lax.ppermute(value, axis, pairs)  41.1 us
    ppermute x29, waiting for transfers between devices, swap(): return lax.ppermute(value, axis, pairs)  26.3 us
    dot_general x6, matrix products, dot_nn(): return jnp.dot(left, right, preferred_element_type=F32)  21.4 us
    ppermute x14, starting transfers between devices, cross(): return lax.ppermute(bucket, 'fsdp', [(i, i ^ d) for i in range(peer_count)])  18.7 us
    pallas_call x6, Pallas kernels, add(): pl.pallas_call(kernel, out_shape=shapes, in_specs=[pl.BlockSpec(memory_sp...  17.9 us
    dot_general x4, matrix products, dot_nt(): lax.dot_general(left, right, (((1,), (1,)), ((), ())), preferred_element_...  17.7 us
    reduce_scatter x1, waiting for transfers between devices, per_device(): sum_down = lax.psum_scatter(d_w_down, AXES, scatter_dimension=0, tiled=True)  16.3 us
  transfers between devices with their start and end apart: 47, of which 18 were waited for; matrix products, arithmetic and copies ran while one was open for 21% of the time, Pallas kernels for 24%

profile of v1, /device:TPU:0, one launch (start us, length us, event | category | flops | bytes accessed | tf_op | source)
XLA Modules:
  0.0 356.5 jit_solution(14192762667039593179)
XLA Ops:
  12.0 4.1 %collective-permute-start = (bf16[1,24,2432]{2,1,0:T(8,128)(2,1)S(1)}, bf16[1,24,2432]{2,1,0:T(8,128)(2,1)S(1)}, u32[]{:S(2)}, u32[]{:S(2)}) collective-permute-start(bf16[1,24,2432]{2,1,0:T(8,128)(2,1)S(1)} %pad_maximum_fusion.4), channel_id=1, source_target_pairs={{0,4},{1,5},{2,6},{3,7},{4,0},{5,1},{6,2},{7,3},{8,12},{9,13},{10,... | collective-permute-start | bytes 350216 | tf_op jit(solution)/shard_map/ppermute | solution.py:39
  16.1 2.6 deal_tokens.1
  18.9 1.8 collective-permute-start.3
  21.9 7.8 %collective-permute-start.1 = (bf16[2,24,2432]{2,1,0:T(8,128)(2,1)S(1)}, bf16[2,24,2432]{2,1,0:T(8,128)(2,1)S(1)}, u32[]{:S(2)}, u32[]{:S(2)}) collective-permute-start(bf16[2,24,2432]{2,1,0:T(8,128)(2,1)S(1)} %pad_maximum_fusion.3), channel_id=1, source_target_pairs={{0,2},{1,3},{2,0},{3,1},{4,6},{5,7},{6,4},{7,5},{8,10},{9,11},{10,... | collective-permute-start | bytes 700424 | tf_op jit(solution)/shard_map/ppermute | solution.py:39
  30.3 5.5 %collective-permute-done.2.refs_4_ = bf16[128,768]{1,0:T(8,128)(2,1)S(1)} collective-permute-done((bf16[128,768]{1,0:T(8,128)(2,1)}, bf16[128,768]{1,0:T(8,128)(2,1)S(1)}, u32[]{:S(2)}, u32[]{:S(2)}) %collective-permute-start.2) | collective-permute-done | bytes 196640 | tf_op jit(solution)/shard_map/ppermute | solution.py:707
  35.8 6.7 %collective-permute-done.1 = bf16[2,24,2432]{2,1,0:T(8,128)(2,1)S(1)} collective-permute-done((bf16[2,24,2432]{2,1,0:T(8,128)(2,1)S(1)}, bf16[2,24,2432]{2,1,0:T(8,128)(2,1)S(1)}, u32[]{:S(2)}, u32[]{:S(2)}) %collective-permute-start.1) | collective-permute-done | bytes 233504 | tf_op jit(solution)/shard_map/ppermute | solution.py:39
  45.1 3.5 collective-permute-start.6
  51.8 11.5 %collective-permute-done.7.refs_2_ = bf16[128,768]{1,0:T(8,128)(2,1)S(1)} collective-permute-done((bf16[128,768]{1,0:T(8,128)(2,1)S(1)}, bf16[128,768]{1,0:T(8,128)(2,1)S(1)}, u32[]{:S(2)}, u32[]{:S(2)}) %collective-permute-start.7) | collective-permute-done | bytes 196640 | tf_op jit(solution)/shard_map/ppermute | solution.py:707
  63.3 3.2 collective-permute-done.6.refs_6_
  70.6 15.4 %collective-permute-done.9.refs_5_ = bf16[128,768]{1,0:T(8,128)(2,1)S(1)} collective-permute-done((bf16[128,768]{1,0:T(8,128)(2,1)S(1)}, bf16[128,768]{1,0:T(8,128)(2,1)S(1)}, u32[]{:S(2)}, u32[]{:S(2)}) %collective-permute-start.9) | collective-permute-done | bytes 196640 | tf_op jit(solution)/shard_map/ppermute | solution.py:707
  87.2 3.0 take_tokens.1
  92.2 2.7 deal_cotangent.1
  96.9 5.4 %interleave.1 = (bf16[2,2,8,1,24,2304]{5,4,3,2,1,0:T(8,128)(2,1)}, bf16[2,2,8,1,24,128]{5,4,3,2,1,0:T(8,128)(2,1)}) custom-call(s32[2]{0:T(128)} %pad_add_fusion.scalar_ref.me_ref, bf16[8,24,1280]{2,1,0:T(8,128)(2,1)} %copy-done.19, bf16[8,24,1280]{2,1,0:T(8,128)(2,1)} %copy-done.24, bf16[8,24,1152]{2,1,0:T(8,128)(2,1)} %copy-done.20, ...), custom_call_target="tpu_custom_call" | custom-call | tf_op jit(solution)/shard_map/interleave/pallas_call | solution.py:79
  105.6 5.5 %fusion.8.q_ref.k_ref.v_ref = bf16[512,2304]{1,0:T(8,128)(2,1)} fusion(bf16[512,768]{1,0:T(8,128)(2,1)S(1)} %fusion.15.refs_0_, bf16[768,2304]{1,0:T(8,128)(2,1)} %bitcast.147, f32[2304]{0:T(1024)S(1)} %pad_maximum_fusion.5), kind=kOutput, calls=%fused_computation.17 | convolution fusion | flops 1814298624 | bytes 6693888 | tf_op jit(solution)/shard_map/dot_general | solution.py:495
  111.1 6.3 %all-to-all-start.1 = ((bf16[8,128,768]{2,1,0:T(8,128)(2,1)}), bf16[8,128,768]{2,1,0:T(8,128)(2,1)}, u32[]{:S(2)}, u32[]{:S(2)}) async-start(bf16[8,128,768]{2,1,0:T(8,128)(2,1)} %deal_cotangent.1), calls=%async_computation.1 | async-start | bytes 3145728 | tf_op jit(solution)/shard_map/all_to_all | solution.py:778
  117.4 10.4 %attend_forward.1 = (bf16[512,768]{1,0:T(8,128)(2,1)}, f32[6,2,512]{2,1,0:T(2,128)}) custom-call(bf16[512,2304]{1,0:T(8,128)(2,1)} %fusion.8.q_ref.k_ref.v_ref, bf16[512,2304]{1,0:T(8,128)(2,1)} %fusion.8.q_ref.k_ref.v_ref, bf16[512,2304]{1,0:T(8,128)(2,1)} %fusion.8.q_ref.k_ref.v_ref, s32[1,512]{1,0:T(1,128)} %bitcast.139, s32[512,1]{1,0:T(8,128)} %copy.43.ks_ref), custom_call_target="tpu_custom_call" | custom-call | tf_op jit(solution)/shard_map/attend_forward/pallas_call | solution.py:529
  128.5 2.6 slice.219
  131.2 4.8 %fusion.59 = (bf16[32,24,768]{2,1,0:T(8,128)(2,1)S(1)}, bf16[32,24,768]{2,1,0:T(8,128)(2,1)S(1)}, bf16[32,24,768]{2,1,0:T(8,128)(2,1)S(1)}, bf16[32,24,768]{2,1,0:T(8,128)(2,1)S(1)}, bf16[32,24,768]{2,1,0:T(8,128)(2,1)S(1)}) fusion(bf16[32,216,768]{2,1,0:T(8,128)(2,1)} %bitcast.119), kind=kLoop, calls=%fused_computation.185 | loop fusion | bytes 11796480 | tf_op jit(solution)/shard_map/slice | solution.py:699
  138.4 9.8 %fusion.7 = (f32[512,3072]{1,0:T(8,128)}, bf16[512,3072]{1,0:T(8,128)(2,1)S(1)}) fusion(f32[3072]{0:T(1024)S(1)} %fusion.27, bf16[512,768]{1,0:T(8,128)(2,1)S(1)} %add_convert_fusion.1.refs_0_, bf16[768,768]{1,0:T(8,128)(2,1)S(1)} %bitcast.127, bf16[768,768]{1,0:T(8,128)(2,1)S(1)} %bitcast.129, bf16[768,768]{1,0:T(8,128)(2,1)S(1)} %bitcast.131, ...), kind=kOutput, calls=%fused_computation.9 | convolution fusion | flops 2464677888 | bytes 14954496 | tf_op jit(solution)/shard_map/dot_general | solution.py:495
  148.3 3.5 add_convert_fusion
  151.8 2.6 return_mixed.1
  154.4 2.5 all-to-all-done.1.src
  156.9 5.8 %all-to-all-start = ((bf16[8,128,768]{2,1,0:T(8,128)(2,1)}), bf16[8,128,768]{2,1,0:T(8,128)(2,1)}, u32[]{:S(2)}, u32[]{:S(2)}) async-start(bf16[8,128,768]{2,1,0:T(8,128)(2,1)} %return_mixed.1), calls=%async_computation | async-start | bytes 3145728 | tf_op jit(solution)/shard_map/all_to_all | solution.py:790
  162.8 2.6 take_cotangent.1
  166.8 7.0 %convolution_convert_fusion = bf16[3072,768]{1,0:T(8,128)(2,1)} fusion(bf16[512,3072]{1,0:T(8,128)(2,1)} %copy-done.81, bf16[512,768]{1,0:T(8,128)(2,1)S(1)} %fusion.26), kind=kOutput, calls=%fused_computation.14 | convolution fusion | flops 2418278400 | bytes 8650752 | tf_op jit(solution)/shard_map/dot_general | solution.py:499
  173.9 6.6 %convert_reduce_fusion = (f32[3072]{0:T(1024)S(1)}, bf16[512,3072]{1,0:T(8,128)(2,1)S(1)}) fusion(f32[512,3072]{1,0:T(8,128)} %get-tuple-element.135, bf16[512,768]{1,0:T(8,128)(2,1)S(1)} %fusion.26, bf16[3072,768]{1,0:T(8,128)(2,1)} %bitcast.121), kind=kOutput, calls=%fused_computation.10 | convolution fusion | flops 2422207488 | bytes 14954496 | tf_op jit(solution)/shard_map/dot_general | solution.py:503
  180.5 3.5 multiply_reduce_fusion
  184.0 2.1 convert_reduce_fusion.3
  186.1 9.4 %weight_grads.2 = (bf16[16,24,3840]{2,1,0:T(8,128)(2,1)}, bf16[16,24,3840]{2,1,0:T(8,128)(2,1)}) custom-call(s32[2]{0:T(128)} %pad_add_fusion.scalar_ref.me_ref, bf16[512,768]{1,0:T(8,128)(2,1)} %copy-done.7, bf16[512,3072]{1,0:T(8,128)(2,1)} %copy-done.5, bf16[512,768]{1,0:T(8,128)(2,1)} %get-tuple-element.129.refs_2_, ...), custom_call_target="tpu_custom_call" | custom-call | tf_op jit(solution)/shard_map/weight_grads/pallas_call | solution.py:383
  195.5 4.8 %all-to-all-done.src = bf16[8,128,768]{2,1,0:T(8,128)(2,1)} async-done(((bf16[8,128,768]{2,1,0:T(8,128)(2,1)}), bf16[8,128,768]{2,1,0:T(8,128)(2,1)}, u32[]{:S(2)}, u32[]{:S(2)}) %all-to-all-start) | async-done | bytes 1572896 | tf_op jit(solution)/shard_map/all_to_all | solution.py:790
  200.3 1.7 convolution_convert_fusion.1.d_ref
  202.0 4.7 %add_step.6 = (bf16[8,24,1920]{2,1,0:T(8,128)(2,1)}, bf16[8,24,1920]{2,1,0:T(8,128)(2,1)}, bf16[8,24,1920]{2,1,0:T(8,128)(2,1)}, bf16[8,24,1920]{2,1,0:T(8,128)(2,1)}) custom-call(bf16[16,24,3840]{2,1,0:T(8,128)(2,1)} %get-tuple-element.138.refs_0_, bf16[16,24,3840]{2,1,0:T(8,128)(2,1)} %collective-permute-done.17.refs_1_), custom_call_target="tpu_custom_call" | custom-call | tf_op jit(solution)/shard_map/add_step/pallas_call | solution.py:484
  206.7 1.6 collective-permute-start.18
  209.2 14.6 %attend_backward.1.refs_1_ = bf16[512,2304]{1,0:T(8,128)(2,1)} custom-call(bf16[512,2304]{1,0:T(8,128)(2,1)} %fusion.8.q_ref.k_ref.v_ref, bf16[512,2304]{1,0:T(8,128)(2,1)} %fusion.8.q_ref.k_ref.v_ref, bf16[512,2304]{1,0:T(8,128)(2,1)} %fusion.8.q_ref.k_ref.v_ref, bf16[512,768]{1,0:T(8,128)(2,1)} %convolution_convert_fusion.1.d_ref, ...), custom_call_target="tpu_custom_call" | custom-call | tf_op jit(solution)/shard_map/attend_backward/pallas_call | solution.py:583
  223.8 2.7 collective-permute-done.18.refs_2_
  226.5 2.2 collective-permute-done.19.refs_3_
  229.6 3.0 add_step.7
  232.6 6.7 %weight_grads.3 = (bf16[16,24,2304]{2,1,0:T(8,128)(2,1)}, bf16[16,24,2304]{2,1,0:T(8,128)(2,1)}) custom-call(s32[2]{0:T(128)} %pad_add_fusion.scalar_ref.me_ref, bf16[512,768]{1,0:T(8,128)(2,1)} %copy-done.6, bf16[512,2304]{1,0:T(8,128)(2,1)} %attend_backward.1.refs_1_), custom_call_target="tpu_custom_call" | custom-call | tf_op jit(solution)/shard_map/weight_grads/pallas_call | solution.py:383
  239.4 1.7 collective-permute-start.21
  241.0 6.0 %fusion.21 = (f32[768]{0:T(1024)}, f32[512]{0:T(512)S(1)}, f32[512]{0:T(512)S(1)}, f32[768]{0:T(1024)}, f32[512,768]{1,0:T(8,128)}) fusion(f32[512]{0:T(512)S(1)} %rsqrt_bitcast_fusion, f32[512]{0:T(512)S(1)} %get-tuple-element.246, bf16[4,128,768]{2,1,0:T(8,128)(2,1)S(1)} %copy-done, f32[768]{0:T(1024)S(1)} %get-tuple-element.214, ...), kind=kOutput, calls=%fused_computation.35 | convolution fusion | flops 1815868928 | bytes 8274944 | tf_op jit(solution)/shard_map/dot_general | solution.py:503
  247.0 3.3 add_step.8
  250.3 2.0 collective-permute-start.23
  252.8 3.3 fusion.20
  256.1 2.8 return_gradient.1
  258.9 2.3 collective-permute-start.25
  264.6 8.5 %collective-permute-done.25.refs_4_ = bf16[128,768]{1,0:T(8,128)(2,1)S(1)} collective-permute-done((bf16[128,768]{1,0:T(8,128)(2,1)}, bf16[128,768]{1,0:T(8,128)(2,1)S(1)}, u32[]{:S(2)}, u32[]{:S(2)}) %collective-permute-start.25) | collective-permute-done | bytes 196640 | tf_op jit(solution)/shard_map/ppermute | solution.py:707
  273.0 2.0 collective-permute-start.30
  275.1 16.3 %reduce-scatter.2.cloned.1.call-done = bf16[96,768]{1,0:T(8,128)(2,1)} async-done(((bf16[3072,768]{1,0:T(8,128)(2,1)}), bf16[96,768]{1,0:T(8,128)(2,1)}) %reduce-scatter.2.cloned.1.call-update) | async-done | bytes 147472 | tf_op jit(solution)/shard_map/reduce_scatter | solution.py:798
  291.4 2.4 add_step.9
  295.7 1.6 collective-permute-start.33
  297.3 2.4 add_step.11
  299.7 2.2 collective-permute-done.33
  303.9 3.1 collective-permute-done.34
  308.5 2.0 collective-permute-start.29
  310.5 1.8 collective-permute-start.31
  313.2 5.9 %collective-permute-start.37 = (f32[12,768]{1,0:T(8,128)S(1)}, f32[12,768]{1,0:T(8,128)S(1)}, u32[]{:S(2)}, u32[]{:S(2)}) collective-permute-start(f32[12,768]{1,0:T(8,128)S(1)} %add.245), channel_id=1, source_target_pairs={{0,2},{1,3},{2,0},{3,1},{4,6},{5,7},{6,4},{7,5},{8,10},{9,11},{10,... | collective-permute-start | bytes 110600 | tf_op jit(solution)/shard_map/ppermute | solution.py:39
  319.1 2.6 take_mixed.1
  322.5 2.6 collective-permute-done.31.refs_7_
  325.8 2.6 take_gradient.1
  328.5 2.1 add_step.10
  330.6 2.0 collective-permute-start.38
  333.3 6.1 %collective-permute-done.38 = bf16[2,24,2304]{2,1,0:T(8,128)(2,1)S(1)} collective-permute-done((bf16[2,24,2304]{2,1,0:T(8,128)(2,1)}, bf16[2,24,2304]{2,1,0:T(8,128)(2,1)S(1)}, u32[]{:S(2)}, u32[]{:S(2)}) %collective-permute-start.38) | collective-permute-done | bytes 221216 | tf_op jit(solution)/shard_map/ppermute | solution.py:39
  340.7 2.6 collective-permute-start.40
  343.3 3.1 collective-permute-done.39
  (324 shorter events, 47.4 us)
Async XLA Ops:
  7.3 121.2 %all-gather.3.cloned.1.call-start = ((), (), s32[]{:S(2)}) async-start(), calls=%async_computation.4 | async-start | bytes 10948608 | tf_op jit(solution)/shard_map/all_gather | solution.py:696
  12.0 9.8 %collective-permute-start = (bf16[1,24,2432]{2,1,0:T(8,128)(2,1)S(1)}, bf16[1,24,2432]{2,1,0:T(8,128)(2,1)S(1)}, u32[]{:S(2)}, u32[]{:S(2)}) collective-permute-start(bf16[1,24,2432]{2,1,0:T(8,128)(2,1)S(1)} %pad_maximum_fusion.4), channel_id=1, source_target_pairs={{0,4},{1,5},{2,6},{3,7},{4,0},{5,1},{6,2},{7,3},{8,12},{9,13},{10,... | collective-permute-start | bytes 350216 | tf_op jit(solution)/shard_map/ppermute | solution.py:39
  18.8 26.3 %copy-start.79 = (bf16[128,768]{1,0:T(8,128)(2,1)S(1)}, bf16[128,768]{1,0:T(8,128)(2,1)}, u32[]{:S(2)}) copy-start(bf16[128,768]{1,0:T(8,128)(2,1)} %get-tuple-element.113) | copy-start | bytes 589828
  18.8 26.3 %copy-start.78 = (bf16[128,768]{1,0:T(8,128)(2,1)S(1)}, bf16[128,768]{1,0:T(8,128)(2,1)}, u32[]{:S(2)}) copy-start(bf16[128,768]{1,0:T(8,128)(2,1)} %get-tuple-element.111) | copy-start | bytes 589828
  18.8 32.5 %copy-start.77 = (bf16[128,768]{1,0:T(8,128)(2,1)S(1)}, bf16[128,768]{1,0:T(8,128)(2,1)}, u32[]{:S(2)}) copy-start(bf16[128,768]{1,0:T(8,128)(2,1)} %get-tuple-element.120) | copy-start | bytes 589828
  18.8 44.5 %copy-start.75 = (bf16[128,768]{1,0:T(8,128)(2,1)S(1)}, bf16[128,768]{1,0:T(8,128)(2,1)}, u32[]{:S(2)}) copy-start(bf16[128,768]{1,0:T(8,128)(2,1)} %get-tuple-element.118) | copy-start | bytes 589828
  18.8 17.0 %collective-permute-start.2 = (bf16[128,768]{1,0:T(8,128)(2,1)}, bf16[128,768]{1,0:T(8,128)(2,1)S(1)}, u32[]{:S(2)}, u32[]{:S(2)}) collective-permute-start(bf16[128,768]{1,0:T(8,128)(2,1)} %get-tuple-element.106), channel_id=1, source_target_pairs={{0,4},{1,5},{2,6},{3,7},{4,0},{5,1},{6,2},{7,3},{8,12},{9,13},{10,... | collective-permute-start | bytes 589832 | tf_op jit(solution)/shard_map/ppermute | solution.py:707
  18.9 16.9 %collective-permute-start.3 = (bf16[128,768]{1,0:T(8,128)(2,1)}, bf16[128,768]{1,0:T(8,128)(2,1)S(1)}, u32[]{:S(2)}, u32[]{:S(2)}) collective-permute-start(bf16[128,768]{1,0:T(8,128)(2,1)} %get-tuple-element.107), channel_id=1, source_target_pairs={{0,1},{1,0},{2,3},{3,2},{4,5},{5,4},{6,7},{7,6},{8,9},{9,8},{10,11... | collective-permute-start | bytes 589832 | tf_op jit(solution)/shard_map/ppermute | solution.py:707
  21.1 45.4 %copy-start.49 = (s32[512]{0:T(512)}, s32[512]{0:T(512)S(1)}, u32[]{:S(2)}) copy-start(s32[512]{0:T(512)S(1)} %get-tuple-element.217) | copy-start | bytes 6148
  21.9 20.7 %collective-permute-start.1 = (bf16[2,24,2432]{2,1,0:T(8,128)(2,1)S(1)}, bf16[2,24,2432]{2,1,0:T(8,128)(2,1)S(1)}, u32[]{:S(2)}, u32[]{:S(2)}) collective-permute-start(bf16[2,24,2432]{2,1,0:T(8,128)(2,1)S(1)} %pad_maximum_fusion.3), channel_id=1, source_target_pairs={{0,2},{1,3},{2,0},{3,1},{4,6},{5,7},{6,4},{7,5},{8,10},{9,11},{10,... | collective-permute-start | bytes 700424 | tf_op jit(solution)/shard_map/ppermute | solution.py:39
  35.8 30.7 %copy-start.35 = (bf16[128,768]{1,0:T(8,128)(2,1)}, bf16[128,768]{1,0:T(8,128)(2,1)S(1)}, u32[]{:S(2)}) copy-start(bf16[128,768]{1,0:T(8,128)(2,1)S(1)} %collective-permute-done.2.refs_4_) | copy-start | bytes 589828
  35.8 30.7 %copy-start.36 = (bf16[128,768]{1,0:T(8,128)(2,1)}, bf16[128,768]{1,0:T(8,128)(2,1)S(1)}, u32[]{:S(2)}) copy-start(bf16[128,768]{1,0:T(8,128)(2,1)S(1)} %collective-permute-done.3.refs_1_) | copy-start | bytes 589828
  42.6 27.3 %copy-start.62 = (s32[8]{0:T(128)S(1)}, s32[8]{0:T(128)}, u32[]{:S(2)}) copy-start(s32[8]{0:T(128)} %constant.113.clone) | copy-start | bytes 100
  42.6 23.8 %collective-permute-start.4 = (bf16[4,24,1280]{2,1,0:T(8,128)(2,1)S(1)}, bf16[4,24,1280]{2,1,0:T(8,128)(2,1)S(1)}, u32[]{:S(2)}, u32[]{:S(2)}) collective-permute-start(bf16[4,24,1280]{2,1,0:T(8,128)(2,1)S(1)} %slice.205), channel_id=1, source_target_pairs={{0,16},{8,24},{16,0},{24,8},{1,17},{9,25},{17,1},{25,9},{2,18},{10... | collective-permute-start | bytes 737288 | tf_op jit(solution)/shard_map/ppermute | solution.py:39
  45.0 18.2 %collective-permute-start.7 = (bf16[128,768]{1,0:T(8,128)(2,1)S(1)}, bf16[128,768]{1,0:T(8,128)(2,1)S(1)}, u32[]{:S(2)}, u32[]{:S(2)}) collective-permute-start(bf16[128,768]{1,0:T(8,128)(2,1)S(1)} %copy-done.79), channel_id=1, source_target_pairs={{0,2},{1,3},{2,0},{3,1},{4,6},{5,7},{6,4},{7,5},{8,10},{9,11},{10,... | collective-permute-start | bytes 589832 | tf_op jit(solution)/shard_map/ppermute | solution.py:707
  45.1 21.4 %collective-permute-start.6 = (bf16[128,768]{1,0:T(8,128)(2,1)S(1)}, bf16[128,768]{1,0:T(8,128)(2,1)S(1)}, u32[]{:S(2)}, u32[]{:S(2)}) collective-permute-start(bf16[128,768]{1,0:T(8,128)(2,1)S(1)} %copy-done.78), channel_id=1, source_target_pairs={{0,6},{1,7},{2,4},{3,5},{4,2},{5,3},{6,0},{7,1},{8,14},{9,15},{10,... | collective-permute-start | bytes 589832 | tf_op jit(solution)/shard_map/ppermute | solution.py:707
  48.6 17.9 %collective-permute-start.5 = (bf16[4,24,1152]{2,1,0:T(8,128)(2,1)S(1)}, bf16[4,24,1152]{2,1,0:T(8,128)(2,1)S(1)}, u32[]{:S(2)}, u32[]{:S(2)}) collective-permute-start(bf16[4,24,1152]{2,1,0:T(8,128)(2,1)S(1)} %slice.206), channel_id=1, source_target_pairs={{0,1},{1,0},{2,3},{3,2},{4,5},{5,4},{6,7},{7,6},{8,9},{9,8},{10,11... | collective-permute-start | bytes 663560 | tf_op jit(solution)/shard_map/ppermute | solution.py:39
  51.3 34.7 %collective-permute-start.9 = (bf16[128,768]{1,0:T(8,128)(2,1)S(1)}, bf16[128,768]{1,0:T(8,128)(2,1)S(1)}, u32[]{:S(2)}, u32[]{:S(2)}) collective-permute-start(bf16[128,768]{1,0:T(8,128)(2,1)S(1)} %copy-done.77), channel_id=1, source_target_pairs={{0,5},{1,4},{2,7},{3,6},{4,1},{5,0},{6,3},{7,2},{8,13},{9,12},{10,... | collective-permute-start | bytes 589832 | tf_op jit(solution)/shard_map/ppermute | solution.py:707
  63.3 23.2 %copy-start.39 = (bf16[128,768]{1,0:T(8,128)(2,1)}, bf16[128,768]{1,0:T(8,128)(2,1)S(1)}, u32[]{:S(2)}) copy-start(bf16[128,768]{1,0:T(8,128)(2,1)S(1)} %collective-permute-done.7.refs_2_) | copy-start | bytes 589828
  63.3 22.7 %collective-permute-start.8 = (bf16[128,768]{1,0:T(8,128)(2,1)S(1)}, bf16[128,768]{1,0:T(8,128)(2,1)S(1)}, u32[]{:S(2)}, u32[]{:S(2)}) collective-permute-start(bf16[128,768]{1,0:T(8,128)(2,1)S(1)} %copy-done.75), channel_id=1, source_target_pairs={{0,3},{1,2},{2,1},{3,0},{4,7},{5,6},{6,5},{7,4},{8,11},{9,10},{10,... | collective-permute-start | bytes 589832 | tf_op jit(solution)/shard_map/ppermute | solution.py:707
  66.4 20.1 %copy-start.40 = (bf16[128,768]{1,0:T(8,128)(2,1)}, bf16[128,768]{1,0:T(8,128)(2,1)S(1)}, u32[]{:S(2)}) copy-start(bf16[128,768]{1,0:T(8,128)(2,1)S(1)} %collective-permute-done.6.refs_6_) | copy-start | bytes 589828
  66.5 23.6 %copy-start.19 = (bf16[8,24,1280]{2,1,0:T(8,128)(2,1)}, bf16[8,24,1280]{2,1,0:T(8,128)(2,1)S(1)}, u32[]{:S(2)}) copy-start(bf16[8,24,1280]{2,1,0:T(8,128)(2,1)S(1)} %constant_dynamic-update-slice_fusion.4.refs_0_) | copy-start | bytes 1474564
  66.6 25.2 %collective-permute-start.11 = (bf16[8,24,1280]{2,1,0:T(8,128)(2,1)S(1)}, bf16[8,24,1280]{2,1,0:T(8,128)(2,1)S(1)}, u32[]{:S(2)}, u32[]{:S(2)}) collective-permute-start(bf16[8,24,1280]{2,1,0:T(8,128)(2,1)S(1)} %constant_dynamic-update-slice_fusion.4.refs_0_), channel_id=1, source_target_pairs={{0,1},{1,0},{2,3},{3,2},{4,5},{5,4},{6,7},{7,6},{8,9},{9,8},{10,11... | collective-permute-start | bytes 1474568 | tf_op jit(solution)/shard_map/ppermute | solution.py:39
  68.2 23.4 %copy-start.20 = (bf16[8,24,1152]{2,1,0:T(8,128)(2,1)}, bf16[8,24,1152]{2,1,0:T(8,128)(2,1)S(1)}, u32[]{:S(2)}) copy-start(bf16[8,24,1152]{2,1,0:T(8,128)(2,1)S(1)} %constant_dynamic-update-slice_fusion.2.refs_2_) | copy-start | bytes 1327108
  68.2 23.3 %collective-permute-start.12 = (bf16[8,24,1152]{2,1,0:T(8,128)(2,1)S(1)}, bf16[8,24,1152]{2,1,0:T(8,128)(2,1)}, u32[]{:S(2)}, u32[]{:S(2)}) collective-permute-start(bf16[8,24,1152]{2,1,0:T(8,128)(2,1)S(1)} %constant_dynamic-update-slice_fusion.2.refs_2_), channel_id=1, source_target_pairs={{0,16},{8,24},{16,0},{24,8},{1,17},{9,25},{17,1},{25,9},{2,18},{10... | collective-permute-start | bytes 1327112 | tf_op jit(solution)/shard_map/ppermute | solution.py:39
  68.3 18.2 %collective-permute-start.10 = (bf16[128,768]{1,0:T(8,128)(2,1)}, bf16[128,768]{1,0:T(8,128)(2,1)S(1)}, u32[]{:S(2)}, u32[]{:S(2)}) collective-permute-start(bf16[128,768]{1,0:T(8,128)(2,1)} %get-tuple-element.122), channel_id=1, source_target_pairs={{0,7},{1,6},{2,5},{3,4},{4,3},{5,2},{6,1},{7,0},{8,15},{9,14},{10,... | collective-permute-start | bytes 589832 | tf_op jit(solution)/shard_map/ppermute | solution.py:707
  86.0 9.3 %collective-permute-start.15 = (bf16[8,24,1152]{2,1,0:T(8,128)(2,1)S(1)}, bf16[8,24,1152]{2,1,0:T(8,128)(2,1)}, u32[]{:S(2)}, u32[]{:S(2)}) collective-permute-start(bf16[8,24,1152]{2,1,0:T(8,128)(2,1)S(1)} %constant_dynamic-update-slice_fusion.2.refs_2_), channel_id=1, source_target_pairs={{0,8},{8,0},{16,24},{24,16},{1,9},{9,1},{17,25},{25,17},{2,10},{10... | collective-permute-start | bytes 1327112 | tf_op jit(solution)/shard_map/ppermute | solution.py:39
  86.0 9.3 %collective-permute-start.13 = (bf16[8,24,1280]{2,1,0:T(8,128)(2,1)S(1)}, bf16[8,24,1280]{2,1,0:T(8,128)(2,1)S(1)}, u32[]{:S(2)}, u32[]{:S(2)}) collective-permute-start(bf16[8,24,1280]{2,1,0:T(8,128)(2,1)S(1)} %constant_dynamic-update-slice_fusion.4.refs_0_), channel_id=1, source_target_pairs={{0,8},{8,0},{16,24},{24,16},{1,9},{9,1},{17,25},{25,17},{2,10},{10... | collective-permute-start | bytes 1474568 | tf_op jit(solution)/shard_map/ppermute | solution.py:39
  91.6 3.7 %collective-permute-start.16 = (bf16[8,24,1152]{2,1,0:T(8,128)(2,1)}, bf16[8,24,1152]{2,1,0:T(8,128)(2,1)}, u32[]{:S(2)}, u32[]{:S(2)}) collective-permute-start(bf16[8,24,1152]{2,1,0:T(8,128)(2,1)} %collective-permute-done.12.refs_3_), channel_id=1, source_target_pairs={{0,8},{8,0},{16,24},{24,16},{1,9},{9,1},{17,25},{25,17},{2,10},{10... | collective-permute-start | bytes 1327112 | tf_op jit(solution)/shard_map/ppermute | solution.py:39
  91.8 3.6 %collective-permute-start.14 = (bf16[8,24,1280]{2,1,0:T(8,128)(2,1)S(1)}, bf16[8,24,1280]{2,1,0:T(8,128)(2,1)S(1)}, u32[]{:S(2)}, u32[]{:S(2)}) collective-permute-start(bf16[8,24,1280]{2,1,0:T(8,128)(2,1)S(1)} %collective-permute-done.11.refs_1_), channel_id=1, source_target_pairs={{0,8},{8,0},{16,24},{24,16},{1,9},{9,1},{17,25},{25,17},{2,10},{10... | collective-permute-start | bytes 1474568 | tf_op jit(solution)/shard_map/ppermute | solution.py:39
  111.1 45.9 %all-to-all-start.1 = ((bf16[8,128,768]{2,1,0:T(8,128)(2,1)}), bf16[8,128,768]{2,1,0:T(8,128)(2,1)}, u32[]{:S(2)}, u32[]{:S(2)}) async-start(bf16[8,128,768]{2,1,0:T(8,128)(2,1)} %deal_cotangent.1), calls=%async_computation.1 | async-start | bytes 3145728 | tf_op jit(solution)/shard_map/all_to_all | solution.py:778
  156.9 43.4 %all-to-all-start = ((bf16[8,128,768]{2,1,0:T(8,128)(2,1)}), bf16[8,128,768]{2,1,0:T(8,128)(2,1)}, u32[]{:S(2)}, u32[]{:S(2)}) async-start(bf16[8,128,768]{2,1,0:T(8,128)(2,1)} %return_mixed.1), calls=%async_computation | async-start | bytes 3145728 | tf_op jit(solution)/shard_map/all_to_all | solution.py:790
  162.8 128.6 %reduce-scatter.2.cloned.1.call-start = ((), (), s32[]{:S(2)}) async-start(), calls=%async_computation.3 | async-start | bytes 4866048 | tf_op jit(solution)/shard_map/reduce_scatter | solution.py:798
  195.5 6.5 %collective-permute-start.17 = (bf16[16,24,3840]{2,1,0:T(8,128)(2,1)}, bf16[16,24,3840]{2,1,0:T(8,128)(2,1)}, u32[]{:S(2)}, u32[]{:S(2)}) collective-permute-start(bf16[16,24,3840]{2,1,0:T(8,128)(2,1)} %get-tuple-element.136), channel_id=1, source_target_pairs={{0,8},{8,0},{16,24},{24,16},{1,9},{9,1},{17,25},{25,17},{2,10},{10... | collective-permute-start | bytes 8847368 | tf_op jit(solution)/shard_map/ppermute | solution.py:39
  206.7 19.8 %collective-permute-start.18 = (bf16[8,24,1920]{2,1,0:T(8,128)(2,1)}, bf16[8,24,1920]{2,1,0:T(8,128)(2,1)S(1)}, u32[]{:S(2)}, u32[]{:S(2)}) collective-permute-start(bf16[8,24,1920]{2,1,0:T(8,128)(2,1)} %get-tuple-element.140), channel_id=1, source_target_pairs={{0,1},{1,0},{2,3},{3,2},{4,5},{5,4},{6,7},{7,6},{8,9},{9,8},{10,11... | collective-permute-start | bytes 2211848 | tf_op jit(solution)/shard_map/ppermute | solution.py:39
  208.3 20.4 %collective-permute-start.19 = (bf16[8,24,1920]{2,1,0:T(8,128)(2,1)}, bf16[8,24,1920]{2,1,0:T(8,128)(2,1)S(1)}, u32[]{:S(2)}, u32[]{:S(2)}) collective-permute-start(bf16[8,24,1920]{2,1,0:T(8,128)(2,1)} %get-tuple-element.141), channel_id=1, source_target_pairs={{0,16},{8,24},{16,0},{24,8},{1,17},{9,25},{17,1},{25,9},{2,18},{10... | collective-permute-start | bytes 2211848 | tf_op jit(solution)/shard_map/ppermute | solution.py:39
  239.4 7.7 %collective-permute-start.20 = (bf16[16,24,2304]{2,1,0:T(8,128)(2,1)}, bf16[16,24,2304]{2,1,0:T(8,128)(2,1)}, u32[]{:S(2)}, u32[]{:S(2)}) collective-permute-start(bf16[16,24,2304]{2,1,0:T(8,128)(2,1)} %get-tuple-element.151), channel_id=1, source_target_pairs={{0,8},{8,0},{16,24},{24,16},{1,9},{9,1},{17,25},{25,17},{2,10},{10... | collective-permute-start | bytes 5308424 | tf_op jit(solution)/shard_map/ppermute | solution.py:39
  239.4 16.7 %collective-permute-start.21 = (bf16[4,24,1920]{2,1,0:T(8,128)(2,1)}, bf16[4,24,1920]{2,1,0:T(8,128)(2,1)S(1)}, u32[]{:S(2)}, u32[]{:S(2)}) collective-permute-start(bf16[4,24,1920]{2,1,0:T(8,128)(2,1)} %get-tuple-element.148), channel_id=1, source_target_pairs={{0,16},{8,24},{16,0},{24,8},{1,17},{9,25},{17,1},{25,9},{2,18},{10... | collective-permute-start | bytes 1105928 | tf_op jit(solution)/shard_map/ppermute | solution.py:39
  241.0 15.1 %collective-permute-start.22 = (bf16[4,24,1920]{2,1,0:T(8,128)(2,1)}, bf16[4,24,1920]{2,1,0:T(8,128)(2,1)}, u32[]{:S(2)}, u32[]{:S(2)}) collective-permute-start(bf16[4,24,1920]{2,1,0:T(8,128)(2,1)} %get-tuple-element.149), channel_id=1, source_target_pairs={{0,1},{1,0},{2,3},{3,2},{4,5},{5,4},{6,7},{7,6},{8,9},{9,8},{10,11... | collective-permute-start | bytes 1105928 | tf_op jit(solution)/shard_map/ppermute | solution.py:39
  250.3 24.7 %collective-permute-start.23 = (bf16[8,24,1152]{2,1,0:T(8,128)(2,1)}, bf16[8,24,1152]{2,1,0:T(8,128)(2,1)}, u32[]{:S(2)}, u32[]{:S(2)}) collective-permute-start(bf16[8,24,1152]{2,1,0:T(8,128)(2,1)} %get-tuple-element.155), channel_id=1, source_target_pairs={{0,1},{1,0},{2,3},{3,2},{4,5},{5,4},{6,7},{7,6},{8,9},{9,8},{10,11... | collective-permute-start | bytes 1327112 | tf_op jit(solution)/shard_map/ppermute | solution.py:39
  252.3 22.7 %collective-permute-start.24 = (bf16[8,24,1152]{2,1,0:T(8,128)(2,1)}, bf16[8,24,1152]{2,1,0:T(8,128)(2,1)}, u32[]{:S(2)}, u32[]{:S(2)}) collective-permute-start(bf16[8,24,1152]{2,1,0:T(8,128)(2,1)} %get-tuple-element.156), channel_id=1, source_target_pairs={{0,16},{8,24},{16,0},{24,8},{1,17},{9,25},{17,1},{25,9},{2,18},{10... | collective-permute-start | bytes 1327112 | tf_op jit(solution)/shard_map/ppermute | solution.py:39
  258.9 14.1 %collective-permute-start.25 = (bf16[128,768]{1,0:T(8,128)(2,1)}, bf16[128,768]{1,0:T(8,128)(2,1)S(1)}, u32[]{:S(2)}, u32[]{:S(2)}) collective-permute-start(bf16[128,768]{1,0:T(8,128)(2,1)} %get-tuple-element.162), channel_id=1, source_target_pairs={{0,4},{1,5},{2,6},{3,7},{4,0},{5,1},{6,2},{7,3},{8,12},{9,13},{10,... | collective-permute-start | bytes 589832 | tf_op jit(solution)/shard_map/ppermute | solution.py:707
  263.0 32.7 %collective-permute-start.32 = (f32[12,768]{1,0:T(8,128)S(1)}, f32[12,768]{1,0:T(8,128)S(1)}, u32[]{:S(2)}, u32[]{:S(2)}) collective-permute-start(f32[12,768]{1,0:T(8,128)S(1)} %concatenate.54), channel_id=1, source_target_pairs={{0,8},{8,0},{16,24},{24,16},{1,9},{9,1},{17,25},{25,17},{2,10},{10... | collective-permute-start | bytes 110600 | tf_op jit(solution)/shard_map/ppermute | solution.py:39
  263.1 39.8 %collective-permute-start.27 = (bf16[128,768]{1,0:T(8,128)(2,1)}, bf16[128,768]{1,0:T(8,128)(2,1)S(1)}, u32[]{:S(2)}, u32[]{:S(2)}) collective-permute-start(bf16[128,768]{1,0:T(8,128)(2,1)} %get-tuple-element.160), channel_id=1, source_target_pairs={{0,2},{1,3},{2,0},{3,1},{4,6},{5,7},{6,4},{7,5},{8,10},{9,11},{10,... | collective-permute-start | bytes 589832 | tf_op jit(solution)/shard_map/ppermute | solution.py:707
  273.0 26.6 %copy-start.34 = (bf16[128,768]{1,0:T(8,128)(2,1)}, bf16[128,768]{1,0:T(8,128)(2,1)S(1)}, u32[]{:S(2)}) copy-start(bf16[128,768]{1,0:T(8,128)(2,1)S(1)} %collective-permute-done.25.refs_4_) | copy-start | bytes 589828
  273.0 30.6 %collective-permute-start.30 = (bf16[128,768]{1,0:T(8,128)(2,1)}, bf16[128,768]{1,0:T(8,128)(2,1)S(1)}, u32[]{:S(2)}, u32[]{:S(2)}) collective-permute-start(bf16[128,768]{1,0:T(8,128)(2,1)} %get-tuple-element.164), channel_id=1, source_target_pairs={{0,6},{1,7},{2,4},{3,5},{4,2},{5,3},{6,0},{7,1},{8,14},{9,15},{10,... | collective-permute-start | bytes 589832 | tf_op jit(solution)/shard_map/ppermute | solution.py:707
  293.8 14.7 %collective-permute-start.35 = (bf16[4,24,1152]{2,1,0:T(8,128)(2,1)}, bf16[4,24,1152]{2,1,0:T(8,128)(2,1)S(1)}, u32[]{:S(2)}, u32[]{:S(2)}) collective-permute-start(bf16[4,24,1152]{2,1,0:T(8,128)(2,1)} %get-tuple-element.177), channel_id=1, source_target_pairs={{0,16},{8,24},{16,0},{24,8},{1,17},{9,25},{17,1},{25,9},{2,18},{10... | collective-permute-start | bytes 663560 | tf_op jit(solution)/shard_map/ppermute | solution.py:39
  295.2 15.3 %collective-permute-start.36 = (bf16[4,24,1152]{2,1,0:T(8,128)(2,1)}, bf16[4,24,1152]{2,1,0:T(8,128)(2,1)S(1)}, u32[]{:S(2)}, u32[]{:S(2)}) collective-permute-start(bf16[4,24,1152]{2,1,0:T(8,128)(2,1)} %get-tuple-element.178), channel_id=1, source_target_pairs={{0,1},{1,0},{2,3},{3,2},{4,5},{5,4},{6,7},{7,6},{8,9},{9,8},{10,11... | collective-permute-start | bytes 663560 | tf_op jit(solution)/shard_map/ppermute | solution.py:39
  295.7 6.2 %collective-permute-start.33 = (f32[12,768]{1,0:T(8,128)S(1)}, f32[12,768]{1,0:T(8,128)S(1)}, u32[]{:S(2)}, u32[]{:S(2)}) collective-permute-start(f32[12,768]{1,0:T(8,128)S(1)} %add.243), channel_id=1, source_target_pairs={{0,1},{1,0},{2,3},{3,2},{4,5},{5,4},{6,7},{7,6},{8,9},{9,8},{10,11... | collective-permute-start | bytes 110600 | tf_op jit(solution)/shard_map/ppermute | solution.py:39
  299.7 22.1 %copy-start.48 = (bf16[96,768]{1,0:T(8,128)(2,1)S(1)}, bf16[96,768]{1,0:T(8,128)(2,1)}, u32[]{:S(2)}) copy-start(bf16[96,768]{1,0:T(8,128)(2,1)} %reduce-scatter.2.cloned.1.call-done) | copy-start | bytes 442372
  301.9 30.7 %collective-permute-start.41 = (bf16[2,24,3840]{2,1,0:T(8,128)(2,1)}, bf16[2,24,3840]{2,1,0:T(8,128)(2,1)S(1)}, u32[]{:S(2)}, u32[]{:S(2)}) collective-permute-start(bf16[2,24,3840]{2,1,0:T(8,128)(2,1)} %get-tuple-element.194), channel_id=1, source_target_pairs={{0,2},{1,3},{2,0},{3,1},{4,6},{5,7},{6,4},{7,5},{8,10},{9,11},{10,... | collective-permute-start | bytes 1105928 | tf_op jit(solution)/shard_map/ppermute | solution.py:39
  302.9 22.2 %copy-start.37 = (bf16[128,768]{1,0:T(8,128)(2,1)}, bf16[128,768]{1,0:T(8,128)(2,1)S(1)}, u32[]{:S(2)}) copy-start(bf16[128,768]{1,0:T(8,128)(2,1)S(1)} %collective-permute-done.27.refs_2_) | copy-start | bytes 589828
  302.9 4.2 %collective-permute-start.34 = (f32[12,768]{1,0:T(8,128)S(1)}, f32[12,768]{1,0:T(8,128)S(1)}, u32[]{:S(2)}, u32[]{:S(2)}) collective-permute-start(f32[12,768]{1,0:T(8,128)S(1)} %add.244), channel_id=1, source_target_pairs={{0,16},{8,24},{16,0},{24,8},{1,17},{9,25},{17,1},{25,9},{2,18},{10... | collective-permute-start | bytes 110600 | tf_op jit(solution)/shard_map/ppermute | solution.py:39
  303.6 21.5 %copy-start.38 = (bf16[128,768]{1,0:T(8,128)(2,1)}, bf16[128,768]{1,0:T(8,128)(2,1)S(1)}, u32[]{:S(2)}) copy-start(bf16[128,768]{1,0:T(8,128)(2,1)S(1)} %collective-permute-done.30.refs_6_) | copy-start | bytes 589828
  303.6 9.7 %collective-permute-start.26 = (bf16[128,768]{1,0:T(8,128)(2,1)S(1)}, bf16[128,768]{1,0:T(8,128)(2,1)S(1)}, u32[]{:S(2)}, u32[]{:S(2)}) collective-permute-start(bf16[128,768]{1,0:T(8,128)(2,1)S(1)} %copy-done.76), channel_id=1, source_target_pairs={{0,1},{1,0},{2,3},{3,2},{4,5},{5,4},{6,7},{7,6},{8,9},{9,8},{10,11... | collective-permute-start | bytes 589832 | tf_op jit(solution)/shard_map/ppermute | solution.py:707
  307.1 15.4 %collective-permute-start.28 = (bf16[128,768]{1,0:T(8,128)(2,1)S(1)}, bf16[128,768]{1,0:T(8,128)(2,1)S(1)}, u32[]{:S(2)}, u32[]{:S(2)}) collective-permute-start(bf16[128,768]{1,0:T(8,128)(2,1)S(1)} %copy-done.74), channel_id=1, source_target_pairs={{0,3},{1,2},{2,1},{3,0},{4,7},{5,6},{6,5},{7,4},{8,11},{9,10},{10,... | collective-permute-start | bytes 589832 | tf_op jit(solution)/shard_map/ppermute | solution.py:707
  308.5 20.0 %copy-start.30 = (bf16[4,24,1152]{2,1,0:T(8,128)(2,1)}, bf16[4,24,1152]{2,1,0:T(8,128)(2,1)S(1)}, u32[]{:S(2)}) copy-start(bf16[4,24,1152]{2,1,0:T(8,128)(2,1)S(1)} %collective-permute-done.35.refs_2_) | copy-start | bytes 663556
  308.5 14.0 %collective-permute-start.29 = (bf16[128,768]{1,0:T(8,128)(2,1)S(1)}, bf16[128,768]{1,0:T(8,128)(2,1)S(1)}, u32[]{:S(2)}, u32[]{:S(2)}) collective-permute-start(bf16[128,768]{1,0:T(8,128)(2,1)S(1)} %copy-done.73), channel_id=1, source_target_pairs={{0,5},{1,4},{2,7},{3,6},{4,1},{5,0},{6,3},{7,2},{8,13},{9,12},{10,... | collective-permute-start | bytes 589832 | tf_op jit(solution)/shard_map/ppermute | solution.py:707
  310.5 14.6 %collective-permute-start.31 = (bf16[128,768]{1,0:T(8,128)(2,1)S(1)}, bf16[128,768]{1,0:T(8,128)(2,1)S(1)}, u32[]{:S(2)}, u32[]{:S(2)}) collective-permute-start(bf16[128,768]{1,0:T(8,128)(2,1)S(1)} %copy-done.72), channel_id=1, source_target_pairs={{0,7},{1,6},{2,5},{3,4},{4,3},{5,2},{6,1},{7,0},{8,15},{9,14},{10,... | collective-permute-start | bytes 589832 | tf_op jit(solution)/shard_map/ppermute | solution.py:707
  313.2 19.3 %collective-permute-start.37 = (f32[12,768]{1,0:T(8,128)S(1)}, f32[12,768]{1,0:T(8,128)S(1)}, u32[]{:S(2)}, u32[]{:S(2)}) collective-permute-start(f32[12,768]{1,0:T(8,128)S(1)} %add.245), channel_id=1, source_target_pairs={{0,2},{1,3},{2,0},{3,1},{4,6},{5,7},{6,4},{7,5},{8,10},{9,11},{10,... | collective-permute-start | bytes 110600 | tf_op jit(solution)/shard_map/ppermute | solution.py:39
  330.6 8.8 %collective-permute-start.38 = (bf16[2,24,2304]{2,1,0:T(8,128)(2,1)}, bf16[2,24,2304]{2,1,0:T(8,128)(2,1)S(1)}, u32[]{:S(2)}, u32[]{:S(2)}) collective-permute-start(bf16[2,24,2304]{2,1,0:T(8,128)(2,1)} %get-tuple-element.184), channel_id=1, source_target_pairs={{0,2},{1,3},{2,0},{3,1},{4,6},{5,7},{6,4},{7,5},{8,10},{9,11},{10,... | collective-permute-start | bytes 663560 | tf_op jit(solution)/shard_map/ppermute | solution.py:39
  332.7 14.9 %collective-permute-start.42 = (bf16[1,24,3840]{2,1,0:T(8,128)(2,1)S(1)}, bf16[1,24,3840]{2,1,0:T(8,128)(2,1)S(1)}, u32[]{:S(2)}, u32[]{:S(2)}) collective-permute-start(bf16[1,24,3840]{2,1,0:T(8,128)(2,1)S(1)} %get-tuple-element.232), channel_id=1, source_target_pairs={{0,4},{1,5},{2,6},{3,7},{4,0},{5,1},{6,2},{7,3},{8,12},{9,13},{10,... | collective-permute-start | bytes 552968 | tf_op jit(solution)/shard_map/ppermute | solution.py:39
  339.4 7.0 %collective-permute-start.39 = (f32[12,768]{1,0:T(8,128)S(1)}, f32[12,768]{1,0:T(8,128)S(1)}, u32[]{:S(2)}, u32[]{:S(2)}) collective-permute-start(f32[12,768]{1,0:T(8,128)S(1)} %add.246), channel_id=1, source_target_pairs={{0,4},{1,5},{2,6},{3,7},{4,0},{5,1},{6,2},{7,3},{8,12},{9,13},{10,... | collective-permute-start | bytes 110600 | tf_op jit(solution)/shard_map/ppermute | solution.py:39
  340.7 8.3 %collective-permute-start.40 = (bf16[1,24,2304]{2,1,0:T(8,128)(2,1)S(1)}, bf16[1,24,2304]{2,1,0:T(8,128)(2,1)S(1)}, u32[]{:S(2)}, u32[]{:S(2)}) collective-permute-start(bf16[1,24,2304]{2,1,0:T(8,128)(2,1)S(1)} %add_convert_fusion.4), channel_id=1, source_target_pairs={{0,4},{1,5},{2,6},{3,7},{4,0},{5,1},{6,2},{7,3},{8,12},{9,13},{10,... | collective-permute-start | bytes 331784 | tf_op jit(solution)/shard_map/ppermute | solution.py:39
  (65 other events, 437.7 us)
Sparse Core Ops, SparseCore 0:
  11.3 114.7 all-gather.2
  173.9 117.3 reduce-scatter.1

commit v2 on v1

--- a/solution.py
+++ b/solution.py
@@ -853,11 +853,14 @@
     got = {0: buckets[0]}
     first = [d for d in far + near if not d & 1]
     second = [d for d in far + near if d & 1]
-    waits = [first[:1], first[1:], second[:2], second[2:]]
+    waits = [first, second]
     for d in first:
         got[d] = cross(buckets[d], d)
+    for d, bucket in zip(second, tied([buckets[d] for d in second], got[first[0]])):
+        got[d] = cross(bucket, d)
     s_qkv = s_up = None
     value = value + cube.swap(value, vector_links[0])
+    pending = cube.swap(after(value, *buckets), vector_links[1])
     moved, k = list(buckets), 0
     while s_qkv is None or k + 1 < len(vector_links):
         due = list(moved)
@@ -870,17 +873,14 @@
             s_qkv = qkv.finish(came, [(0, wide, 1)])
             if s_qkv is None:
                 sent_qkv = qkv.start()
-        if k + 1 < len(vector_links):
-            value = after(value, *moved)
-            value = value + cube.swap(value, vector_links[k + 1])
+        if pending is not None:
+            value = value + after(pending, *(qkv.give if s_qkv is None else came))
+            pending = cube.swap(value, vector_links[k + 2]) if k + 2 < len(vector_links) else None
         moved = came
         if s_up is None:
             s_up = up.finish(tied(sent_up, *moved), up_pieces)
             if s_up is None:
                 sent_up = up.start()
-        if k == 0:
-            for d, bucket in zip(second, tied([buckets[d] for d in second], *moved)):
-                got[d] = cross(bucket, d)
         k += 1
     s_rows = value
     grad_tokens = collect(

time: 358 us -> 349 us (0.975)
  starting transfers between devices: 72 us -> 64.7 us
    ppermute x14, waiting for transfers between devices: 47.5 us -> 59.8 us  [cross(): return lax.ppermute(bucket, 'fsdp', [(i, i ^ d) for i in range(peer_count)])]
    reduce_scatter x1, waiting for transfers between devices: 16.3 us -> 5.42 us  [per_device(): sum_down = lax.psum_scatter(d_w_down, AXES, scatter_dimension=0, tiled=True)]
    ppermute x29, starting transfers between devices: 41.1 us -> 34 us  [swap(): return lax.ppermute(value, axis, pairs)]
    ppermute x29, waiting for transfers between devices: 26.3 us -> 22.2 us  [swap(): return lax.ppermute(value, axis, pairs)]
    unnamed x171 -> x153, local copies, waits for them, and re-layouts: 6.57 us -> 7.31 us
  transfers between devices with their start and end apart: 47 -> 47, of which waited for: 18 -> 16; matrix products, arithmetic and copies ran while one was open for 21% -> 22% of each run, Pallas kernels for 24% -> 25%
where the time goes in v2:
time: 349 us; the launch traced here: 348 us
  waiting for transfers between devices  95.2 us (27%)
  Pallas kernels  85.9 us (25%)
  starting transfers between devices  64.7 us (19%)
  matrix products  45.6 us (13%)
  other arithmetic  23.2 us (7%)
  local copies, waits for them, and re-layouts  18.2 us (5%)
  between operations  15.4 us (4%)
    ppermute x14, waiting for transfers between devices, cross(): return lax.ppermute(bucket, 'fsdp', [(i, i ^ d) for i in range(peer_count)])  59.8 us
    ppermute x29, starting transfers between devices, swap(): return lax.ppermute(value, axis, pairs)  34 us
    ppermute x29, waiting for transfers between devices, swap(): return lax.ppermute(value, axis, pairs)  22.2 us
    dot_general x6, matrix products, dot_nn(): return jnp.dot(left, right, preferred_element_type=F32)  21.4 us
    ppermute x14, starting transfers between devices, cross(): return lax.ppermute(bucket, 'fsdp', [(i, i ^ d) for i in range(peer_count)])  18.5 us
    pallas_call x6, Pallas kernels, add(): pl.pallas_call(kernel, out_shape=shapes, in_specs=[pl.BlockSpec(memory_sp...  17.9 us
    dot_general x4, matrix products, dot_nt(): lax.dot_general(left, right, (((1,), (1,)), ((), ())), preferred_element_...  17.2 us
    pallas_call x2, Pallas kernels, weight_grads(): pl.pallas_call(kernel, out_shape=[shape, shape], grid_spec=pltpu.Prefetch...  16.2 us
  transfers between devices with their start and end apart: 47, of which 16 were waited for; matrix products, arithmetic and copies ran while one was open for 22% of the time, Pallas kernels for 25%

profile of v2, /device:TPU:0, one launch (start us, length us, event | category | flops | bytes accessed | tf_op | source)
XLA Modules:
  0.0 348.2 jit_solution(5431726426651609400)
XLA Ops:
  12.0 4.1 %collective-permute-start = (bf16[1,24,2432]{2,1,0:T(8,128)(2,1)S(1)}, bf16[1,24,2432]{2,1,0:T(8,128)(2,1)S(1)}, u32[]{:S(2)}, u32[]{:S(2)}) collective-permute-start(bf16[1,24,2432]{2,1,0:T(8,128)(2,1)S(1)} %pad_maximum_fusion.4), channel_id=1, source_target_pairs={{0,4},{1,5},{2,6},{3,7},{4,0},{5,1},{6,2},{7,3},{8,12},{9,13},{10,... | collective-permute-start | bytes 350216 | tf_op jit(solution)/shard_map/ppermute | solution.py:39
  16.1 2.6 deal_tokens.1
  18.9 1.8 collective-permute-start.3
  21.8 7.8 %collective-permute-start.1 = (bf16[2,24,2432]{2,1,0:T(8,128)(2,1)S(1)}, bf16[2,24,2432]{2,1,0:T(8,128)(2,1)S(1)}, u32[]{:S(2)}, u32[]{:S(2)}) collective-permute-start(bf16[2,24,2432]{2,1,0:T(8,128)(2,1)S(1)} %pad_maximum_fusion.3), channel_id=1, source_target_pairs={{0,2},{1,3},{2,0},{3,1},{4,6},{5,7},{6,4},{7,5},{8,10},{9,11},{10,... | collective-permute-start | bytes 700424 | tf_op jit(solution)/shard_map/ppermute | solution.py:39
  30.3 5.5 %collective-permute-done.2.refs_4_ = bf16[128,768]{1,0:T(8,128)(2,1)S(1)} collective-permute-done((bf16[128,768]{1,0:T(8,128)(2,1)}, bf16[128,768]{1,0:T(8,128)(2,1)S(1)}, u32[]{:S(2)}, u32[]{:S(2)}) %collective-permute-start.2) | collective-permute-done | bytes 196640 | tf_op jit(solution)/shard_map/ppermute | solution.py:707
  35.8 6.7 %collective-permute-done.1 = bf16[2,24,2432]{2,1,0:T(8,128)(2,1)S(1)} collective-permute-done((bf16[2,24,2432]{2,1,0:T(8,128)(2,1)S(1)}, bf16[2,24,2432]{2,1,0:T(8,128)(2,1)S(1)}, u32[]{:S(2)}, u32[]{:S(2)}) %collective-permute-start.1) | collective-permute-done | bytes 233504 | tf_op jit(solution)/shard_map/ppermute | solution.py:39
  42.6 1.6 collective-permute-start.4
  45.0 3.5 %collective-permute-start.6 = (bf16[128,768]{1,0:T(8,128)(2,1)S(1)}, bf16[128,768]{1,0:T(8,128)(2,1)S(1)}, u32[]{:S(2)}, u32[]{:S(2)}) collective-permute-start(bf16[128,768]{1,0:T(8,128)(2,1)S(1)} %copy-done.69), channel_id=1, source_target_pairs={{0,6},{1,7},{2,4},{3,5},{4,2},{5,3},{6,0},{7,1},{8,14},{9,15},{10,... | collective-permute-start | bytes 589832 | tf_op jit(solution)/shard_map/ppermute | solution.py:707
  48.5 1.6 collective-permute-start.5
  51.8 11.5 %collective-permute-done.7.refs_2_ = bf16[128,768]{1,0:T(8,128)(2,1)S(1)} collective-permute-done((bf16[128,768]{1,0:T(8,128)(2,1)S(1)}, bf16[128,768]{1,0:T(8,128)(2,1)S(1)}, u32[]{:S(2)}, u32[]{:S(2)}) %collective-permute-start.7) | collective-permute-done | bytes 196640 | tf_op jit(solution)/shard_map/ppermute | solution.py:707
  63.3 3.2 collective-permute-done.6.refs_6_
  66.5 1.6 collective-permute-start.11
  68.3 1.5 collective-permute-start.10
  70.6 15.4 %collective-permute-done.9.refs_5_ = bf16[128,768]{1,0:T(8,128)(2,1)S(1)} collective-permute-done((bf16[128,768]{1,0:T(8,128)(2,1)S(1)}, bf16[128,768]{1,0:T(8,128)(2,1)S(1)}, u32[]{:S(2)}, u32[]{:S(2)}) %collective-permute-start.9) | collective-permute-done | bytes 196640 | tf_op jit(solution)/shard_map/ppermute | solution.py:707
  87.2 3.0 take_tokens.1
  92.2 2.7 deal_cotangent.1
  96.8 5.4 %interleave.1 = (bf16[2,2,8,1,24,2304]{5,4,3,2,1,0:T(8,128)(2,1)}, bf16[2,2,8,1,24,128]{5,4,3,2,1,0:T(8,128)(2,1)}) custom-call(s32[2]{0:T(128)} %pad_add_fusion.scalar_ref.me_ref, bf16[8,24,1280]{2,1,0:T(8,128)(2,1)} %copy-done.19, bf16[8,24,1280]{2,1,0:T(8,128)(2,1)} %copy-done.24, bf16[8,24,1152]{2,1,0:T(8,128)(2,1)} %copy-done.20, ...), custom_call_target="tpu_custom_call" | custom-call | tf_op jit(solution)/shard_map/interleave/pallas_call | solution.py:79
  105.5 5.5 %fusion.8.q_ref.k_ref.v_ref = bf16[512,2304]{1,0:T(8,128)(2,1)} fusion(bf16[512,768]{1,0:T(8,128)(2,1)S(1)} %fusion.15.refs_0_, bf16[768,2304]{1,0:T(8,128)(2,1)} %bitcast.147, f32[2304]{0:T(1024)S(1)} %pad_maximum_fusion.5), kind=kOutput, calls=%fused_computation.17 | convolution fusion | flops 1814298624 | bytes 6693888 | tf_op jit(solution)/shard_map/dot_general | solution.py:495
  111.1 6.3 %all-to-all-start.1 = ((bf16[8,128,768]{2,1,0:T(8,128)(2,1)}), bf16[8,128,768]{2,1,0:T(8,128)(2,1)}, u32[]{:S(2)}, u32[]{:S(2)}) async-start(bf16[8,128,768]{2,1,0:T(8,128)(2,1)} %deal_cotangent.1), calls=%async_computation.1 | async-start | bytes 3145728 | tf_op jit(solution)/shard_map/all_to_all | solution.py:778
  117.4 10.4 %attend_forward.1 = (bf16[512,768]{1,0:T(8,128)(2,1)}, f32[6,2,512]{2,1,0:T(2,128)}) custom-call(bf16[512,2304]{1,0:T(8,128)(2,1)} %fusion.8.q_ref.k_ref.v_ref, bf16[512,2304]{1,0:T(8,128)(2,1)} %fusion.8.q_ref.k_ref.v_ref, bf16[512,2304]{1,0:T(8,128)(2,1)} %fusion.8.q_ref.k_ref.v_ref, s32[1,512]{1,0:T(1,128)} %bitcast.139, s32[512,1]{1,0:T(8,128)} %copy.43.ks_ref), custom_call_target="tpu_custom_call" | custom-call | tf_op jit(solution)/shard_map/attend_forward/pallas_call | solution.py:529
  128.5 2.6 slice.219
  131.2 4.8 %fusion.59 = (bf16[32,24,768]{2,1,0:T(8,128)(2,1)S(1)}, bf16[32,24,768]{2,1,0:T(8,128)(2,1)S(1)}, bf16[32,24,768]{2,1,0:T(8,128)(2,1)S(1)}, bf16[32,24,768]{2,1,0:T(8,128)(2,1)S(1)}, bf16[32,24,768]{2,1,0:T(8,128)(2,1)S(1)}) fusion(bf16[32,216,768]{2,1,0:T(8,128)(2,1)} %bitcast.119), kind=kLoop, calls=%fused_computation.185 | loop fusion | bytes 11796480 | tf_op jit(solution)/shard_map/slice | solution.py:699
  138.5 9.8 %fusion.7 = (f32[512,3072]{1,0:T(8,128)}, bf16[512,3072]{1,0:T(8,128)(2,1)S(1)}) fusion(f32[3072]{0:T(1024)S(1)} %fusion.27, bf16[512,768]{1,0:T(8,128)(2,1)S(1)} %add_convert_fusion.1.refs_0_, bf16[768,768]{1,0:T(8,128)(2,1)S(1)} %bitcast.127, bf16[768,768]{1,0:T(8,128)(2,1)S(1)} %bitcast.129, bf16[768,768]{1,0:T(8,128)(2,1)S(1)} %bitcast.131, ...), kind=kOutput, calls=%fused_computation.9 | convolution fusion | flops 2464677888 | bytes 14954496 | tf_op jit(solution)/shard_map/dot_general | solution.py:495
  148.3 3.5 %add_convert_fusion = bf16[512,768]{1,0:T(8,128)(2,1)} fusion(f32[512,768]{1,0:T(8,128)S(1)} %get-tuple-element.252, bf16[512,3072]{1,0:T(8,128)(2,1)S(1)} %get-tuple-element.131, bf16[3072,768]{1,0:T(8,128)(2,1)S(1)} %bitcast.120, f32[768]{0:T(1024)S(1)} %get-tuple-element.209), kind=kOutput, calls=%fused_computation.48 | convolution fusion | flops 2417098752 | bytes 10226688 | tf_op jit(solution)/shard_map/dot_general | solution.py:495
  151.8 2.6 return_mixed.1
  154.5 2.4 all-to-all-done.1.src
  156.9 5.9 %all-to-all-start = ((bf16[8,128,768]{2,1,0:T(8,128)(2,1)}), bf16[8,128,768]{2,1,0:T(8,128)(2,1)}, u32[]{:S(2)}, u32[]{:S(2)}) async-start(bf16[8,128,768]{2,1,0:T(8,128)(2,1)} %return_mixed.1), calls=%async_computation | async-start | bytes 3145728 | tf_op jit(solution)/shard_map/all_to_all | solution.py:790
  162.8 2.6 take_cotangent.1
  166.8 7.0 %convolution_convert_fusion = bf16[3072,768]{1,0:T(8,128)(2,1)} fusion(bf16[512,3072]{1,0:T(8,128)(2,1)} %copy-done.72, bf16[512,768]{1,0:T(8,128)(2,1)S(1)} %fusion.26), kind=kOutput, calls=%fused_computation.14 | convolution fusion | flops 2418278400 | bytes 8650752 | tf_op jit(solution)/shard_map/dot_general | solution.py:499
  173.9 6.6 %convert_reduce_fusion = (f32[3072]{0:T(1024)S(1)}, bf16[512,3072]{1,0:T(8,128)(2,1)S(1)}) fusion(f32[512,3072]{1,0:T(8,128)} %get-tuple-element.136, bf16[512,768]{1,0:T(8,128)(2,1)S(1)} %fusion.26, bf16[3072,768]{1,0:T(8,128)(2,1)} %bitcast.121), kind=kOutput, calls=%fused_computation.10 | convolution fusion | flops 2422207488 | bytes 14954496 | tf_op jit(solution)/shard_map/dot_general | solution.py:503
  180.5 3.0 multiply_reduce_fusion
  183.6 2.1 convert_reduce_fusion.3
  185.7 9.4 %weight_grads.2 = (bf16[16,24,3840]{2,1,0:T(8,128)(2,1)}, bf16[16,24,3840]{2,1,0:T(8,128)(2,1)}) custom-call(s32[2]{0:T(128)} %pad_add_fusion.scalar_ref.me_ref, bf16[512,768]{1,0:T(8,128)(2,1)} %copy-done.7, bf16[512,3072]{1,0:T(8,128)(2,1)} %copy-done.5, bf16[512,768]{1,0:T(8,128)(2,1)} %get-tuple-element.130.refs_2_, ...), custom_call_target="tpu_custom_call" | custom-call | tf_op jit(solution)/shard_map/weight_grads/pallas_call | solution.py:383
  195.1 5.2 %all-to-all-done.src = bf16[8,128,768]{2,1,0:T(8,128)(2,1)} async-done(((bf16[8,128,768]{2,1,0:T(8,128)(2,1)}), bf16[8,128,768]{2,1,0:T(8,128)(2,1)}, u32[]{:S(2)}, u32[]{:S(2)}) %all-to-all-start) | async-done | bytes 1572896 | tf_op jit(solution)/shard_map/all_to_all | solution.py:790
  200.3 1.7 convolution_convert_fusion.1.d_ref
  202.0 4.7 %add_step.6 = (bf16[8,24,1920]{2,1,0:T(8,128)(2,1)}, bf16[8,24,1920]{2,1,0:T(8,128)(2,1)}, bf16[8,24,1920]{2,1,0:T(8,128)(2,1)}, bf16[8,24,1920]{2,1,0:T(8,128)(2,1)}) custom-call(bf16[16,24,3840]{2,1,0:T(8,128)(2,1)} %get-tuple-element.139.refs_0_, bf16[16,24,3840]{2,1,0:T(8,128)(2,1)} %collective-permute-done.17.refs_1_), custom_call_target="tpu_custom_call" | custom-call | tf_op jit(solution)/shard_map/add_step/pallas_call | solution.py:484
  206.7 1.5 collective-permute-start.18
  209.0 14.6 %attend_backward.1.refs_1_ = bf16[512,2304]{1,0:T(8,128)(2,1)} custom-call(bf16[512,2304]{1,0:T(8,128)(2,1)} %fusion.8.q_ref.k_ref.v_ref, bf16[512,2304]{1,0:T(8,128)(2,1)} %fusion.8.q_ref.k_ref.v_ref, bf16[512,2304]{1,0:T(8,128)(2,1)} %fusion.8.q_ref.k_ref.v_ref, bf16[512,768]{1,0:T(8,128)(2,1)} %convolution_convert_fusion.1.d_ref, ...), custom_call_target="tpu_custom_call" | custom-call | tf_op jit(solution)/shard_map/attend_backward/pallas_call | solution.py:583
  223.7 1.6 collective-permute-done.18.refs_2_
  225.3 2.2 collective-permute-done.19.refs_3_
  228.3 3.0 add_step.7
  231.3 6.8 %weight_grads.3 = (bf16[16,24,2304]{2,1,0:T(8,128)(2,1)}, bf16[16,24,2304]{2,1,0:T(8,128)(2,1)}) custom-call(s32[2]{0:T(128)} %pad_add_fusion.scalar_ref.me_ref, bf16[512,768]{1,0:T(8,128)(2,1)} %copy-done.6, bf16[512,2304]{1,0:T(8,128)(2,1)} %attend_backward.1.refs_1_), custom_call_target="tpu_custom_call" | custom-call | tf_op jit(solution)/shard_map/weight_grads/pallas_call | solution.py:383
  239.4 2.2 collective-permute-start.21
  241.6 6.0 %fusion.21 = (f32[768]{0:T(1024)}, f32[512]{0:T(512)S(1)}, f32[512]{0:T(512)S(1)}, f32[768]{0:T(1024)}, f32[512,768]{1,0:T(8,128)}) fusion(f32[512]{0:T(512)S(1)} %rsqrt_bitcast_fusion, f32[512]{0:T(512)S(1)} %get-tuple-element.248, bf16[4,128,768]{2,1,0:T(8,128)(2,1)S(1)} %copy-done, f32[768]{0:T(1024)S(1)} %get-tuple-element.216, ...), kind=kOutput, calls=%fused_computation.35 | convolution fusion | flops 1815868928 | bytes 8274944 | tf_op jit(solution)/shard_map/dot_general | solution.py:503
  248.7 3.4 add_step.8
  252.1 2.0 collective-permute-start.32
  254.4 3.3 fusion.20
  257.8 2.6 return_gradient.1
  261.8 2.2 collective-permute-start.23
  264.9 16.1 %collective-permute-done.23.refs_4_ = bf16[128,768]{1,0:T(8,128)(2,1)} collective-permute-done((bf16[128,768]{1,0:T(8,128)(2,1)}, bf16[128,768]{1,0:T(8,128)(2,1)}, u32[]{:S(2)}, u32[]{:S(2)}) %collective-permute-start.23) | collective-permute-done | bytes 196640 | tf_op jit(solution)/shard_map/ppermute | solution.py:707
  281.6 5.4 %reduce-scatter.2.cloned.1.call-done = bf16[96,768]{1,0:T(8,128)(2,1)} async-done(((bf16[3072,768]{1,0:T(8,128)(2,1)}), bf16[96,768]{1,0:T(8,128)(2,1)}) %reduce-scatter.2.cloned.1.call-update) | async-done | bytes 147472 | tf_op jit(solution)/shard_map/reduce_scatter | solution.py:798
  287.0 2.4 add_step.11
  291.9 3.0 collective-permute-start.27
  294.9 2.4 add_step.9
  298.9 3.1 collective-permute-start.29
  302.0 8.1 %collective-permute-done.27.refs_5_ = bf16[128,768]{1,0:T(8,128)(2,1)S(1)} collective-permute-done((bf16[128,768]{1,0:T(8,128)(2,1)}, bf16[128,768]{1,0:T(8,128)(2,1)S(1)}, u32[]{:S(2)}, u32[]{:S(2)}) %collective-permute-start.27) | collective-permute-done | bytes 196640 | tf_op jit(solution)/shard_map/ppermute | solution.py:707
  310.1 1.4 collective-permute-start.34
  311.5 2.6 take_mixed.1
  314.9 2.6 take_gradient.1
  319.1 2.1 add_step.10
  321.2 2.1 collective-permute-start.37
  323.6 6.4 %collective-permute-done.38 = bf16[2,24,2304]{2,1,0:T(8,128)(2,1)S(1)} collective-permute-done((bf16[2,24,2304]{2,1,0:T(8,128)(2,1)}, bf16[2,24,2304]{2,1,0:T(8,128)(2,1)S(1)}, u32[]{:S(2)}, u32[]{:S(2)}) %collective-permute-start.38) | collective-permute-done | bytes 221216 | tf_op jit(solution)/shard_map/ppermute | solution.py:39
  331.1 3.0 collective-permute-start.39
  334.0 3.9 %collective-permute-done.42 = bf16[1,24,3840]{2,1,0:T(8,128)(2,1)S(1)} collective-permute-done((bf16[1,24,3840]{2,1,0:T(8,128)(2,1)S(1)}, bf16[1,24,3840]{2,1,0:T(8,128)(2,1)S(1)}, u32[]{:S(2)}, u32[]{:S(2)}) %collective-permute-start.42) | collective-permute-done | bytes 184352 | tf_op jit(solution)/shard_map/ppermute | solution.py:39
  (306 shorter events, 41.1 us)
Async XLA Ops:
  7.3 121.2 %all-gather.3.cloned.1.call-start = ((), (), s32[]{:S(2)}) async-start(), calls=%async_computation.4 | async-start | bytes 10948608 | tf_op jit(solution)/shard_map/all_gather | solution.py:696
  12.0 9.8 %collective-permute-start = (bf16[1,24,2432]{2,1,0:T(8,128)(2,1)S(1)}, bf16[1,24,2432]{2,1,0:T(8,128)(2,1)S(1)}, u32[]{:S(2)}, u32[]{:S(2)}) collective-permute-start(bf16[1,24,2432]{2,1,0:T(8,128)(2,1)S(1)} %pad_maximum_fusion.4), channel_id=1, source_target_pairs={{0,4},{1,5},{2,6},{3,7},{4,0},{5,1},{6,2},{7,3},{8,12},{9,13},{10,... | collective-permute-start | bytes 350216 | tf_op jit(solution)/shard_map/ppermute | solution.py:39
  18.8 26.3 %copy-start.70 = (bf16[128,768]{1,0:T(8,128)(2,1)S(1)}, bf16[128,768]{1,0:T(8,128)(2,1)}, u32[]{:S(2)}) copy-start(bf16[128,768]{1,0:T(8,128)(2,1)} %get-tuple-element.114) | copy-start | bytes 589828
  18.8 26.3 %copy-start.69 = (bf16[128,768]{1,0:T(8,128)(2,1)S(1)}, bf16[128,768]{1,0:T(8,128)(2,1)}, u32[]{:S(2)}) copy-start(bf16[128,768]{1,0:T(8,128)(2,1)} %get-tuple-element.112) | copy-start | bytes 589828
  18.8 32.6 %copy-start.68 = (bf16[128,768]{1,0:T(8,128)(2,1)S(1)}, bf16[128,768]{1,0:T(8,128)(2,1)}, u32[]{:S(2)}) copy-start(bf16[128,768]{1,0:T(8,128)(2,1)} %get-tuple-element.121) | copy-start | bytes 589828
  18.8 44.5 %copy-start.67 = (bf16[128,768]{1,0:T(8,128)(2,1)S(1)}, bf16[128,768]{1,0:T(8,128)(2,1)}, u32[]{:S(2)}) copy-start(bf16[128,768]{1,0:T(8,128)(2,1)} %get-tuple-element.119) | copy-start | bytes 589828
  18.8 17.0 %collective-permute-start.2 = (bf16[128,768]{1,0:T(8,128)(2,1)}, bf16[128,768]{1,0:T(8,128)(2,1)S(1)}, u32[]{:S(2)}, u32[]{:S(2)}) collective-permute-start(bf16[128,768]{1,0:T(8,128)(2,1)} %get-tuple-element.107), channel_id=1, source_target_pairs={{0,4},{1,5},{2,6},{3,7},{4,0},{5,1},{6,2},{7,3},{8,12},{9,13},{10,... | collective-permute-start | bytes 589832 | tf_op jit(solution)/shard_map/ppermute | solution.py:707
  18.9 16.9 %collective-permute-start.3 = (bf16[128,768]{1,0:T(8,128)(2,1)}, bf16[128,768]{1,0:T(8,128)(2,1)S(1)}, u32[]{:S(2)}, u32[]{:S(2)}) collective-permute-start(bf16[128,768]{1,0:T(8,128)(2,1)} %get-tuple-element.108), channel_id=1, source_target_pairs={{0,1},{1,0},{2,3},{3,2},{4,5},{5,4},{6,7},{7,6},{8,9},{9,8},{10,11... | collective-permute-start | bytes 589832 | tf_op jit(solution)/shard_map/ppermute | solution.py:707
  21.1 45.4 %copy-start.45 = (s32[512]{0:T(512)}, s32[512]{0:T(512)S(1)}, u32[]{:S(2)}) copy-start(s32[512]{0:T(512)S(1)} %get-tuple-element.219) | copy-start | bytes 6148
  21.8 20.7 %collective-permute-start.1 = (bf16[2,24,2432]{2,1,0:T(8,128)(2,1)S(1)}, bf16[2,24,2432]{2,1,0:T(8,128)(2,1)S(1)}, u32[]{:S(2)}, u32[]{:S(2)}) collective-permute-start(bf16[2,24,2432]{2,1,0:T(8,128)(2,1)S(1)} %pad_maximum_fusion.3), channel_id=1, source_target_pairs={{0,2},{1,3},{2,0},{3,1},{4,6},{5,7},{6,4},{7,5},{8,10},{9,11},{10,... | collective-permute-start | bytes 700424 | tf_op jit(solution)/shard_map/ppermute | solution.py:39
  35.8 30.7 %copy-start.34 = (bf16[128,768]{1,0:T(8,128)(2,1)}, bf16[128,768]{1,0:T(8,128)(2,1)S(1)}, u32[]{:S(2)}) copy-start(bf16[128,768]{1,0:T(8,128)(2,1)S(1)} %collective-permute-done.2.refs_4_) | copy-start | bytes 589828
  35.8 30.7 %copy-start.35 = (bf16[128,768]{1,0:T(8,128)(2,1)}, bf16[128,768]{1,0:T(8,128)(2,1)S(1)}, u32[]{:S(2)}) copy-start(bf16[128,768]{1,0:T(8,128)(2,1)S(1)} %collective-permute-done.3.refs_1_) | copy-start | bytes 589828
  42.6 27.3 %copy-start.56 = (s32[8]{0:T(128)S(1)}, s32[8]{0:T(128)}, u32[]{:S(2)}) copy-start(s32[8]{0:T(128)} %constant.113.clone) | copy-start | bytes 100
  42.6 23.8 %collective-permute-start.4 = (bf16[4,24,1280]{2,1,0:T(8,128)(2,1)S(1)}, bf16[4,24,1280]{2,1,0:T(8,128)(2,1)S(1)}, u32[]{:S(2)}, u32[]{:S(2)}) collective-permute-start(bf16[4,24,1280]{2,1,0:T(8,128)(2,1)S(1)} %slice.205), channel_id=1, source_target_pairs={{0,16},{8,24},{16,0},{24,8},{1,17},{9,25},{17,1},{25,9},{2,18},{10... | collective-permute-start | bytes 737288 | tf_op jit(solution)/shard_map/ppermute | solution.py:39
  45.0 18.2 %collective-permute-start.7 = (bf16[128,768]{1,0:T(8,128)(2,1)S(1)}, bf16[128,768]{1,0:T(8,128)(2,1)S(1)}, u32[]{:S(2)}, u32[]{:S(2)}) collective-permute-start(bf16[128,768]{1,0:T(8,128)(2,1)S(1)} %copy-done.70), channel_id=1, source_target_pairs={{0,2},{1,3},{2,0},{3,1},{4,6},{5,7},{6,4},{7,5},{8,10},{9,11},{10,... | collective-permute-start | bytes 589832 | tf_op jit(solution)/shard_map/ppermute | solution.py:707
  45.0 21.4 %collective-permute-start.6 = (bf16[128,768]{1,0:T(8,128)(2,1)S(1)}, bf16[128,768]{1,0:T(8,128)(2,1)S(1)}, u32[]{:S(2)}, u32[]{:S(2)}) collective-permute-start(bf16[128,768]{1,0:T(8,128)(2,1)S(1)} %copy-done.69), channel_id=1, source_target_pairs={{0,6},{1,7},{2,4},{3,5},{4,2},{5,3},{6,0},{7,1},{8,14},{9,15},{10,... | collective-permute-start | bytes 589832 | tf_op jit(solution)/shard_map/ppermute | solution.py:707
  48.5 17.9 %collective-permute-start.5 = (bf16[4,24,1152]{2,1,0:T(8,128)(2,1)S(1)}, bf16[4,24,1152]{2,1,0:T(8,128)(2,1)S(1)}, u32[]{:S(2)}, u32[]{:S(2)}) collective-permute-start(bf16[4,24,1152]{2,1,0:T(8,128)(2,1)S(1)} %slice.206), channel_id=1, source_target_pairs={{0,1},{1,0},{2,3},{3,2},{4,5},{5,4},{6,7},{7,6},{8,9},{9,8},{10,11... | collective-permute-start | bytes 663560 | tf_op jit(solution)/shard_map/ppermute | solution.py:39
  51.3 34.6 %collective-permute-start.9 = (bf16[128,768]{1,0:T(8,128)(2,1)S(1)}, bf16[128,768]{1,0:T(8,128)(2,1)S(1)}, u32[]{:S(2)}, u32[]{:S(2)}) collective-permute-start(bf16[128,768]{1,0:T(8,128)(2,1)S(1)} %copy-done.68), channel_id=1, source_target_pairs={{0,5},{1,4},{2,7},{3,6},{4,1},{5,0},{6,3},{7,2},{8,13},{9,12},{10,... | collective-permute-start | bytes 589832 | tf_op jit(solution)/shard_map/ppermute | solution.py:707
  63.3 23.2 %copy-start.37 = (bf16[128,768]{1,0:T(8,128)(2,1)}, bf16[128,768]{1,0:T(8,128)(2,1)S(1)}, u32[]{:S(2)}) copy-start(bf16[128,768]{1,0:T(8,128)(2,1)S(1)} %collective-permute-done.7.refs_2_) | copy-start | bytes 589828
  63.3 22.7 %collective-permute-start.8 = (bf16[128,768]{1,0:T(8,128)(2,1)S(1)}, bf16[128,768]{1,0:T(8,128)(2,1)S(1)}, u32[]{:S(2)}, u32[]{:S(2)}) collective-permute-start(bf16[128,768]{1,0:T(8,128)(2,1)S(1)} %copy-done.67), channel_id=1, source_target_pairs={{0,3},{1,2},{2,1},{3,0},{4,7},{5,6},{6,5},{7,4},{8,11},{9,10},{10,... | collective-permute-start | bytes 589832 | tf_op jit(solution)/shard_map/ppermute | solution.py:707
  66.4 20.1 %copy-start.38 = (bf16[128,768]{1,0:T(8,128)(2,1)}, bf16[128,768]{1,0:T(8,128)(2,1)S(1)}, u32[]{:S(2)}) copy-start(bf16[128,768]{1,0:T(8,128)(2,1)S(1)} %collective-permute-done.6.refs_6_) | copy-start | bytes 589828
  66.5 23.6 %copy-start.19 = (bf16[8,24,1280]{2,1,0:T(8,128)(2,1)}, bf16[8,24,1280]{2,1,0:T(8,128)(2,1)S(1)}, u32[]{:S(2)}) copy-start(bf16[8,24,1280]{2,1,0:T(8,128)(2,1)S(1)} %constant_dynamic-update-slice_fusion.4.refs_0_) | copy-start | bytes 1474564
  66.5 25.2 %collective-permute-start.11 = (bf16[8,24,1280]{2,1,0:T(8,128)(2,1)S(1)}, bf16[8,24,1280]{2,1,0:T(8,128)(2,1)S(1)}, u32[]{:S(2)}, u32[]{:S(2)}) collective-permute-start(bf16[8,24,1280]{2,1,0:T(8,128)(2,1)S(1)} %constant_dynamic-update-slice_fusion.4.refs_0_), channel_id=1, source_target_pairs={{0,1},{1,0},{2,3},{3,2},{4,5},{5,4},{6,7},{7,6},{8,9},{9,8},{10,11... | collective-permute-start | bytes 1474568 | tf_op jit(solution)/shard_map/ppermute | solution.py:39
  68.2 23.4 %copy-start.20 = (bf16[8,24,1152]{2,1,0:T(8,128)(2,1)}, bf16[8,24,1152]{2,1,0:T(8,128)(2,1)S(1)}, u32[]{:S(2)}) copy-start(bf16[8,24,1152]{2,1,0:T(8,128)(2,1)S(1)} %constant_dynamic-update-slice_fusion.2.refs_2_) | copy-start | bytes 1327108
  68.2 23.3 %collective-permute-start.12 = (bf16[8,24,1152]{2,1,0:T(8,128)(2,1)S(1)}, bf16[8,24,1152]{2,1,0:T(8,128)(2,1)}, u32[]{:S(2)}, u32[]{:S(2)}) collective-permute-start(bf16[8,24,1152]{2,1,0:T(8,128)(2,1)S(1)} %constant_dynamic-update-slice_fusion.2.refs_2_), channel_id=1, source_target_pairs={{0,16},{8,24},{16,0},{24,8},{1,17},{9,25},{17,1},{25,9},{2,18},{10... | collective-permute-start | bytes 1327112 | tf_op jit(solution)/shard_map/ppermute | solution.py:39
  68.3 18.2 %collective-permute-start.10 = (bf16[128,768]{1,0:T(8,128)(2,1)}, bf16[128,768]{1,0:T(8,128)(2,1)S(1)}, u32[]{:S(2)}, u32[]{:S(2)}) collective-permute-start(bf16[128,768]{1,0:T(8,128)(2,1)} %get-tuple-element.123), channel_id=1, source_target_pairs={{0,7},{1,6},{2,5},{3,4},{4,3},{5,2},{6,1},{7,0},{8,15},{9,14},{10,... | collective-permute-start | bytes 589832 | tf_op jit(solution)/shard_map/ppermute | solution.py:707
  86.0 9.3 %collective-permute-start.15 = (bf16[8,24,1152]{2,1,0:T(8,128)(2,1)S(1)}, bf16[8,24,1152]{2,1,0:T(8,128)(2,1)}, u32[]{:S(2)}, u32[]{:S(2)}) collective-permute-start(bf16[8,24,1152]{2,1,0:T(8,128)(2,1)S(1)} %constant_dynamic-update-slice_fusion.2.refs_2_), channel_id=1, source_target_pairs={{0,8},{8,0},{16,24},{24,16},{1,9},{9,1},{17,25},{25,17},{2,10},{10... | collective-permute-start | bytes 1327112 | tf_op jit(solution)/shard_map/ppermute | solution.py:39
  86.0 9.3 %collective-permute-start.13 = (bf16[8,24,1280]{2,1,0:T(8,128)(2,1)S(1)}, bf16[8,24,1280]{2,1,0:T(8,128)(2,1)S(1)}, u32[]{:S(2)}, u32[]{:S(2)}) collective-permute-start(bf16[8,24,1280]{2,1,0:T(8,128)(2,1)S(1)} %constant_dynamic-update-slice_fusion.4.refs_0_), channel_id=1, source_target_pairs={{0,8},{8,0},{16,24},{24,16},{1,9},{9,1},{17,25},{25,17},{2,10},{10... | collective-permute-start | bytes 1474568 | tf_op jit(solution)/shard_map/ppermute | solution.py:39
  91.6 3.7 %collective-permute-start.16 = (bf16[8,24,1152]{2,1,0:T(8,128)(2,1)}, bf16[8,24,1152]{2,1,0:T(8,128)(2,1)}, u32[]{:S(2)}, u32[]{:S(2)}) collective-permute-start(bf16[8,24,1152]{2,1,0:T(8,128)(2,1)} %collective-permute-done.12.refs_3_), channel_id=1, source_target_pairs={{0,8},{8,0},{16,24},{24,16},{1,9},{9,1},{17,25},{25,17},{2,10},{10... | collective-permute-start | bytes 1327112 | tf_op jit(solution)/shard_map/ppermute | solution.py:39
  91.7 3.6 %collective-permute-start.14 = (bf16[8,24,1280]{2,1,0:T(8,128)(2,1)S(1)}, bf16[8,24,1280]{2,1,0:T(8,128)(2,1)S(1)}, u32[]{:S(2)}, u32[]{:S(2)}) collective-permute-start(bf16[8,24,1280]{2,1,0:T(8,128)(2,1)S(1)} %collective-permute-done.11.refs_1_), channel_id=1, source_target_pairs={{0,8},{8,0},{16,24},{24,16},{1,9},{9,1},{17,25},{25,17},{2,10},{10... | collective-permute-start | bytes 1474568 | tf_op jit(solution)/shard_map/ppermute | solution.py:39
  111.1 45.8 %all-to-all-start.1 = ((bf16[8,128,768]{2,1,0:T(8,128)(2,1)}), bf16[8,128,768]{2,1,0:T(8,128)(2,1)}, u32[]{:S(2)}, u32[]{:S(2)}) async-start(bf16[8,128,768]{2,1,0:T(8,128)(2,1)} %deal_cotangent.1), calls=%async_computation.1 | async-start | bytes 3145728 | tf_op jit(solution)/shard_map/all_to_all | solution.py:778
  131.1 17.2 %copy-start.3 = (bf16[32,96,768]{2,1,0:T(8,128)(2,1)}, bf16[32,96,768]{2,1,0:T(8,128)(2,1)S(1)}, u32[]{:S(2)}) copy-start(bf16[32,96,768]{2,1,0:T(8,128)(2,1)S(1)} %slice.219) | copy-start | bytes 14155780
  156.9 43.4 %all-to-all-start = ((bf16[8,128,768]{2,1,0:T(8,128)(2,1)}), bf16[8,128,768]{2,1,0:T(8,128)(2,1)}, u32[]{:S(2)}, u32[]{:S(2)}) async-start(bf16[8,128,768]{2,1,0:T(8,128)(2,1)} %return_mixed.1), calls=%async_computation | async-start | bytes 3145728 | tf_op jit(solution)/shard_map/all_to_all | solution.py:790
  162.8 124.3 %reduce-scatter.2.cloned.1.call-start = ((), (), s32[]{:S(2)}) async-start(), calls=%async_computation.3 | async-start | bytes 4866048 | tf_op jit(solution)/shard_map/reduce_scatter | solution.py:798
  195.1 6.9 %collective-permute-start.17 = (bf16[16,24,3840]{2,1,0:T(8,128)(2,1)}, bf16[16,24,3840]{2,1,0:T(8,128)(2,1)}, u32[]{:S(2)}, u32[]{:S(2)}) collective-permute-start(bf16[16,24,3840]{2,1,0:T(8,128)(2,1)} %get-tuple-element.137), channel_id=1, source_target_pairs={{0,8},{8,0},{16,24},{24,16},{1,9},{9,1},{17,25},{25,17},{2,10},{10... | collective-permute-start | bytes 8847368 | tf_op jit(solution)/shard_map/ppermute | solution.py:39
  206.7 18.6 %collective-permute-start.18 = (bf16[8,24,1920]{2,1,0:T(8,128)(2,1)}, bf16[8,24,1920]{2,1,0:T(8,128)(2,1)S(1)}, u32[]{:S(2)}, u32[]{:S(2)}) collective-permute-start(bf16[8,24,1920]{2,1,0:T(8,128)(2,1)} %get-tuple-element.141), channel_id=1, source_target_pairs={{0,1},{1,0},{2,3},{3,2},{4,5},{5,4},{6,7},{7,6},{8,9},{9,8},{10,11... | collective-permute-start | bytes 2211848 | tf_op jit(solution)/shard_map/ppermute | solution.py:39
  208.1 19.3 %collective-permute-start.19 = (bf16[8,24,1920]{2,1,0:T(8,128)(2,1)}, bf16[8,24,1920]{2,1,0:T(8,128)(2,1)S(1)}, u32[]{:S(2)}, u32[]{:S(2)}) collective-permute-start(bf16[8,24,1920]{2,1,0:T(8,128)(2,1)} %get-tuple-element.142), channel_id=1, source_target_pairs={{0,16},{8,24},{16,0},{24,8},{1,17},{9,25},{17,1},{25,9},{2,18},{10... | collective-permute-start | bytes 2211848 | tf_op jit(solution)/shard_map/ppermute | solution.py:39
  238.1 10.6 %collective-permute-start.20 = (bf16[16,24,2304]{2,1,0:T(8,128)(2,1)}, bf16[16,24,2304]{2,1,0:T(8,128)(2,1)}, u32[]{:S(2)}, u32[]{:S(2)}) collective-permute-start(bf16[16,24,2304]{2,1,0:T(8,128)(2,1)} %get-tuple-element.152), channel_id=1, source_target_pairs={{0,8},{8,0},{16,24},{24,16},{1,9},{9,1},{17,25},{25,17},{2,10},{10... | collective-permute-start | bytes 5308424 | tf_op jit(solution)/shard_map/ppermute | solution.py:39
  239.4 18.3 %collective-permute-start.21 = (bf16[4,24,1920]{2,1,0:T(8,128)(2,1)}, bf16[4,24,1920]{2,1,0:T(8,128)(2,1)S(1)}, u32[]{:S(2)}, u32[]{:S(2)}) collective-permute-start(bf16[4,24,1920]{2,1,0:T(8,128)(2,1)} %get-tuple-element.149), channel_id=1, source_target_pairs={{0,16},{8,24},{16,0},{24,8},{1,17},{9,25},{17,1},{25,9},{2,18},{10... | collective-permute-start | bytes 1105928 | tf_op jit(solution)/shard_map/ppermute | solution.py:39
  241.6 16.2 %collective-permute-start.22 = (bf16[4,24,1920]{2,1,0:T(8,128)(2,1)}, bf16[4,24,1920]{2,1,0:T(8,128)(2,1)}, u32[]{:S(2)}, u32[]{:S(2)}) collective-permute-start(bf16[4,24,1920]{2,1,0:T(8,128)(2,1)} %get-tuple-element.150), channel_id=1, source_target_pairs={{0,1},{1,0},{2,3},{3,2},{4,5},{5,4},{6,7},{7,6},{8,9},{9,8},{10,11... | collective-permute-start | bytes 1105928 | tf_op jit(solution)/shard_map/ppermute | solution.py:39
  252.1 29.6 %collective-permute-start.32 = (bf16[8,24,1152]{2,1,0:T(8,128)(2,1)}, bf16[8,24,1152]{2,1,0:T(8,128)(2,1)}, u32[]{:S(2)}, u32[]{:S(2)}) collective-permute-start(bf16[8,24,1152]{2,1,0:T(8,128)(2,1)} %get-tuple-element.156), channel_id=1, source_target_pairs={{0,1},{1,0},{2,3},{3,2},{4,5},{5,4},{6,7},{7,6},{8,9},{9,8},{10,11... | collective-permute-start | bytes 1327112 | tf_op jit(solution)/shard_map/ppermute | solution.py:39
  254.1 27.5 %collective-permute-start.33 = (bf16[8,24,1152]{2,1,0:T(8,128)(2,1)}, bf16[8,24,1152]{2,1,0:T(8,128)(2,1)}, u32[]{:S(2)}, u32[]{:S(2)}) collective-permute-start(bf16[8,24,1152]{2,1,0:T(8,128)(2,1)} %get-tuple-element.157), channel_id=1, source_target_pairs={{0,16},{8,24},{16,0},{24,8},{1,17},{9,25},{17,1},{25,9},{2,18},{10... | collective-permute-start | bytes 1327112 | tf_op jit(solution)/shard_map/ppermute | solution.py:39
  257.8 29.3 %copy-start.29 = (bf16[4,24,1920]{2,1,0:T(8,128)(2,1)}, bf16[4,24,1920]{2,1,0:T(8,128)(2,1)S(1)}, u32[]{:S(2)}) copy-start(bf16[4,24,1920]{2,1,0:T(8,128)(2,1)S(1)} %collective-permute-done.21.refs_2_) | copy-start | bytes 1105924
  260.4 29.3 %copy-start.50 = (f32[768]{0:T(1024)S(1)}, f32[768]{0:T(1024)}, u32[]{:S(2)}) copy-start(f32[768]{0:T(1024)} %get-tuple-element.201) | copy-start | bytes 9220
  260.4 29.3 %copy-start.49 = (f32[768]{0:T(1024)S(1)}, f32[768]{0:T(1024)}, u32[]{:S(2)}) copy-start(f32[768]{0:T(1024)} %get-tuple-element.208) | copy-start | bytes 9220
  260.4 20.6 %collective-permute-start.25 = (bf16[128,768]{1,0:T(8,128)(2,1)}, bf16[128,768]{1,0:T(8,128)(2,1)}, u32[]{:S(2)}, u32[]{:S(2)}) collective-permute-start(bf16[128,768]{1,0:T(8,128)(2,1)} %get-tuple-element.161), channel_id=1, source_target_pairs={{0,2},{1,3},{2,0},{3,1},{4,6},{5,7},{6,4},{7,5},{8,10},{9,11},{10,... | collective-permute-start | bytes 589832 | tf_op jit(solution)/shard_map/ppermute | solution.py:707
  261.8 19.2 %collective-permute-start.23 = (bf16[128,768]{1,0:T(8,128)(2,1)}, bf16[128,768]{1,0:T(8,128)(2,1)}, u32[]{:S(2)}, u32[]{:S(2)}) collective-permute-start(bf16[128,768]{1,0:T(8,128)(2,1)} %get-tuple-element.163), channel_id=1, source_target_pairs={{0,4},{1,5},{2,6},{3,7},{4,0},{5,1},{6,2},{7,3},{8,12},{9,13},{10,... | collective-permute-start | bytes 589832 | tf_op jit(solution)/shard_map/ppermute | solution.py:707
  264.0 17.6 %collective-permute-start.28 = (bf16[128,768]{1,0:T(8,128)(2,1)}, bf16[128,768]{1,0:T(8,128)(2,1)}, u32[]{:S(2)}, u32[]{:S(2)}) collective-permute-start(bf16[128,768]{1,0:T(8,128)(2,1)} %get-tuple-element.165), channel_id=1, source_target_pairs={{0,6},{1,7},{2,4},{3,5},{4,2},{5,3},{6,0},{7,1},{8,14},{9,15},{10,... | collective-permute-start | bytes 589832 | tf_op jit(solution)/shard_map/ppermute | solution.py:707
  281.0 17.3 %collective-permute-start.24 = (bf16[128,768]{1,0:T(8,128)(2,1)}, bf16[128,768]{1,0:T(8,128)(2,1)S(1)}, u32[]{:S(2)}, u32[]{:S(2)}) collective-permute-start(bf16[128,768]{1,0:T(8,128)(2,1)} %get-tuple-element.168), channel_id=1, source_target_pairs={{0,1},{1,0},{2,3},{3,2},{4,5},{5,4},{6,7},{7,6},{8,9},{9,8},{10,11... | collective-permute-start | bytes 589832 | tf_op jit(solution)/shard_map/ppermute | solution.py:707
  281.0 17.8 %collective-permute-start.26 = (bf16[128,768]{1,0:T(8,128)(2,1)}, bf16[128,768]{1,0:T(8,128)(2,1)}, u32[]{:S(2)}, u32[]{:S(2)}) collective-permute-start(bf16[128,768]{1,0:T(8,128)(2,1)} %get-tuple-element.169), channel_id=1, source_target_pairs={{0,3},{1,2},{2,1},{3,0},{4,7},{5,6},{6,5},{7,4},{8,11},{9,10},{10,... | collective-permute-start | bytes 589832 | tf_op jit(solution)/shard_map/ppermute | solution.py:707
  289.4 33.9 %collective-permute-start.41 = (bf16[2,24,3840]{2,1,0:T(8,128)(2,1)}, bf16[2,24,3840]{2,1,0:T(8,128)(2,1)S(1)}, u32[]{:S(2)}, u32[]{:S(2)}) collective-permute-start(bf16[2,24,3840]{2,1,0:T(8,128)(2,1)} %get-tuple-element.196), channel_id=1, source_target_pairs={{0,2},{1,3},{2,0},{3,1},{4,6},{5,7},{6,4},{7,5},{8,10},{9,11},{10,... | collective-permute-start | bytes 1105928 | tf_op jit(solution)/shard_map/ppermute | solution.py:39
  289.8 1.3 collective-permute-start.30
  291.1 6.2 %collective-permute-start.31 = (f32[12,768]{1,0:T(8,128)S(1)}, f32[12,768]{1,0:T(8,128)S(1)}, u32[]{:S(2)}, u32[]{:S(2)}) collective-permute-start(f32[12,768]{1,0:T(8,128)S(1)} %add.243), channel_id=1, source_target_pairs={{0,1},{1,0},{2,3},{3,2},{4,5},{5,4},{6,7},{7,6},{8,9},{9,8},{10,11... | collective-permute-start | bytes 110600 | tf_op jit(solution)/shard_map/ppermute | solution.py:39
  291.9 18.2 %collective-permute-start.27 = (bf16[128,768]{1,0:T(8,128)(2,1)}, bf16[128,768]{1,0:T(8,128)(2,1)S(1)}, u32[]{:S(2)}, u32[]{:S(2)}) collective-permute-start(bf16[128,768]{1,0:T(8,128)(2,1)} %get-tuple-element.170), channel_id=1, source_target_pairs={{0,5},{1,4},{2,7},{3,6},{4,1},{5,0},{6,3},{7,2},{8,13},{9,12},{10,... | collective-permute-start | bytes 589832 | tf_op jit(solution)/shard_map/ppermute | solution.py:707
  297.3 21.0 %collective-permute-start.35 = (bf16[4,24,1152]{2,1,0:T(8,128)(2,1)}, bf16[4,24,1152]{2,1,0:T(8,128)(2,1)S(1)}, u32[]{:S(2)}, u32[]{:S(2)}) collective-permute-start(bf16[4,24,1152]{2,1,0:T(8,128)(2,1)} %get-tuple-element.177), channel_id=1, source_target_pairs={{0,16},{8,24},{16,0},{24,8},{1,17},{9,25},{17,1},{25,9},{2,18},{10... | collective-permute-start | bytes 663560 | tf_op jit(solution)/shard_map/ppermute | solution.py:39
  298.3 20.0 %collective-permute-start.36 = (bf16[4,24,1152]{2,1,0:T(8,128)(2,1)}, bf16[4,24,1152]{2,1,0:T(8,128)(2,1)S(1)}, u32[]{:S(2)}, u32[]{:S(2)}) collective-permute-start(bf16[4,24,1152]{2,1,0:T(8,128)(2,1)} %get-tuple-element.178), channel_id=1, source_target_pairs={{0,1},{1,0},{2,3},{3,2},{4,5},{5,4},{6,7},{7,6},{8,9},{9,8},{10,11... | collective-permute-start | bytes 663560 | tf_op jit(solution)/shard_map/ppermute | solution.py:39
  298.9 15.3 %collective-permute-start.29 = (bf16[128,768]{1,0:T(8,128)(2,1)S(1)}, bf16[128,768]{1,0:T(8,128)(2,1)S(1)}, u32[]{:S(2)}, u32[]{:S(2)}) collective-permute-start(bf16[128,768]{1,0:T(8,128)(2,1)S(1)} %copy-done.66), channel_id=1, source_target_pairs={{0,7},{1,6},{2,5},{3,4},{4,3},{5,2},{6,1},{7,0},{8,15},{9,14},{10,... | collective-permute-start | bytes 589832 | tf_op jit(solution)/shard_map/ppermute | solution.py:707
  310.1 11.1 %collective-permute-start.34 = (f32[12,768]{1,0:T(8,128)S(1)}, f32[12,768]{1,0:T(8,128)S(1)}, u32[]{:S(2)}, u32[]{:S(2)}) collective-permute-start(f32[12,768]{1,0:T(8,128)S(1)} %add.244), channel_id=1, source_target_pairs={{0,16},{8,24},{16,0},{24,8},{1,17},{9,25},{17,1},{25,9},{2,18},{10... | collective-permute-start | bytes 110600 | tf_op jit(solution)/shard_map/ppermute | solution.py:39
  321.2 18.2 %copy-start.33 = (bf16[2,24,2304]{2,1,0:T(8,128)(2,1)S(1)}, bf16[2,24,2304]{2,1,0:T(8,128)(2,1)}, u32[]{:S(2)}) copy-start(bf16[2,24,2304]{2,1,0:T(8,128)(2,1)} %get-tuple-element.186) | copy-start | bytes 663556
  321.2 8.8 %collective-permute-start.38 = (bf16[2,24,2304]{2,1,0:T(8,128)(2,1)}, bf16[2,24,2304]{2,1,0:T(8,128)(2,1)S(1)}, u32[]{:S(2)}, u32[]{:S(2)}) collective-permute-start(bf16[2,24,2304]{2,1,0:T(8,128)(2,1)} %get-tuple-element.184), channel_id=1, source_target_pairs={{0,2},{1,3},{2,0},{3,1},{4,6},{5,7},{6,4},{7,5},{8,10},{9,11},{10,... | collective-permute-start | bytes 663560 | tf_op jit(solution)/shard_map/ppermute | solution.py:39
  321.2 9.8 %collective-permute-start.37 = (f32[12,768]{1,0:T(8,128)S(1)}, f32[12,768]{1,0:T(8,128)S(1)}, u32[]{:S(2)}, u32[]{:S(2)}) collective-permute-start(f32[12,768]{1,0:T(8,128)S(1)} %add.245), channel_id=1, source_target_pairs={{0,2},{1,3},{2,0},{3,1},{4,6},{5,7},{6,4},{7,5},{8,10},{9,11},{10,... | collective-permute-start | bytes 110600 | tf_op jit(solution)/shard_map/ppermute | solution.py:39
  323.4 14.6 %collective-permute-start.42 = (bf16[1,24,3840]{2,1,0:T(8,128)(2,1)S(1)}, bf16[1,24,3840]{2,1,0:T(8,128)(2,1)S(1)}, u32[]{:S(2)}, u32[]{:S(2)}) collective-permute-start(bf16[1,24,3840]{2,1,0:T(8,128)(2,1)S(1)} %get-tuple-element.234), channel_id=1, source_target_pairs={{0,4},{1,5},{2,6},{3,7},{4,0},{5,1},{6,2},{7,3},{8,12},{9,13},{10,... | collective-permute-start | bytes 552968 | tf_op jit(solution)/shard_map/ppermute | solution.py:39
  331.0 8.4 %collective-permute-start.40 = (bf16[1,24,2304]{2,1,0:T(8,128)(2,1)S(1)}, bf16[1,24,2304]{2,1,0:T(8,128)(2,1)S(1)}, u32[]{:S(2)}, u32[]{:S(2)}) collective-permute-start(bf16[1,24,2304]{2,1,0:T(8,128)(2,1)S(1)} %add_convert_fusion.5), channel_id=1, source_target_pairs={{0,4},{1,5},{2,6},{3,7},{4,0},{5,1},{6,2},{7,3},{8,12},{9,13},{10,... | collective-permute-start | bytes 331784 | tf_op jit(solution)/shard_map/ppermute | solution.py:39
  331.1 9.0 %collective-permute-start.39 = (f32[12,768]{1,0:T(8,128)S(1)}, f32[12,768]{1,0:T(8,128)S(1)}, u32[]{:S(2)}, u32[]{:S(2)}) collective-permute-start(f32[12,768]{1,0:T(8,128)S(1)} %add.247), channel_id=1, source_target_pairs={{0,4},{1,5},{2,6},{3,7},{4,0},{5,1},{6,2},{7,3},{8,12},{9,13},{10,... | collective-permute-start | bytes 110600 | tf_op jit(solution)/shard_map/ppermute | solution.py:39
  (56 other events, 301.7 us)
Sparse Core Ops, SparseCore 0:
  11.2 114.7 all-gather.2
  174.0 113.0 reduce-scatter.1
